TPU v7x, 32 devices: a whole 2x2x4 slice. The times are simulated.
32 devices in a mesh: wide: 8 (over y, x, core), narrow: 4 (over z).
Axes of the slice: x: 2, y: 2, z: 4, core: 2. Of those that a mesh axis runs over, the one named last changes fastest.
Arguments:
- tokens: bfloat16 [8192, 768], P(('wide', 'narrow')), may hold values from -6 to 6
- memory: bfloat16 [8, 512, 768], P('wide', 'narrow'), may hold values from -6 to 6
- segments: int32 [8, 1024], P('wide'), may hold values from 0 to 3, never falling along the last dimension, each value on 1 to 512 neighbouring positions
- valid_rows: int32 [8], P('wide'), may hold values from 64 to 512, as said below
- norm_gains: float32 [3, 768], replicated, may hold values from 0.5 to 1.5
- rel_table: float32 [32, 12], replicated, may hold values from -6 to 6
- self_weights: bfloat16 [4, 768, 768], P(None, None, 'narrow')
- cross_weights: bfloat16 [4, 768, 768], P(None, None, 'narrow')
- ffn_weights: bfloat16 [3, 768, 2048], P(None, None, 'narrow'), may hold values from -0.21875 to 0.21875
- cotangent: bfloat16 [8192, 768], P(('wide', 'narrow')), may hold values from -6 to 6
Outputs:
- output: bfloat16 [8192, 768], P(('wide', 'narrow'))
- tokens_grad: float32 [8192, 768], P(('wide', 'narrow'))
- memory_grad: float32 [8, 512, 768], P('wide', 'narrow')
- gains_grad: float32 [3, 768], replicated
- rel_grad: float32 [32, 12], replicated
- self_grad: float32 [4, 768, 768], P(None, 'wide', 'narrow')
- cross_grad: float32 [4, 768, 768], P(None, 'wide', 'narrow')
- ffn_grad: float32 [3, 768, 2048], P(None, 'wide', 'narrow')
- attn_row_stats: float32 [6, 768], P(None, 'wide')
- attn_col_stats: float32 [6, 768], P(None, 'narrow')
- proj_stats: float32 [2, 1536], replicated
- ffn_row_stats: float32 [3, 768], P(None, 'wide')
- ffn_col_stats: float32 [3, 2048], P(None, 'narrow')
Inputs may be any that keep to these rules, and one draw needn't show every extreme that they name: `segments`: segment numbers never fall along a sequence; a segment has at most 512 tokens. memory rows below valid_rows of a sequence are real, the others padding; some sequence has 512 and some 512 // 8.
All inputs are finite; a program needn't handle non-finite values.
Results may differ from a plain program's by a relative error of at most 0.025.
The roundings to bfloat16 on the way count: a program that leaves them out, or rounds other values in their place, can miss the bound.
Values may be sent and summed in bfloat16 or wider, within the bound.
A program may use at most 128 MiB of HBM per device.

v0:
```python
import math

import jax
import jax.numpy as jnp
import numpy as np
from jax import lax
from jax.sharding import PartitionSpec as P

BUCKETS = 32
MAX_DIST = 128


eps_norm = 1e-06
masked_score = -1000000000.0


def bucket_table(seq_length, bucket_count, max_distance):
    exact_count = bucket_count // 2
    bucket_ids = np.zeros((seq_length,), np.int32)
    for distance in range(seq_length):
        if distance < exact_count:
            bucket_ids[distance] = distance
        else:
            scaled_log = (
                math.log(distance / exact_count)
                / math.log(max_distance / exact_count)
                * (bucket_count - exact_count)
            )
            bucket_ids[distance] = min(bucket_count - 1, exact_count + int(scaled_log))
    return bucket_ids


def bucket_thresholds(seq_length, bucket_count, max_distance):
    bucket_ids = bucket_table(seq_length, bucket_count, max_distance)
    thresholds = []
    for bucket_number in range(1, bucket_count):
        first_reach = -1
        for distance in range(seq_length):
            if first_reach < 0 and int(bucket_ids[distance]) >= bucket_number:
                first_reach = distance
        if first_reach >= 0:
            thresholds.append(first_reach)
    return thresholds


def rms_scaled(values, gain_row):
    return (
        values * lax.rsqrt(jnp.mean(values * values, axis=-1, keepdims=True) + eps_norm) * gain_row
    )


def gelu_product(gate_values, up_values):
    return jax.nn.gelu(gate_values, approximate=True) * up_values


def matmul(left_side, right_side):
    return jnp.dot(left_side, right_side, preferred_element_type=jnp.float32)


def matmul_tn(left_side, right_side):
    return lax.dot_general(
        left_side, right_side, (((0,), (0,)), ((), ())), preferred_element_type=jnp.float32
    )


def matmul_nt(left_side, right_side):
    return lax.dot_general(
        left_side, right_side, (((1,), (1,)), ((), ())), preferred_element_type=jnp.float32
    )


def gather_rows(row_values):
    return lax.all_gather(row_values, "narrow", axis=0, tiled=True)


def reduce_rows(partial_sum):
    return lax.psum_scatter(partial_sum, "narrow", scatter_dimension=0, tiled=True)


def split_heads(values, head_count):
    return values.reshape(values.shape[0], head_count, values.shape[1] // head_count)


def block_scores(queries, key_rows, bias_terms, allowed, head_count):
    scores = jnp.einsum(
        "qhd,khd->hqk",
        split_heads(queries, head_count),
        split_heads(key_rows, head_count),
        preferred_element_type=jnp.float32,
    )
    scores = scores + bias_terms
    return jnp.where(allowed[None], scores, masked_score)


def attend_block(queries, key_rows, values_in, bias_terms, allowed, head_count):
    scores = block_scores(queries, key_rows, bias_terms, allowed, head_count)
    row_max = jnp.max(scores, axis=-1, keepdims=True)
    weights_exp = jnp.exp(scores - row_max)
    totals = jnp.sum(weights_exp, axis=-1, keepdims=True)
    probabilities = (weights_exp / totals).astype(jnp.bfloat16)
    mixed_heads = jnp.einsum(
        "hqk,khd->qhd",
        probabilities,
        split_heads(values_in, head_count),
        preferred_element_type=jnp.float32,
    )
    log_totals = (row_max + jnp.log(totals))[:, :, 0]
    return (mixed_heads.reshape(queries.shape[0], -1).astype(jnp.bfloat16), log_totals)


def attend_back(
    queries, key_rows, values_in, grad_out, log_totals, bias_terms, allowed, head_count
):
    scores = block_scores(queries, key_rows, bias_terms, allowed, head_count)
    probabilities = jnp.exp(scores - log_totals[:, :, None])
    probs_low = probabilities.astype(jnp.bfloat16)
    grad_heads = split_heads(grad_out, head_count)
    grad_values = jnp.einsum(
        "hqk,qhd->khd", probs_low, grad_heads, preferred_element_type=jnp.float32
    )
    grad_probs = jnp.einsum(
        "qhd,khd->hqk",
        grad_heads,
        split_heads(values_in, head_count),
        preferred_element_type=jnp.float32,
    )
    centered = grad_probs - jnp.sum(probabilities * grad_probs, axis=-1, keepdims=True)
    grad_scores = (probabilities * centered).astype(jnp.bfloat16)
    grad_queries = jnp.einsum(
        "hqk,khd->qhd",
        grad_scores,
        split_heads(key_rows, head_count),
        preferred_element_type=jnp.float32,
    )
    grad_keys = jnp.einsum(
        "hqk,qhd->khd",
        grad_scores,
        split_heads(queries, head_count),
        preferred_element_type=jnp.float32,
    )
    key_count = key_rows.shape[0]
    return (
        grad_queries.reshape(queries.shape[0], -1),
        grad_keys.reshape(key_count, -1),
        grad_values.reshape(key_count, -1),
        grad_scores,
    )


def self_geometry(rel_local, thresholds, segment_row, offset, block_rows, seq_length):
    query_pos = offset + jnp.arange(block_rows)
    key_pos = jnp.arange(seq_length)
    distance = jnp.maximum(query_pos[:, None] - key_pos[None, :], 0)
    bucket_tile = jnp.zeros(distance.shape, jnp.int32)
    for threshold in thresholds:
        bucket_tile = bucket_tile + (distance >= threshold).astype(jnp.int32)
    bias_terms = jnp.broadcast_to(
        rel_local[0][:, None, None], (rel_local.shape[1], block_rows, seq_length)
    )
    for bucket_number in range(1, len(thresholds) + 1):
        bias_terms = jnp.where(
            bucket_tile[None] == bucket_number, rel_local[bucket_number][:, None, None], bias_terms
        )
    query_segments = segment_row[offset : offset + block_rows]
    allowed = (key_pos[None, :] <= query_pos[:, None]) & (
        query_segments[:, None] == segment_row[None, :]
    )
    return (bucket_tile, bias_terms, allowed)


def local(
    tokens,
    memory,
    segments,
    valid_rows,
    norm_gains,
    rel_table,
    self_weights,
    cross_weights,
    ffn_weights,
    cotangent,
):
    narrow_count = lax.axis_size("narrow")
    head_count = rel_table.shape[1] // narrow_count
    seq_count = segments.shape[0]
    seq_length = segments.shape[1]
    model_width = tokens.shape[1]
    block_rows = min(512, seq_length)
    local_width = self_weights.shape[2]
    ffn_local = ffn_weights.shape[2]
    head_start = lax.axis_index("narrow") * head_count
    rel_local = lax.dynamic_slice_in_dim(rel_table, head_start, head_count, 1)
    thresholds = bucket_thresholds(seq_length, BUCKETS, MAX_DIST)
    bucket_range = jnp.arange(BUCKETS)

    def per_seq(values):
        return values.reshape(seq_count, -1, values.shape[-1])

    token_values = tokens.astype(jnp.float32)
    hidden_one = gather_rows(rms_scaled(token_values, norm_gains[0]).astype(jnp.bfloat16))
    q_self = matmul(hidden_one, self_weights[0]).astype(jnp.bfloat16)
    k_self = matmul(hidden_one, self_weights[1]).astype(jnp.bfloat16)
    v_self = matmul(hidden_one, self_weights[2]).astype(jnp.bfloat16)

    def self_forward(seq_item):
        q_seq, k_seq, v_seq, segment_row = seq_item
        mixed_parts = []
        total_parts = []
        for offset in range(0, seq_length, block_rows):
            bucket_tile, bias_terms, allowed = self_geometry(
                rel_local, thresholds, segment_row, offset, block_rows, seq_length
            )
            mixed_block, log_block = attend_block(
                q_seq[offset : offset + block_rows], k_seq, v_seq, bias_terms, allowed, head_count
            )
            mixed_parts.append(mixed_block)
            total_parts.append(log_block)
        return (jnp.concatenate(mixed_parts, 0), jnp.concatenate(total_parts, 1))

    out_self, totals_self = lax.map(
        self_forward, (per_seq(q_self), per_seq(k_self), per_seq(v_self), segments)
    )
    out_self = out_self.reshape(-1, local_width)
    state_one = token_values + reduce_rows(matmul_nt(out_self, self_weights[3]))
    hidden_two = gather_rows(rms_scaled(state_one, norm_gains[1]).astype(jnp.bfloat16))
    memory_full = lax.all_gather(memory, "narrow", axis=1, tiled=True)
    mem_length = memory_full.shape[1]
    memory_flat = memory_full.reshape(-1, model_width)
    q_cross = matmul(hidden_two, cross_weights[0]).astype(jnp.bfloat16)
    k_cross = (
        matmul(memory_flat, cross_weights[1])
        .astype(jnp.bfloat16)
        .reshape(seq_count, mem_length, local_width)
    )
    v_cross = (
        matmul(memory_flat, cross_weights[2])
        .astype(jnp.bfloat16)
        .reshape(seq_count, mem_length, local_width)
    )
    key_index = jnp.arange(mem_length)

    def cross_forward(seq_item):
        q_seq, k_seq, v_seq, valid_count = seq_item
        allowed = jnp.broadcast_to(key_index[None, :] < valid_count, (block_rows, mem_length))
        mixed_parts = []
        total_parts = []
        for offset in range(0, seq_length, block_rows):
            mixed_block, log_block = attend_block(
                q_seq[offset : offset + block_rows], k_seq, v_seq, 0.0, allowed, head_count
            )
            mixed_parts.append(mixed_block)
            total_parts.append(log_block)
        return (jnp.concatenate(mixed_parts, 0), jnp.concatenate(total_parts, 1))

    out_cross, totals_cross = lax.map(
        cross_forward, (per_seq(q_cross), k_cross, v_cross, valid_rows)
    )
    out_cross = out_cross.reshape(-1, local_width)
    state_two = state_one + reduce_rows(matmul_nt(out_cross, cross_weights[3]))
    hidden_three = gather_rows(rms_scaled(state_two, norm_gains[2]).astype(jnp.bfloat16))
    gate_values = matmul(hidden_three, ffn_weights[0])
    up_values = matmul(hidden_three, ffn_weights[1])
    activated = gelu_product(gate_values, up_values).astype(jnp.bfloat16)
    result_rows = state_two + reduce_rows(matmul_nt(activated, ffn_weights[2]))
    output = result_rows.astype(jnp.bfloat16)
    grad_output = cotangent.astype(jnp.float32)
    grad_ffn = gather_rows(cotangent)
    down_grad = matmul_tn(grad_ffn, activated)
    grad_activated = matmul(grad_ffn, ffn_weights[2])
    gelu_value, pull_gelu = jax.vjp(gelu_product, gate_values, up_values)
    grad_gate, grad_up = pull_gelu(grad_activated)
    grad_gate = grad_gate.astype(jnp.bfloat16)
    grad_up = grad_up.astype(jnp.bfloat16)
    gate_grad = matmul_tn(hidden_three, grad_gate)
    up_grad = matmul_tn(hidden_three, grad_up)
    grad_hidden = reduce_rows(
        matmul_nt(grad_gate, ffn_weights[0]) + matmul_nt(grad_up, ffn_weights[1])
    )
    norm_value, pull_norm = jax.vjp(rms_scaled, state_two, norm_gains[2])
    grad_state, gain_three = pull_norm(grad_hidden)
    grad_state_two = grad_output + grad_state
    grad_cross = gather_rows(grad_state_two.astype(jnp.bfloat16))
    cross_out_grad = matmul_tn(grad_cross, out_cross)
    grad_out_cross = matmul(grad_cross, cross_weights[3]).astype(jnp.bfloat16)

    def cross_backward(seq_item):
        q_seq, k_seq, v_seq, grad_seq, log_seq, valid_count = seq_item
        allowed = jnp.broadcast_to(key_index[None, :] < valid_count, (block_rows, mem_length))
        query_parts = []
        key_sum = jnp.zeros((mem_length, local_width), jnp.float32)
        value_sum = jnp.zeros((mem_length, local_width), jnp.float32)
        for offset in range(0, seq_length, block_rows):
            grad_query_block, grad_key_block, grad_value_block, grad_score_block = attend_back(
                q_seq[offset : offset + block_rows],
                k_seq,
                v_seq,
                grad_seq[offset : offset + block_rows],
                log_seq[:, offset : offset + block_rows],
                0.0,
                allowed,
                head_count,
            )
            query_parts.append(grad_query_block)
            key_sum = key_sum + grad_key_block
            value_sum = value_sum + grad_value_block
        return (jnp.concatenate(query_parts, 0), key_sum, value_sum)

    grad_q_cross, grad_k_cross, grad_v_cross = lax.map(
        cross_backward,
        (per_seq(q_cross), k_cross, v_cross, per_seq(grad_out_cross), totals_cross, valid_rows),
    )
    query_low = grad_q_cross.reshape(-1, local_width).astype(jnp.bfloat16)
    key_low = grad_k_cross.reshape(-1, local_width).astype(jnp.bfloat16)
    value_low = grad_v_cross.reshape(-1, local_width).astype(jnp.bfloat16)
    cross_local = jnp.stack(
        [
            matmul_tn(hidden_two, query_low),
            matmul_tn(memory_flat, key_low),
            matmul_tn(memory_flat, value_low),
            cross_out_grad,
        ]
    )
    memory_partial = (
        matmul_nt(key_low, cross_weights[1]) + matmul_nt(value_low, cross_weights[2])
    ).reshape(seq_count, mem_length, model_width)
    memory_grad = lax.psum_scatter(
        memory_partial.astype(jnp.bfloat16), "narrow", scatter_dimension=1, tiled=True
    ).astype(jnp.float32)
    grad_hidden = reduce_rows(matmul_nt(query_low, cross_weights[0]))
    norm_value, pull_norm = jax.vjp(rms_scaled, state_one, norm_gains[1])
    grad_state, gain_two = pull_norm(grad_hidden)
    grad_state_one = grad_state_two + grad_state
    grad_self = gather_rows(grad_state_one.astype(jnp.bfloat16))
    self_out_grad = matmul_tn(grad_self, out_self)
    grad_out_self = matmul(grad_self, self_weights[3]).astype(jnp.bfloat16)

    def self_backward(seq_item):
        q_seq, k_seq, v_seq, grad_seq, log_seq, segment_row = seq_item
        query_parts = []
        key_sum = jnp.zeros((seq_length, local_width), jnp.float32)
        value_sum = jnp.zeros((seq_length, local_width), jnp.float32)
        bucket_sum = jnp.zeros((BUCKETS, head_count), jnp.float32)
        for offset in range(0, seq_length, block_rows):
            bucket_tile, bias_terms, allowed = self_geometry(
                rel_local, thresholds, segment_row, offset, block_rows, seq_length
            )
            grad_query_block, grad_key_block, grad_value_block, grad_score_block = attend_back(
                q_seq[offset : offset + block_rows],
                k_seq,
                v_seq,
                grad_seq[offset : offset + block_rows],
                log_seq[:, offset : offset + block_rows],
                bias_terms,
                allowed,
                head_count,
            )
            query_parts.append(grad_query_block)
            key_sum = key_sum + grad_key_block
            value_sum = value_sum + grad_value_block
            bucket_onehot = (bucket_tile[:, :, None] == bucket_range[None, None, :]).astype(
                jnp.bfloat16
            )
            bucket_sum = bucket_sum + jnp.einsum(
                "hqk,qkb->bh", grad_score_block, bucket_onehot, preferred_element_type=jnp.float32
            )
        return (jnp.concatenate(query_parts, 0), key_sum, value_sum, bucket_sum)

    grad_q_self, grad_k_self, grad_v_self, bucket_sums = lax.map(
        self_backward,
        (
            per_seq(q_self),
            per_seq(k_self),
            per_seq(v_self),
            per_seq(grad_out_self),
            totals_self,
            segments,
        ),
    )
    query_low = grad_q_self.reshape(-1, local_width).astype(jnp.bfloat16)
    key_low = grad_k_self.reshape(-1, local_width).astype(jnp.bfloat16)
    value_low = grad_v_self.reshape(-1, local_width).astype(jnp.bfloat16)
    self_local = jnp.stack(
        [
            matmul_tn(hidden_one, query_low),
            matmul_tn(hidden_one, key_low),
            matmul_tn(hidden_one, value_low),
            self_out_grad,
        ]
    )
    rel_part = jnp.sum(bucket_sums, axis=0)
    rel_full = lax.dynamic_update_slice_in_dim(
        jnp.zeros(rel_table.shape, jnp.float32), rel_part, head_start, 1
    )
    grad_hidden = reduce_rows(
        matmul_nt(query_low, self_weights[0])
        + matmul_nt(key_low, self_weights[1])
        + matmul_nt(value_low, self_weights[2])
    )
    norm_value, pull_norm = jax.vjp(rms_scaled, token_values, norm_gains[0])
    grad_state, gain_one = pull_norm(grad_hidden)
    tokens_grad = grad_state_one + grad_state
    gains_grad, rel_grad = lax.psum(
        (jnp.stack([gain_one, gain_two, gain_three]), rel_full), ("wide", "narrow")
    )
    ffn_local_grads = jnp.stack([gate_grad, up_grad, down_grad])
    wide_count = lax.axis_size("wide")
    own_rows = model_width // wide_count
    row_start = lax.axis_index("wide") * own_rows
    col_start = lax.axis_index("narrow") * local_width
    full_width = local_width * narrow_count
    summed = lax.psum((self_local, cross_local, ffn_local_grads), "wide")
    attn_full = jnp.concatenate([summed[0][:3], summed[1][:3]], 0)
    attn_col_stats = jnp.mean(attn_full * attn_full, axis=1)
    ffn_col_stats = jnp.mean(summed[2] * summed[2], axis=1)
    outer_full = jnp.stack([summed[0][3], summed[1][3]])
    outer_squares = outer_full * outer_full
    proj_row_part = jnp.sum(outer_squares, axis=2)
    proj_col_own = jnp.mean(outer_squares, axis=1)
    self_grad = lax.dynamic_slice_in_dim(summed[0], row_start, own_rows, 1)
    cross_grad = lax.dynamic_slice_in_dim(summed[1], row_start, own_rows, 1)
    ffn_grad = lax.dynamic_slice_in_dim(summed[2], row_start, own_rows, 1)
    proj_col_padded = lax.dynamic_update_slice_in_dim(
        jnp.zeros((2, full_width), jnp.float32), proj_col_own, col_start, 1
    )
    attn_own = jnp.concatenate([self_grad[:3], cross_grad[:3]], 0)
    row_attn, row_ffn, proj_rows, proj_cols = lax.psum(
        (
            jnp.sum(attn_own * attn_own, axis=2),
            jnp.sum(ffn_grad * ffn_grad, axis=2),
            proj_row_part,
            proj_col_padded,
        ),
        "narrow",
    )
    attn_row_stats = row_attn / full_width
    ffn_row_stats = row_ffn / (ffn_local * narrow_count)
    proj_stats = jnp.concatenate([proj_rows / full_width, proj_cols], 1)
    return (
        output,
        tokens_grad,
        memory_grad,
        gains_grad,
        rel_grad,
        self_grad,
        cross_grad,
        ffn_grad,
        attn_row_stats,
        attn_col_stats,
        proj_stats,
        ffn_row_stats,
        ffn_col_stats,
    )


def solution(mesh):
    in_specs = (
        P(("wide", "narrow"), None),
        P("wide", "narrow", None),
        P("wide", None),
        P("wide"),
        P(),
        P(),
        P(None, None, "narrow"),
        P(None, None, "narrow"),
        P(None, None, "narrow"),
        P(("wide", "narrow"), None),
    )
    out_specs = (
        P(("wide", "narrow"), None),
        P(("wide", "narrow"), None),
        P("wide", "narrow", None),
        P(),
        P(),
        P(None, "wide", "narrow"),
        P(None, "wide", "narrow"),
        P(None, "wide", "narrow"),
        P(None, "wide"),
        P(None, "narrow"),
        P(),
        P(None, "wide"),
        P(None, "narrow"),
    )
    return jax.shard_map(local, mesh=mesh, in_specs=in_specs, out_specs=out_specs, check_vma=False)
```

profile of v0, /device:TPU:0, one launch (start us, length us, event | category | flops | bytes accessed | tf_op | source)
XLA Modules:
  0.0 1060.6 jit_solution(15200843431141844698)
XLA Ops:
  12.4 7.8 broadcast_compare_fusion.1
  28.1 7.8 broadcast_compare_fusion.9
  35.9 8.3 broadcast_compare_fusion.13
  52.0 7.8 broadcast_compare_fusion.21
  59.9 8.0 broadcast_compare_fusion.25
  75.7 7.8 broadcast_compare_fusion.33
  83.5 8.0 broadcast_compare_fusion.37
  91.5 7.8 broadcast_compare_fusion.41
  99.4 7.9 broadcast_compare_fusion.45
  107.2 8.3 broadcast_compare_fusion.49
  115.5 19.4 %fusion.88 = (pred[512,1024]{1,0:T(8,128)(4,1)}, pred[512,1024]{1,0:T(8,128)(4,1)}, pred[512,1024]{1,0:T(8,128)(4,1)}, pred[512,1024]{1,0:T(8,128)(4,1)}, pred[5...) fusion(s32[1024]{0:T(1024)S(1)} %bitcast.289, ...), kind=kLoop, calls=%fused_computation.128 | loop fusion | flops 68681728 | bytes 17311744 | tf_op jit(solution)/shard_map/while/body/eval_jaxpr/and | solution.py:165
  144.4 8.0 broadcast_compare_fusion.53
  152.4 7.8 broadcast_compare_fusion.57
  164.4 26.6 %fusion.221 = (f32[3,512]{1,0:T(4,128)S(1)}, f32[3,512,1024]{2,1,0:T(8,128)}) fusion(f32[3]{0:T(128)S(1)} %copy-done.136, f32[3]{0:T(128)S(1)} %copy-done.138, pred[512,1024]{1,0:T(8,128)(4,1)} %broadcast_compare_fusion.61, f32[3]{0:T(128)S(1)} %copy-done.140, pred[512,1024]{1,0:T(8,128)(4,1)} %get-tuple-element.300, f32[3]{0:T(128)S(1)} %copy-done.142, ...), kind=kOutput, calls=%fused_computation.425 | convolution fusion | flops 254802432 | bytes 23665024 | tf_op jit(solution)/shard_map/while/body/eval_jaxpr/qhd,khd->hqk/dot_general | solution.py:85
  198.3 26.0 %fusion.220 = (f32[3,512]{1,0:T(4,128)S(1)}, f32[3,512,1024]{2,1,0:T(8,128)}) fusion(f32[3]{0:T(128)S(1)} %copy-done.137, f32[3]{0:T(128)S(1)} %copy-done.139, pred[512,1024]{1,0:T(8,128)(4,1)} %get-tuple-element.256, f32[3]{0:T(128)S(1)} %copy-done.141, pred[512,1024]{1,0:T(8,128)(4,1)} %get-tuple-element.255, f32[3]{0:T(128)S(1)} %copy-done.143, ...), kind=kOutput, calls=%fused_computation.424 | convolution fusion | flops 254802432 | bytes 23665024 | tf_op jit(solution)/shard_map/while/body/eval_jaxpr/qhd,khd->hqk/dot_general | solution.py:85
  233.1 63.2 %reduce-scatter.8.cloned.1.call-done = f32[256,768]{1,0:T(8,128)} async-done(((f32[1024,768]{1,0:T(8,128)}), f32[256,768]{1,0:T(8,128)}) %reduce-scatter.8.cloned.1.call-update) | async-done | bytes 786448 | tf_op jit(solution)/shard_map/reduce_scatter | solution.py:77
  300.1 24.3 %all_gather.22 = bf16[1,512,768]{2,1,0:T(8,128)(2,1)S(1)} all-gather(bf16[1,128,768]{2,1,0:T(8,128)(2,1)S(1)} %copy-done.76), channel_id=1, replica_groups=mesh['wide'=8,'narrow'=4] {'narrow'}, dimensions={1}, use_global_device_ids=true | all-gather | bytes 983040 | tf_op jit(solution)/shard_map/all_gather | solution.py:226
  326.3 16.1 %all-gather.9.cloned.1.call-done = bf16[1024,768]{1,0:T(8,128)(2,1)} async-done(((bf16[256,768]{1,0:T(8,128)(2,1)}), bf16[1024,768]{1,0:T(8,128)(2,1)}) %all-gather.9.cloned.1.call-update) | async-done | bytes 1572880 | tf_op jit(solution)/shard_map/all_gather | solution.py:73
  354.2 60.3 %reduce-scatter.10.cloned.1.call-done = f32[256,768]{1,0:T(8,128)} async-done(((f32[1024,768]{1,0:T(8,128)}), f32[256,768]{1,0:T(8,128)}) %reduce-scatter.10.cloned.1.call-update) | async-done | bytes 786448 | tf_op jit(solution)/shard_map/reduce_scatter | solution.py:77
  418.7 36.2 %all-gather.11.cloned.1.call-done = bf16[1024,768]{1,0:T(8,128)(2,1)} async-done(((bf16[256,768]{1,0:T(8,128)(2,1)}), bf16[1024,768]{1,0:T(8,128)(2,1)}) %all-gather.11.cloned.1.call-update) | async-done | bytes 1572880 | tf_op jit(solution)/shard_map/all_gather | solution.py:73
  462.4 29.9 %all-gather.13.cloned.1.call-done = bf16[1024,768]{1,0:T(8,128)(2,1)} async-done(((bf16[256,768]{1,0:T(8,128)(2,1)}), bf16[1024,768]{1,0:T(8,128)(2,1)}) %all-gather.13.cloned.1.call-update) | async-done | bytes 1572880 | tf_op jit(solution)/shard_map/all_gather | solution.py:73
  502.9 59.4 %reduce-scatter.14.cloned.1.call-done = f32[256,768]{1,0:T(8,128)} async-done(((f32[1024,768]{1,0:T(8,128)}), f32[256,768]{1,0:T(8,128)}) %reduce-scatter.14.cloned.1.call-update) | async-done | bytes 786448 | tf_op jit(solution)/shard_map/reduce_scatter | solution.py:77
  568.2 35.6 %all-gather.15.cloned.1.call-done = bf16[1024,768]{1,0:T(8,128)(2,1)} async-done(((bf16[256,768]{1,0:T(8,128)(2,1)}), bf16[1024,768]{1,0:T(8,128)(2,1)}) %all-gather.15.cloned.1.call-update) | async-done | bytes 1572880 | tf_op jit(solution)/shard_map/all_gather | solution.py:73
  630.3 46.5 %reduce-scatter.16.cloned.1.call-done = f32[256,768]{1,0:T(8,128)} async-done(((f32[1024,768]{1,0:T(8,128)}), f32[256,768]{1,0:T(8,128)}) %reduce-scatter.16.cloned.1.call-update) | async-done | bytes 786448 | tf_op jit(solution)/shard_map/reduce_scatter | solution.py:77
  680.2 59.1 %reduce-scatter.12.cloned.1.call-done = f32[256,768]{1,0:T(8,128)} async-done(((f32[1024,768]{1,0:T(8,128)}), f32[256,768]{1,0:T(8,128)}) %reduce-scatter.12.cloned.1.call-update) | async-done | bytes 786448 | tf_op jit(solution)/shard_map/reduce_scatter | solution.py:77
  761.9 18.3 %all-gather.17.cloned.1.call-done = bf16[1024,768]{1,0:T(8,128)(2,1)} async-done(((bf16[256,768]{1,0:T(8,128)(2,1)}), bf16[1024,768]{1,0:T(8,128)(2,1)}) %all-gather.17.cloned.1.call-update) | async-done | bytes 1572880 | tf_op jit(solution)/shard_map/all_gather | solution.py:73
  850.0 12.3 %fusion.123 = f32[32,3]{0,1:T(4,128)S(1)} fusion(bf16[3,512,1024]{1,0,2:T(4,128)(2,1)} %copy.34, s32[512,1024]{0,1:T(8,128)} %copy.33), kind=kOutput, calls=%fused_computation.190 | convolution fusion | flops 117440512 | bytes 5243264 | tf_op jit(solution)/shard_map/while/body/eval_jaxpr/hqk,qkb->bh/dot_general | solution.py:363
  862.3 10.8 %fusion.125 = f32[32,3]{0,1:T(4,128)S(1)} fusion(f32[32,3]{0,1:T(4,128)S(1)} %fusion.123, bf16[3,512,1024]{1,0,2:T(4,128)(2,1)S(1)} %copy-done.23, s32[512,1024]{0,1:T(8,128)S(1)} %copy-done.31), kind=kOutput, calls=%fused_computation.192 | convolution fusion | flops 117440608 | bytes 5243648 | tf_op jit(solution)/shard_map/while/body/eval_jaxpr/hqk,qkb->bh/dot_general | solution.py:363
  873.2 72.4 %all-reduce.5.cloned.1.call-done = (f32[4,768,192]{1,2,0:T(8,128)}, f32[4,768,192]{1,2,0:T(8,128)}, f32[3,768,512]{2,1,0:T(8,128)}) async-done(((f32[4,768,192]{1,2,0:T(8,128)}, f32[4,768,192]{1,2,0:T(8,128)}, f32[3,768,512]{2,1,0:T(8,128)}), (f32[4,768,192]{1,2,0:T(8,128)}, f32[4,768,192]{1,2,0:T(8,128)}, f32[3,768,512]{2,1,0:T(8,128)})) %all-reduce.5.cloned.1.call-update) | async-done | bytes 9437200 | tf_op jit(solution)/shard_map/psum | solution.py:411
  961.6 20.6 %all-reduce.2 = (f32[6,96]{1,0:T(8,128)S(1)}, f32[2,768]{1,0:T(2,128)S(1)}, f32[2,768]{1,0:T(2,128)S(1)}, f32[3,96]{1,0:T(4,128)S(1)}) all-reduce(f32[6,96]{1,0:T(8,128)S(1)} %fusion.158, f32[2,768]{1,0:T(2,128)S(1)} %dynamic_update_slice.34, f32[2,768]{1,0:T(2,128)S(1)} %get-tuple-element.137, ...), channel_id=1, replica_groups=mesh['wide'=8,'narrow'=4] {'narrow'}, use_global_device_ids=true, to_apply=%region_34.35 | all-reduce | flops 3936 | bytes 31488 | tf_op jit(solution)/shard_map/psum | solution.py:426
  989.9 19.3 %reduce-scatter.18.cloned.1.call-done = f32[256,768]{1,0:T(8,128)} async-done(((f32[1024,768]{1,0:T(8,128)}), f32[256,768]{1,0:T(8,128)}) %reduce-scatter.18.cloned.1.call-update) | async-done | bytes 786448 | tf_op jit(solution)/shard_map/reduce_scatter | solution.py:77
  1010.7 40.6 %all-reduce = (f32[3,768]{1,0:T(4,128)}, f32[32,12]{0,1:T(8,128)}) all-reduce(f32[3,768]{1,0:T(4,128)S(1)} %pad_maximum_fusion.15, f32[32,12]{0,1:T(8,128)S(1)} %dynamic_update_slice.33), channel_id=1, replica_groups=mesh['wide'=8,'narrow'=4] {'wide','narrow'}, use_global_device_ids=true, to_apply=%region_28.29 | all-reduce | flops 2688 | bytes 21504 | tf_op jit(solution)/shard_map/psum | solution.py:402
  (526 shorter events, 250.8 us)
Async XLA Ops:
  7.2 135.2 %copy-start = (f32[32,12]{0,1:T(8,128)S(1)}, f32[32,12]{0,1:T(8,128)}, u32[]{:S(2)}) copy-start(f32[32,12]{0,1:T(8,128)} %param.15) | copy-start | bytes 4612
  7.2 153.0 %all-gather.7.cloned.1.call-start = ((), (), s32[]{:S(2)}) async-start(), calls=%async_computation.7 | async-start | bytes 1966080 | tf_op jit(solution)/shard_map/all_gather | solution.py:73
  8.1 289.5 %copy-start.85 = (f32[768]{0:T(1024)}, f32[768]{0:T(1024)S(1)}, u32[]{:S(2)}) copy-start(f32[768]{0:T(1024)S(1)} %get-tuple-element.143) | copy-start | bytes 9220
  8.1 556.5 %copy-start.80 = (f32[768]{0:T(1024)}, f32[768]{0:T(1024)S(1)}, u32[]{:S(2)}) copy-start(f32[768]{0:T(1024)S(1)} %get-tuple-element.141) | copy-start | bytes 9220
  12.4 283.9 %reduce-scatter.8.cloned.1.call-start = ((), (), s32[]{:S(2)}) async-start(), calls=%async_computation.8 | async-start | bytes 3932160 | tf_op jit(solution)/shard_map/reduce_scatter | solution.py:77
  12.4 103.1 %copy-start.96 = (s32[512]{0:T(512)}, s32[512]{0:T(512)S(1)}, u32[]{:S(2)}) copy-start(s32[512]{0:T(512)S(1)} %iota_add_fusion) | copy-start | bytes 6148
  83.5 32.0 %copy-start.103 = (s32[1,1024]{1,0:T(1,128)S(1)}, s32[1,1024]{1,0:T(1,128)}, u32[]{:S(2)}) copy-start(s32[1,1024]{1,0:T(1,128)} %param.12) | copy-start | bytes 12292
  164.1 33.9 %copy-start.50 = (bf16[1024,192]{0,1:T(8,128)(2,1)}, bf16[1024,192]{0,1:T(8,128)(2,1)S(1)}, u32[]{:S(2)}) copy-start(bf16[1024,192]{0,1:T(8,128)(2,1)S(1)} %convolution_convert_fusion.3) | copy-start | bytes 1179652
  195.8 32.7 %copy-start.46 = (bf16[1024,192]{0,1:T(8,128)(2,1)}, bf16[1024,192]{0,1:T(8,128)(2,1)S(1)}, u32[]{:S(2)}) copy-start(bf16[1024,192]{0,1:T(8,128)(2,1)S(1)} %convolution_convert_fusion.5) | copy-start | bytes 1179652
  197.9 32.8 %copy-start.64 = (bf16[3,64,512]{2,1,0:T(8,128)(2,1)}, bf16[3,64,512]{2,1,0:T(8,128)(2,1)S(1)}, u32[]{:S(2)}) copy-start(bf16[3,64,512]{2,1,0:T(8,128)(2,1)S(1)} %fusion.122) | copy-start | bytes 589828
  232.9 63.3 %copy-start.17 = (bf16[256,768]{1,0:T(8,128)(2,1)S(1)}, bf16[256,768]{1,0:T(8,128)(2,1)}, u32[]{:S(2)}) copy-start(bf16[256,768]{1,0:T(8,128)(2,1)} %param.10) | copy-start | bytes 1179652
  233.0 67.1 %copy-start.76 = (bf16[1,128,768]{2,1,0:T(8,128)(2,1)S(1)}, bf16[1,128,768]{2,1,0:T(8,128)(2,1)}, u32[]{:S(2)}) copy-start(bf16[1,128,768]{2,1,0:T(8,128)(2,1)} %param.11) | copy-start | bytes 589828
  233.0 91.4 %copy-start.53 = (bf16[4,768,192]{1,2,0:T(8,128)(2,1)S(1)}, bf16[4,768,192]{1,2,0:T(8,128)(2,1)}, u32[]{:S(2)}) copy-start(bf16[4,768,192]{1,2,0:T(8,128)(2,1)} %param.17) | copy-start | bytes 3538948
  233.0 109.4 %all-gather.9.cloned.1.call-start = ((), (), s32[]{:S(2)}) async-start(), calls=%async_computation.9 | async-start | bytes 1966080 | tf_op jit(solution)/shard_map/all_gather | solution.py:73
  297.6 28.7 %copy-start.104 = (f32[256]{0:T(256)}, f32[256]{0:T(256)S(1)}, u32[]{:S(2)}) copy-start(f32[256]{0:T(256)S(1)} %get-tuple-element.208) | copy-start | bytes 3076
  297.6 28.7 %copy-start.102 = (f32[256]{0:T(256)}, f32[256]{0:T(256)S(1)}, u32[]{:S(2)}) copy-start(f32[256]{0:T(256)S(1)} %fusion.198) | copy-start | bytes 3076
  299.4 115.2 %reduce-scatter.10.cloned.1.call-start = ((), (), s32[]{:S(2)}) async-start(), calls=%async_computation.10 | async-start | bytes 3932160 | tf_op jit(solution)/shard_map/reduce_scatter | solution.py:77
  300.1 49.3 %copy-start.93 = (pred[512]{0:T(512)(128)(4,1)}, pred[512]{0:T(512)(128)(4,1)S(1)}, u32[]{:S(2)}) copy-start(pred[512]{0:T(512)(128)(4,1)S(1)} %iota_compare_fusion.12) | copy-start | bytes 1540
  354.2 100.8 %all-gather.11.cloned.1.call-start = ((), (), s32[]{:S(2)}) async-start(), calls=%async_computation.11 | async-start | bytes 1966080 | tf_op jit(solution)/shard_map/all_gather | solution.py:73
  416.1 148.5 %copy-start.92 = (f32[256]{0:T(256)}, f32[256]{0:T(256)S(1)}, u32[]{:S(2)}) copy-start(f32[256]{0:T(256)S(1)} %fusion.199) | copy-start | bytes 3076
  417.9 74.4 %all-gather.13.cloned.1.call-start = ((), (), s32[]{:S(2)}) async-start(), calls=%async_computation.13 | async-start | bytes 1966080 | tf_op jit(solution)/shard_map/all_gather | solution.py:73
  418.5 143.8 %reduce-scatter.14.cloned.1.call-start = ((), (), s32[]{:S(2)}) async-start(), calls=%async_computation.14 | async-start | bytes 3932160 | tf_op jit(solution)/shard_map/reduce_scatter | solution.py:77
  502.8 100.9 %all-gather.15.cloned.1.call-start = ((), (), s32[]{:S(2)}) async-start(), calls=%async_computation.15 | async-start | bytes 1966080 | tf_op jit(solution)/shard_map/all_gather | solution.py:73
  566.7 110.1 %reduce-scatter.16.cloned.1.call-start = ((), (), s32[]{:S(2)}) async-start(), calls=%async_computation.16 | async-start | bytes 3932160 | tf_op jit(solution)/shard_map/reduce_scatter | solution.py:77
  567.4 42.2 %copy-start.77 = (f32[3,512]{1,0:T(4,128)}, f32[3,512]{1,0:T(4,128)S(1)}, u32[]{:S(2)}) copy-start(f32[3,512]{1,0:T(4,128)S(1)} %log_add_fusion.2) | copy-start | bytes 18436
  617.4 121.9 %reduce-scatter.12.cloned.1.call-start = ((), (), s32[]{:S(2)}) async-start(), calls=%async_computation.12 | async-start | bytes 3932160 | tf_op jit(solution)/shard_map/reduce_scatter | solution.py:77
  621.6 158.6 %all-gather.17.cloned.1.call-start = ((), (), s32[]{:S(2)}) async-start(), calls=%async_computation.17 | async-start | bytes 1966080 | tf_op jit(solution)/shard_map/all_gather | solution.py:73
  743.1 91.8 %reduce-scatter.20.cloned.1.call-start = ((), (), s32[]{:S(2)}) async-start(), calls=%async_computation.19 | async-start | bytes 983040 | tf_op jit(solution)/shard_map/reduce_scatter | solution.py:326
  756.3 189.2 %all-reduce.5.cloned.1.call-start = ((), (), s32[]{:S(2)}) async-start(), calls=%async_computation.20 | async-start | bytes 18874368 | tf_op jit(solution)/shard_map/psum | solution.py:411
  807.7 201.5 %reduce-scatter.18.cloned.1.call-start = ((), (), s32[]{:S(2)}) async-start(), calls=%async_computation.18 | async-start | bytes 3932160 | tf_op jit(solution)/shard_map/reduce_scatter | solution.py:77
  985.8 65.6 %copy-start.27 = (f32[256,768]{1,0:T(8,128)S(1)}, f32[256,768]{1,0:T(8,128)}, u32[]{:S(2)}) copy-start(f32[256,768]{1,0:T(8,128)} %get-tuple-element.205) | copy-start | bytes 2359300
  985.8 67.8 %copy-start.1 = (f32[32,12]{0,1:T(8,128)S(1)}, f32[32,12]{0,1:T(8,128)}, u32[]{:S(2)}) copy-start(f32[32,12]{0,1:T(8,128)} %param.15) | copy-start | bytes 4612
  (160 other events, 515.4 us)
Sparse Core Ops, SparseCore 0:
  12.5 39.7 all-gather.6
  233.1 63.1 reduce-scatter.7
  299.5 42.9 all-gather.8
  354.3 60.2 reduce-scatter.9
  418.0 36.9 all-gather.10
  456.4 35.8 all-gather.12
  503.0 59.2 reduce-scatter.13
  566.8 36.9 all-gather.14
  617.5 59.2 reduce-scatter.15
  678.9 60.3 reduce-scatter.11
  743.2 36.9 all-gather.16
  782.4 22.0 reduce-scatter.19
  808.3 137.1 all-reduce.4
  947.7 61.4 reduce-scatter.17
where the time goes:
time: 1070 us; the launch traced here: 1060 us
  waiting for transfers between devices  517 us (48%)
  other arithmetic  219 us (20%)
  matrix products  168 us (16%)
  blocking collectives  85.5 us (8%)
  local copies, waits for them, and re-layouts  52.6 us (5%)
  between operations  17.6 us (2%)
    reduce_scatter x6, waiting for transfers between devices, reduce_rows(): lax.psum_scatter(partial_sum, 'narrow', scatter_dimension=0, tiled=True)  308 us
    all_gather x6, waiting for transfers between devices, gather_rows(): return lax.all_gather(row_values, 'narrow', axis=0, tiled=True)  136 us
    eq x16, other arithmetic, self_geometry(): bucket_tile[None] == bucket_number  126 us
    psum x1, waiting for transfers between devices, local(): summed = lax.psum((self_local, cross_local, ffn_local_grads), 'wide')  72.4 us
    dot_general x4, matrix products, block_scores(): jnp.einsum('qhd,khd->hqk', split_heads(queries, head_count), split_heads(...  55.8 us
    psum x1, blocking collectives, local(): lax.psum((jnp.stack([gain_one, gain_two, gain_three]), rel_full), ('wide'...  40.6 us
    dot_general x11, matrix products, matmul(): return jnp.dot(left_side, right_side, preferred_element_type=jnp.float32)  25.2 us
    all_gather x1, blocking collectives, local(): memory_full = lax.all_gather(memory, 'narrow', axis=1, tiled=True)  24.3 us
  transfers between devices with their start and end apart: 14, of which 12 were waited for; matrix products, arithmetic and copies ran while one was open for 28% of the time, Pallas kernels for 0%

commit v1 on v0

v1 whole, which is shorter than its diff:
```python
import functools
import math

import jax
import jax.numpy as jnp
import numpy as np
from jax import lax
from jax.experimental import pallas as pl
from jax.experimental.pallas import tpu as pltpu
from jax.sharding import PartitionSpec as P

BUCKETS = 32
MAX_DIST = 128
EPS = 1e-06
MASKED = -1000000000.0
MESH = pl.DeviceIdType.MESH
BF = jnp.bfloat16
F32 = jnp.float32
VMEM_LIMIT = 64 * 1024 * 1024 - 65536


def bucket_table(seq_length, bucket_count, max_distance):
    exact_count = bucket_count // 2
    bucket_ids = np.zeros((seq_length,), np.int32)
    for distance in range(seq_length):
        if distance < exact_count:
            bucket_ids[distance] = distance
        else:
            scaled_log = (
                math.log(distance / exact_count)
                / math.log(max_distance / exact_count)
                * (bucket_count - exact_count)
            )
            bucket_ids[distance] = min(bucket_count - 1, exact_count + int(scaled_log))
    return bucket_ids


def mm(a, b):
    return jnp.dot(a, b, preferred_element_type=F32)


def mm_nt(a, b):
    return lax.dot_general(a, b, (((1,), (1,)), ((), ())), preferred_element_type=F32)


def mm_tn(a, b):
    return lax.dot_general(a, b, (((0,), (0,)), ((), ())), preferred_element_type=F32)


def inv_rms(v):
    return lax.rsqrt(jnp.mean(v * v, axis=-1, keepdims=True) + EPS)


def norm_back(v, gain, dh):
    r = inv_rms(v)
    gain_part = jnp.sum(dh * (v * r), axis=0, keepdims=True)
    gd = gain * dh
    dv = r * gd - v * (r * r * r) * jnp.mean(gd * v, axis=-1, keepdims=True)
    return gain_part, dv


def soft_cols(scores):
    e = jnp.exp(scores - jnp.max(scores, axis=0, keepdims=True))
    return e * (1.0 / jnp.sum(e, axis=0, keepdims=True))


def self_mask_store(mask_ref, segk_ref, segq_ref, rows, span):
    for b in range(2):
        r = lax.broadcasted_iota(jnp.int32, (span, 128), 0)
        c = lax.broadcasted_iota(jnp.int32, (span, 128), 1)
        allowed = (c + 2 * rows >= r) & (
            segk_ref[b * 128 : b * 128 + span, :] == segq_ref[:, b * 128 : b * 128 + 128]
        )
        mask_ref[b] = jnp.where(allowed, 1.0, 0.0)


def self_fwd_kernel(
    z_ref, xt_ref, tok_ref, gain_ref, w_ref, bd_ref, segq_ref, segk_ref,
    x1_ref, h1_ref, q_ref, kv_ref, o_ref, bias_ref,
    mask_ref,
):
    rows = tok_ref.shape[0]
    ext = 3 * rows
    span = 2 * rows + 128
    hw = q_ref.shape[2]
    heads = hw // 64
    j = pl.program_id(0)

    @pl.when(j == 0)
    def _():
        g = gain_ref[0:1, :]
        for t in range(2):
            v = jnp.where(z_ref[0] >= 2 - t, xt_ref[t].astype(F32), 0.0)
            h1_ref[t * rows : (t + 1) * rows, :] = (v * inv_rms(v) * g).astype(BF)
        x = tok_ref[...].astype(F32)
        x1_ref[...] = x
        h1_ref[2 * rows : ext, :] = (x * inv_rms(x) * g).astype(BF)
        self_mask_store(mask_ref, segk_ref, segq_ref, rows, span)

    q = mm(h1_ref[2 * rows : ext, :], w_ref[:, 0:hw]).astype(BF)
    kv = mm(h1_ref[...], w_ref[:, 2 * hw : 4 * hw]).astype(BF)
    q_ref[0] = q
    kv_ref[0] = kv
    parts = []
    for hh in range(heads):
        line = jnp.broadcast_to(bd_ref[0, hh : hh + 1, :], (256, 512))
        bias = pltpu.roll(line, 0, 1, stride=1, stride_axis=0)[:, 0:128]
        bias_ref[0, hh] = bias
        far = bd_ref[0, hh : hh + 1, 127:128]
        cols = []
        for b in range(2):
            k = kv[b * 128 : b * 128 + span, hh * 64 : hh * 64 + 64]
            v = kv[b * 128 : b * 128 + span, hw + hh * 64 : hw + hh * 64 + 64]
            qb = q[b * 128 : b * 128 + 128, hh * 64 : hh * 64 + 64]
            s = mm_nt(k, qb)
            s = jnp.concatenate([s[: span - 256] + far, s[span - 256 :] + bias], axis=0)
            s = jnp.where(mask_ref[b] > 0.5, s, MASKED)
            p = soft_cols(s).astype(BF)
            cols.append(mm_tn(v, p))
        parts.append(jnp.concatenate(cols, axis=1))
    o = jnp.concatenate(parts, axis=0).T.astype(BF)
    o_ref[0] = o
    x1_ref[...] += mm_nt(o, w_ref[:, hw : 2 * hw])


def self_bwd_kernel(
    g1_ref, gain_ref, w_ref, h1_ref, q_ref, kv_ref, o_ref, bias_ref, bd_ref, segq_ref, segk_ref,
    grad_ref, dh_ref, dx_ref, rel_ref,
    mask_ref, da_ref, flip_ref, acc_ref,
):
    rows = g1_ref.shape[0]
    ext = 3 * rows
    span = 2 * rows + 128
    hw = q_ref.shape[2]
    heads = hw // 64
    j = pl.program_id(0)

    @pl.when(j == 0)
    def _():
        da_ref[...] = g1_ref[...].astype(BF)
        self_mask_store(mask_ref, segk_ref, segq_ref, rows, span)
        r = lax.broadcasted_iota(jnp.int32, (256, 256), 0)
        c = lax.broadcasted_iota(jnp.int32, (256, 256), 1)
        flip_ref[...] = jnp.where(r + c == 255, 1.0, 0.0).astype(BF)
        acc_ref[...] = jnp.zeros_like(acc_ref)

    da = da_ref[...]
    q = q_ref[0]
    kv = kv_ref[0]
    do = mm(da, w_ref[:, hw : 2 * hw]).astype(BF)
    dq_parts, dk_parts, dv_parts = [], [], []
    for hh in range(heads):
        far = bd_ref[0, hh : hh + 1, 127:128]
        dq_cols, dks, dvs = [], [], []
        band = jnp.zeros((256, 128), F32)
        total = jnp.zeros((1, 128), F32)
        for b in range(2):
            k = kv[b * 128 : b * 128 + span, hh * 64 : hh * 64 + 64]
            v = kv[b * 128 : b * 128 + span, hw + hh * 64 : hw + hh * 64 + 64]
            qb = q[b * 128 : b * 128 + 128, hh * 64 : hh * 64 + 64]
            dob = do[b * 128 : b * 128 + 128, hh * 64 : hh * 64 + 64]
            s = mm_nt(k, qb)
            s = jnp.concatenate([s[: span - 256] + far, s[span - 256 :] + bias_ref[0, hh]], axis=0)
            s = jnp.where(mask_ref[b] > 0.5, s, MASKED)
            p = soft_cols(s)
            dp = mm_nt(v, dob)
            ds = (p * (dp - jnp.sum(p * dp, axis=0, keepdims=True))).astype(BF)
            dvs.append(mm(p.astype(BF), dob))
            dks.append(mm(ds, qb))
            dq_cols.append(mm_tn(k, ds))
            band = band + mm(flip_ref[...], ds[span - 256 :])
            total = total + jnp.sum(ds[: span - 256].astype(F32), axis=0, keepdims=True)
        gap = jnp.zeros((128, 64), F32)
        dk_parts.append(jnp.concatenate([dks[0], gap], 0) + jnp.concatenate([gap, dks[1]], 0))
        dv_parts.append(jnp.concatenate([dvs[0], gap], 0) + jnp.concatenate([gap, dvs[1]], 0))
        dq_parts.append(jnp.concatenate(dq_cols, axis=1))
        wide_band = jnp.concatenate([band, jnp.zeros((256, 384), F32)], axis=1)
        aligned = pltpu.roll(wide_band, 0, 1, stride=1, stride_axis=0)
        line = jnp.sum(aligned, axis=0, keepdims=True)
        lane = lax.broadcasted_iota(jnp.int32, (1, 512), 1)
        far_sum = jnp.sum(total, axis=1, keepdims=True)
        rel_ref[0, hh : hh + 1, :] = jnp.where(lane == 511, far_sum, line)
    dq = jnp.concatenate(dq_parts, axis=0).T.astype(BF)
    dkv = jnp.concatenate(dk_parts + dv_parts, axis=1).astype(BF)
    zero = jnp.zeros((rows, hw), BF)
    left = jnp.concatenate([h1_ref[2 * rows : ext, :], da], axis=0)
    right = jnp.concatenate(
        [jnp.concatenate([dq, zero], axis=1), jnp.concatenate([zero, o_ref[0]], axis=1)], axis=0
    )
    grad_ref[0, :, 0 : 2 * hw] = mm_tn(left, right).astype(BF)
    grad_ref[0, :, 2 * hw : 4 * hw] = mm_tn(h1_ref[...], dkv).astype(BF)
    acc_ref[...] += mm_nt(dkv, w_ref[:, 2 * hw : 4 * hw])
    acc_ref[2 * rows : ext, :] += mm_nt(dq, w_ref[:, 0:hw])

    @pl.when(j == 3)
    def _():
        dh_ref[...] = acc_ref[2 * rows : ext, :]
        for t in range(2):
            dx_ref[t] = acc_ref[t * rows : (t + 1) * rows, :].astype(BF)


def cross_fwd_kernel(valid_ref, x1_ref, gain_ref, w_ref, mem_ref, x2_ref, h2_ref, q_ref, kv_ref, o_ref):
    rows = x1_ref.shape[0]
    mem = mem_ref.shape[0]
    hw = q_ref.shape[2]
    heads = hw // 64
    j = pl.program_id(0)

    @pl.when(j == 0)
    def _():
        x1 = x1_ref[...]
        x2_ref[...] = x1
        h2_ref[...] = (x1 * inv_rms(x1) * gain_ref[1:2, :]).astype(BF)

    q = mm(h2_ref[...], w_ref[:, 0:hw]).astype(BF)
    kv = mm(mem_ref[...], w_ref[:, 2 * hw : 4 * hw]).astype(BF)
    q_ref[0] = q
    kv_ref[0] = kv
    allowed = lax.broadcasted_iota(jnp.int32, (mem, rows), 0) < valid_ref[0]
    parts = []
    for hh in range(heads):
        k = kv[:, hh * 64 : hh * 64 + 64]
        v = kv[:, hw + hh * 64 : hw + hh * 64 + 64]
        s = jnp.where(allowed, mm_nt(k, q[:, hh * 64 : hh * 64 + 64]), MASKED)
        parts.append(mm_tn(v, soft_cols(s).astype(BF)))
    o = jnp.concatenate(parts, axis=0).T.astype(BF)
    o_ref[0] = o
    x2_ref[...] += mm_nt(o, w_ref[:, hw : 2 * hw])


def cross_bwd_kernel(
    valid_ref, g2_ref, x1_ref, gain_ref, w_ref, mem_ref, h2_ref, q_ref, kv_ref, o_ref,
    grad_ref, g1_ref, dmem_ref, gsum_ref,
    dc_ref, dh_ref, macc_ref,
):
    rows = g2_ref.shape[0]
    mem = mem_ref.shape[0]
    hw = q_ref.shape[2]
    heads = hw // 64
    j = pl.program_id(0)

    @pl.when(j == 0)
    def _():
        dc_ref[...] = g2_ref[...].astype(BF)
        dh_ref[...] = jnp.zeros_like(dh_ref)
        macc_ref[...] = jnp.zeros_like(macc_ref)

    dc = dc_ref[...]
    q = q_ref[0]
    kv = kv_ref[0]
    do = mm(dc, w_ref[:, hw : 2 * hw]).astype(BF)
    allowed = lax.broadcasted_iota(jnp.int32, (mem, rows), 0) < valid_ref[0]
    dq_parts, dk_parts, dv_parts = [], [], []
    for hh in range(heads):
        k = kv[:, hh * 64 : hh * 64 + 64]
        v = kv[:, hw + hh * 64 : hw + hh * 64 + 64]
        qh = q[:, hh * 64 : hh * 64 + 64]
        doh = do[:, hh * 64 : hh * 64 + 64]
        p = soft_cols(jnp.where(allowed, mm_nt(k, qh), MASKED))
        dp = mm_nt(v, doh)
        ds = (p * (dp - jnp.sum(p * dp, axis=0, keepdims=True))).astype(BF)
        dv_parts.append(mm(p.astype(BF), doh))
        dk_parts.append(mm(ds, qh))
        dq_parts.append(mm_tn(k, ds))
    dq = jnp.concatenate(dq_parts, axis=0).T.astype(BF)
    dkv = jnp.concatenate(dk_parts + dv_parts, axis=1).astype(BF)
    zero = jnp.zeros((rows, hw), BF)
    left = jnp.concatenate([h2_ref[...], dc], axis=0)
    right = jnp.concatenate(
        [jnp.concatenate([dq, zero], axis=1), jnp.concatenate([zero, o_ref[0]], axis=1)], axis=0
    )
    grad_ref[0, :, 0 : 2 * hw] = mm_tn(left, right).astype(BF)
    grad_ref[0, :, 2 * hw : 4 * hw] = mm_tn(mem_ref[...], dkv).astype(BF)
    dh_ref[...] += mm_nt(dq, w_ref[:, 0:hw])
    macc_ref[...] += mm_nt(dkv, w_ref[:, 2 * hw : 4 * hw])

    @pl.when(j == 3)
    def _():
        gain_part, dv = norm_back(x1_ref[...], gain_ref[1:2, :], dh_ref[...])
        gsum_ref[...] = jnp.broadcast_to(gain_part, gsum_ref.shape)
        g1_ref[...] = g2_ref[...] + dv
        dmem_ref[...] = macc_ref[...].astype(BF)


def ffn_kernel(
    x2_ref, cot_ref, gain_ref, wa_ref, wb_ref,
    out_ref, g2_ref, grad_ref, gsum_ref,
    h3_ref, acc_ref, dh_ref,
):
    fw = wa_ref.shape[1] * 2 // 3
    j = pl.program_id(0)

    @pl.when(j == 0)
    def _():
        x2 = x2_ref[...]
        acc_ref[...] = x2
        h3_ref[...] = (x2 * inv_rms(x2) * gain_ref[2:3, :]).astype(BF)
        dh_ref[...] = jnp.zeros_like(dh_ref)

    h3 = h3_ref[...]
    df = cot_ref[...]
    wg = wa_ref[:, 0:fw]
    wu = jnp.concatenate([wa_ref[:, fw:], wb_ref[:, 0 : fw // 2]], axis=1)
    wd = wb_ref[:, fw // 2 :]
    gate = mm(h3, wg)
    up = mm(h3, wu)
    c0 = math.sqrt(2.0 / math.pi)
    gate2 = gate * gate
    t = jnp.tanh(c0 * (gate + 0.044715 * gate2 * gate))
    half = 0.5 * (1.0 + t)
    gelu = gate * half
    slope = half + 0.5 * gate * (1.0 - t * t) * (c0 * (1.0 + 3.0 * 0.044715 * gate2))
    act = (gelu * up).astype(BF)
    acc_ref[...] += mm_nt(act, wd)
    da = mm(df, wd)
    dgate = (da * up * slope).astype(BF)
    dup = (da * gelu).astype(BF)
    dgu = jnp.concatenate([dgate, dup], axis=1)
    ggu = mm_tn(h3, dgu).astype(BF)
    grad_ref[0, 0] = ggu[:, 0 : fw * 3 // 2]
    grad_ref[0, 1, :, 0 : fw // 2] = ggu[:, fw * 3 // 2 :]
    grad_ref[0, 1, :, fw // 2 :] = mm_tn(df, act).astype(BF)
    dh_ref[...] += mm_nt(dgate, wg) + mm_nt(dup, wu)

    @pl.when(j == 3)
    def _():
        out_ref[...] = acc_ref[...].astype(BF)
        gain_part, dv = norm_back(x2_ref[...], gain_ref[2:3, :], dh_ref[...])
        gsum_ref[...] = jnp.broadcast_to(gain_part, gsum_ref.shape)
        g2_ref[...] = df.astype(F32) + dv


def full(shape):
    return pl.BlockSpec(shape, lambda j: (0,) * len(shape))


def slot(shape):
    return pl.BlockSpec((1,) + shape, lambda j: (j,) + (0,) * len(shape))


def weight(chunk, shape):
    return pl.BlockSpec((None, None) + shape, lambda j: (chunk, j, 0, 0))


SMEM_SPEC = pl.BlockSpec(memory_space=pltpu.SMEM)


def grid_call(kernel, name, in_specs, out, scratch, args, flops):
    shapes = [jax.ShapeDtypeStruct(s, d) for s, d, _ in out]
    nbytes = sum(math.prod(s) * jnp.dtype(d).itemsize for s, d, _ in out) + 4 * 768 * 768 * 2
    return pl.pallas_call(
        kernel,
        name=name,
        grid=(4,),
        in_specs=in_specs,
        out_specs=[spec for _, _, spec in out],
        out_shape=shapes,
        scratch_shapes=scratch,
        compiler_params=pltpu.CompilerParams(
            dimension_semantics=("arbitrary",), vmem_limit_bytes=VMEM_LIMIT
        ),
        cost_estimate=pl.CostEstimate(flops=flops, bytes_accessed=nbytes, transcendentals=0),
    )(*args)


class Place:
    def __init__(self):
        self.w = lax.axis_index("wide")
        self.z = lax.axis_index("narrow")
        s = lax.rem(self.w, 8)
        self.s = s
        self.c = lax.rem(s, 2)
        self.x = lax.rem(s // 2, 2)
        self.y = s // 4
        dc, dx, dy = 1 - 2 * self.c, 2 * (1 - 2 * self.x), 4 * (1 - 2 * self.y)
        self.core_dev = {"wide": self.w + dc}
        self.x_dev = {"wide": self.w + dx}
        self.y_dev = {"wide": self.w + dy}
        self.sx, self.sy, self.sxy = s + dx, s + dy, s + dx + dy
        self.dc = dc

    def narrow_dev(self, k):
        return {"narrow": lax.rem(self.z + k, 4)}

    def barrier(self):
        sem = pltpu.get_barrier_semaphore()
        devs = [self.core_dev, self.x_dev, self.y_dev] + [self.narrow_dev(k) for k in (1, 2, 3)]
        for dev in devs:
            pl.semaphore_signal(sem, inc=1, device_id=dev, device_id_type=MESH)
        pl.semaphore_wait(sem, len(devs))


def remote(src, dst, send_sem, recv_sem, dev):
    return pltpu.make_async_remote_copy(
        src_ref=src, dst_ref=dst, send_sem=send_sem, recv_sem=recv_sem, device_id=dev, device_id_type=MESH
    )


def gather_kernel(
    p_ref, tok_ref, mem_ref,
    w_ref, xt_ref, mt_ref,
    stage, mstage, zs, zr, ps, pr, ts, tr, ms, mr, ls, lm,
):
    at = Place()
    z, s = at.z, at.s
    chunks = p_ref.shape[0]
    at.barrier()

    def own(c):
        return p_ref.at[c, pl.ds(2 * s, 2)]

    def up0(c):
        return remote(own(c), w_ref.at[c, 3, pl.ds(2 * s, 2)], zs.at[c, 0], zr.at[c, 3], {"narrow": z + 1})

    def down0(c):
        return remote(own(c), w_ref.at[c, 1, pl.ds(2 * s, 2)], zs.at[c, 1], zr.at[c, 1], {"narrow": z - 1})

    def tok1():
        return remote(tok_ref, xt_ref.at[1], ts.at[0], tr.at[1], {"narrow": z + 1})

    def tok2():
        return remote(tok_ref, xt_ref.at[0], ts.at[1], tr.at[0], {"narrow": z + 2})

    def memk(k):
        return remote(mem_ref, mt_ref.at[z], ms.at[k - 1], mr.at[k - 1], at.narrow_dev(k))

    def start_z(c):
        @pl.when(z < 3)
        def _():
            up0(c).start()

        @pl.when(z > 0)
        def _():
            down0(c).start()

    start_z(0)

    @pl.when(z < 3)
    def _():
        tok1().start()

    @pl.when(z < 2)
    def _():
        tok2().start()

    for c in range(1, chunks):
        start_z(c)
    for k in (1, 2, 3):
        memk(k).start()

    mem_in = pltpu.make_async_copy(mem_ref, mstage, lm.at[0])
    mem_in.start()
    loads = [pltpu.make_async_copy(p_ref.at[c], stage.at[c], ls.at[c]) for c in range(chunks)]
    for copy in loads:
        copy.start()
    mem_in.wait()
    mem_out = pltpu.make_async_copy(mstage, mt_ref.at[z], lm.at[1])
    mem_out.start()
    stores = [pltpu.make_async_copy(stage.at[c], w_ref.at[c, 0], ls.at[chunks + c]) for c in range(chunks)]
    for load, store in zip(loads, stores):
        load.wait()
        store.start()

    e0 = 1 - (z + 3) // 4
    e3 = z // 3
    e1 = (1 - z // 2) * lax.rem(z, 2)
    e2 = (z // 2) * (1 - lax.rem(z, 2))
    order = [e0 * 1 + e1 * 3 + e2 * 1 + e3 * 3, e0 * 2 + e1 * 1 + e2 * 3 + e3 * 2, e0 * 3 + e1 * 2 + e2 * 2 + e3 * 1]
    onward = {1: [(3, 2, 1), (1, 2, -1), (2, 3, -1)], 2: [(1, 2, -1), (3, 2, 1), (2, 1, 1)]}

    def forward(c, r, k):
        here, there, step = onward[k][r]
        return remote(
            w_ref.at[c, here, pl.ds(2 * s, 2)], w_ref.at[c, there, pl.ds(2 * s, 2)],
            zs.at[c, 2 + r], zr.at[c, there], {"narrow": k + step},
        )

    def piece(c, r, kind):
        sl = order[r]
        i = c * 3 + r
        table = {
            0: (2 * s, 1, at.x_dev), 1: (2 * s + 1, 1, at.x_dev), 2: (2 * at.sy + 1, 1, at.x_dev),
            3: (2 * s + 1, 1, at.y_dev), 4: (2 * s, 1, at.y_dev), 5: (2 * at.sx, 1, at.y_dev),
            6: (2 * s, 2, at.core_dev), 7: (2 * at.sx, 2, at.core_dev),
            8: (2 * at.sy, 2, at.core_dev), 9: (2 * at.sxy, 2, at.core_dev),
        }
        first, n, dev = table[kind]
        region = w_ref.at[c, sl, pl.ds(first, n)]
        return remote(region, region, ps.at[i, kind], pr.at[i, kind], dev)

    def arrived(c, r, kind):
        sl = order[r]
        i = c * 3 + r
        table = {
            0: (2 * at.sx, 1), 1: (2 * at.sx + 1, 1), 2: (2 * at.sxy + 1, 1),
            3: (2 * at.sy + 1, 1), 4: (2 * at.sy, 1), 5: (2 * at.sxy, 1),
            6: (2 * (s + at.dc), 2), 7: (2 * (at.sx + at.dc), 2),
            8: (2 * (at.sy + at.dc), 2), 9: (2 * (at.sxy + at.dc), 2),
        }
        first, n = table[kind]
        region = w_ref.at[c, sl, pl.ds(first, n)]
        remote(region, region, ps.at[i, kind], pr.at[i, kind], at.x_dev).wait_recv()

    def step0(c, r):
        sl = order[r]
        region = w_ref.at[c, sl, pl.ds(2 * s, 2)]
        remote(region, region, zs.at[c, 0], zr.at[c, sl], at.x_dev).wait_recv()
        for k in (1, 2):
            @pl.when(z == k)
            def _():
                forward(c, r, k).start()
        for kind in (0, 3, 4, 1, 6):
            piece(c, r, kind).start()

    def step1(c, r):
        arrived(c, r, 0)
        piece(c, r, 5).start()
        arrived(c, r, 3)
        piece(c, r, 2).start()
        arrived(c, r, 1)
        piece(c, r, 7).start()
        arrived(c, r, 4)
        piece(c, r, 8).start()

    def step2(c, r):
        arrived(c, r, 5)
        arrived(c, r, 2)
        piece(c, r, 9).start()

    pieces = [(c, r) for c in range(chunks) for r in range(3)]
    for t in range(len(pieces) + 2):
        if t < len(pieces):
            step0(*pieces[t])
        if 0 <= t - 1 < len(pieces):
            step1(*pieces[t - 1])
        if 0 <= t - 2 < len(pieces):
            step2(*pieces[t - 2])

    for c, r in pieces:
        for kind in (6, 7, 8, 9):
            arrived(c, r, kind)
        for kind in range(10):
            piece(c, r, kind).wait_send()
        for k in (1, 2):
            @pl.when(z == k)
            def _():
                forward(c, r, k).wait_send()
    for c in range(chunks):
        stores[c].wait()

        @pl.when(z < 3)
        def _():
            up0(c).wait_send()

        @pl.when(z > 0)
        def _():
            down0(c).wait_send()

    mem_out.wait()
    for k in (1, 2, 3):
        memk(k).wait_send()
        here = mt_ref.at[lax.rem(z + 4 - k, 4)]
        remote(here, here, ms.at[k - 1], mr.at[k - 1], at.x_dev).wait_recv()

    @pl.when(z < 3)
    def _():
        tok1().wait_send()

    @pl.when(z < 2)
    def _():
        tok2().wait_send()

    @pl.when(z > 0)
    def _():
        tok1().wait_recv()

    @pl.when(z > 1)
    def _():
        tok2().wait_recv()


def gather(packed, tokens, memory):
    rows, width = tokens.shape
    chunks = packed.shape[0]
    half = packed.shape[2]
    any_spec = pl.BlockSpec(memory_space=pl.ANY)
    dma = pltpu.SemaphoreType.DMA
    return pl.pallas_call(
        gather_kernel,
        name="gather",
        in_specs=[any_spec] * 3,
        out_specs=[any_spec] * 3,
        out_shape=[
            jax.ShapeDtypeStruct((chunks, 4) + packed.shape[1:], BF),
            jax.ShapeDtypeStruct((2, rows, width), BF),
            jax.ShapeDtypeStruct((4,) + memory.shape, BF),
        ],
        scratch_shapes=[
            pltpu.VMEM((chunks, 16, half, width), BF),
            pltpu.VMEM(memory.shape, BF),
            dma((chunks, 5)), dma((chunks, 4)),
            dma((chunks * 3, 10)), dma((chunks * 3, 10)),
            dma((2,)), dma((2,)), dma((3,)), dma((3,)), dma((2 * chunks,)), dma((2,)),
        ],
        compiler_params=pltpu.CompilerParams(
            collective_id=0, has_side_effects=True, vmem_limit_bytes=VMEM_LIMIT
        ),
    )(packed, tokens, memory)


QUARTERS = (3, 0, 2, 1)


def reduce_kernel(
    gf_ref, gc_ref, gs_ref, dx_ref, dm_ref, dh_ref, tok_ref, g1_ref, gain_ref,
    f_ref, tg_ref, mg_ref, gsum_ref,
    own, rc, xr, yr, x2, y2, zu, zd, dxr, dmr,
    lsem, cs, cr, xs, xrs, ys, yrs, x2s, x2r, y2s, y2r, us, ur, ds_, dr, dxs, dxrs, dms, dmrs,
):
    at = Place()
    z = at.z
    half = own.shape[3] // 2
    at.barrier()
    groups = [
        (2, lambda j: gf_ref.at[j, 0]), (3, lambda j: gf_ref.at[j, 1]),
        (1, lambda j: gc_ref.at[j]), (0, lambda j: gs_ref.at[j]),
    ]
    chunks = [(out, get, q) for out, get in groups for q in QUARTERS]
    n = len(chunks)

    def dx_send(t):
        return remote(dx_ref.at[t], dxr.at[t], dxs.at[t], dxrs.at[t], {"narrow": z - 2 + t})

    def dm_send(k):
        return remote(dm_ref.at[lax.rem(z + k, 4)], dmr.at[k - 1], dms.at[k - 1], dmrs.at[k - 1], at.narrow_dev(k))

    def core_send(i):
        _, get, q = chunks[i]
        src = get(lax.rem(q + 4 - z, 4)).at[:, pl.ds(1 - at.c, 1)]
        return remote(src, rc.at[i], cs.at[i], cr.at[i], at.core_dev)

    def load(i):
        _, get, q = chunks[i]
        src = get(lax.rem(q + 4 - z, 4)).at[:, pl.ds(at.c, 1)]
        return pltpu.make_async_copy(src, own.at[i], lsem.at[i])

    for i in range(n):
        load(i).start()
        core_send(i).start()
    for t in range(2):
        @pl.when(z >= 2 - t)
        def _():
            dx_send(t).start()
    for k in (1, 2, 3):
        dm_send(k).start()

    lo, hi = pl.ds(0, half), pl.ds(half, half)
    yx = 2 * at.y + at.x

    def add(ref, other):
        ref[...] = (ref[...].astype(F32) + other[...].astype(F32)).astype(BF)

    def x_send(i, yb):
        return remote(own.at[i, 2 * yb + 1 - at.x, 0, lo], xr.at[i, yb], xs.at[i, yb], xrs.at[i, yb], at.x_dev)

    def y_send(i, xb):
        return remote(own.at[i, 2 * (1 - at.y) + xb, 0, hi], yr.at[i, xb], ys.at[i, xb], yrs.at[i, xb], at.y_dev)

    def y2_send(i):
        return remote(own.at[i, 2 * (1 - at.y) + at.x, 0, lo], y2.at[i], y2s.at[i], y2r.at[i], at.y_dev)

    def x2_send(i):
        return remote(own.at[i, 2 * at.y + 1 - at.x, 0, hi], x2.at[i], x2s.at[i], x2r.at[i], at.x_dev)

    def step_b(i):
        load(i).wait()
        core_send(i).wait_recv()
        add(own.at[i], rc.at[i])
        for b in range(2):
            x_send(i, b).start()
            y_send(i, b).start()

    def step_c(i):
        for b in range(2):
            x_send(i, b).wait_recv()
            y_send(i, b).wait_recv()
            add(own.at[i, 2 * b + at.x, 0, lo], xr.at[i, b])
            add(own.at[i, 2 * at.y + b, 0, hi], yr.at[i, b])
        y2_send(i).start()
        x2_send(i).start()

    def step_d(i):
        y2_send(i).wait_recv()
        add(own.at[i, yx, 0, lo], y2.at[i])
        x2_send(i).wait_recv()
        add(own.at[i, yx, 0, hi], x2.at[i])

    def up(i, k):
        return remote(own.at[i, yx, 0], zu.at[i], us.at[i], ur.at[i], {"narrow": k + 1})

    def down(i, k):
        return remote(own.at[i, yx, 0], zd.at[i], ds_.at[i], dr.at[i], {"narrow": k - 1})

    def step_e(i, h):
        out, _, q = chunks[i]
        if h < q:
            @pl.when(z == h)
            def _():
                if h > 0:
                    up(i, 0).wait_recv()
                    add(own.at[i, yx, 0], zu.at[i])
                up(i, h).start()
        k = 3 - h
        if k > q:
            @pl.when(z == k)
            def _():
                if k < 3:
                    down(i, 3).wait_recv()
                    add(own.at[i, yx, 0], zd.at[i])
                down(i, k).start()
        if h == max(q, 3 - q):
            @pl.when(z == q)
            def _():
                total = own[i, yx, 0].astype(F32)
                if q > 0:
                    up(i, 0).wait_recv()
                    total = total + zu[i].astype(F32)
                if q < 3:
                    down(i, 3).wait_recv()
                    total = total + zd[i].astype(F32)
                f_ref[out] = total

    for t in range(n + 6):
        if t < n:
            step_b(t)
        if 0 <= t - 1 < n:
            step_c(t - 1)
        if 0 <= t - 2 < n:
            step_d(t - 2)
        for h in range(4):
            if 0 <= t - 3 - h < n:
                step_e(t - 3 - h, h)
        if t == 8:
            mg_ref[...] = dm_ref[z].astype(F32)
            for k in (1, 2, 3):
                dm_send(k).wait_recv()
                mg_ref[...] += dmr[k - 1].astype(F32)
            tg_ref[...] = dh_ref[...]
            for d in range(2):
                @pl.when(z < 2 + d)
                def _():
                    dx_send(d).wait_recv()
                    tg_ref[...] += dxr[d].astype(F32)
            gain_part, dv = norm_back(tok_ref[...].astype(F32), gain_ref[0:1, :], tg_ref[...])
            gsum_ref[...] = jnp.broadcast_to(gain_part, gsum_ref.shape)
            tg_ref[...] = g1_ref[...] + dv

    for i in range(n):
        q = chunks[i][2]
        core_send(i).wait_send()
        for b in range(2):
            x_send(i, b).wait_send()
            y_send(i, b).wait_send()
        y2_send(i).wait_send()
        x2_send(i).wait_send()

        @pl.when(z < q)
        def _():
            up(i, 0).wait_send()

        @pl.when(z > q)
        def _():
            down(i, 3).wait_send()
    for t in range(2):
        @pl.when(z >= 2 - t)
        def _():
            dx_send(t).wait_send()
    for k in (1, 2, 3):
        dm_send(k).wait_send()


def reduce_grads(gf, gc, gs, dx, dm, dh, tok, g1, gains):
    own, width = gs.shape[3:]
    half = own // 2
    rows = tok.shape[0]
    n = 16
    any_spec = pl.BlockSpec(memory_space=pl.ANY)
    vmem = pl.BlockSpec(memory_space=pltpu.VMEM)
    dma = pltpu.SemaphoreType.DMA
    return pl.pallas_call(
        reduce_kernel,
        name="reduce",
        in_specs=[any_spec] * 3 + [vmem] * 6,
        out_specs=[vmem] * 4,
        out_shape=[
            jax.ShapeDtypeStruct((4, own, width), F32),
            jax.ShapeDtypeStruct((rows, width), F32),
            jax.ShapeDtypeStruct(dm.shape[1:], F32),
            jax.ShapeDtypeStruct((8, width), F32),
        ],
        scratch_shapes=[
            pltpu.VMEM((n, 4, 1, own, width), BF), pltpu.VMEM((n, 4, 1, own, width), BF),
            pltpu.VMEM((n, 2, half, width), BF), pltpu.VMEM((n, 2, half, width), BF),
            pltpu.VMEM((n, half, width), BF), pltpu.VMEM((n, half, width), BF),
            pltpu.VMEM((n, own, width), BF), pltpu.VMEM((n, own, width), BF),
            pltpu.VMEM(dx.shape, BF), pltpu.VMEM((3,) + dm.shape[1:], BF),
            dma((n,)), dma((n,)), dma((n,)),
            dma((n, 2)), dma((n, 2)), dma((n, 2)), dma((n, 2)),
            dma((n,)), dma((n,)), dma((n,)), dma((n,)),
            dma((n,)), dma((n,)), dma((n,)), dma((n,)),
            dma((2,)), dma((2,)), dma((3,)), dma((3,)),
        ],
        compiler_params=pltpu.CompilerParams(
            collective_id=1, has_side_effects=True, vmem_limit_bytes=VMEM_LIMIT
        ),
    )(gf, gc, gs, dx, dm, dh, tok, g1, gains)


def stats_kernel(
    wide_count, f_ref, a_ref,
    rsum_ref, csum_ref, asum_ref, prow_ref, pcol_ref,
    rall, aall, call, ball, rs, rr, as_, ar, cs, cr, bs, br, ps, pr,
):
    w = lax.axis_index("wide")
    z = lax.axis_index("narrow")
    own = f_ref.shape[1]
    width = f_ref.shape[2]
    sem = pltpu.get_barrier_semaphore()

    def peer(k):
        return {"narrow": lax.rem(z + k, 4)}

    def wide_peer(k):
        return {"wide": lax.rem(w + k, wide_count)}

    def wide_loop(fn):
        if wide_count <= 8:
            for k in range(1, wide_count):
                fn(k)
        else:
            pl.loop(1, wide_count)(fn)

    for k in (1, 2, 3):
        pl.semaphore_signal(sem, inc=1, device_id=peer(k), device_id_type=MESH)
    wide_loop(lambda k: pl.semaphore_signal(sem, inc=1, device_id=wide_peer(k), device_id_type=MESH))

    lane = lax.broadcasted_iota(jnp.int32, (8, width), 1)
    row = lax.broadcasted_iota(jnp.int32, (8, width), 0)
    quarter = width // 4
    third = 2 * width // 3

    def sums(pick, sq):
        got = lax.dot_general(
            jnp.where(pick, 1.0, 0.0), sq, (((1,), (1,)), ((), ())),
            preferred_element_type=F32, precision=lax.Precision.HIGHEST,
        )
        pad = jnp.zeros((8, 128 - own), F32)
        return jnp.concatenate([got, pad], axis=1)

    sq = [f_ref[i] * f_ref[i] for i in range(4)]
    rall[z, 0:8] = sums(lane // quarter == row, sq[0])
    rall[z, 8:16] = sums(lane // quarter == row, sq[1])
    rall[z, 16:24] = sums(lane // third == row, sq[2]) + sums((lane + width) // third == row, sq[3])
    aall[z] = a_ref[...]
    call[w] = jnp.concatenate(
        [jnp.sum(v, axis=0, keepdims=True) for v in sq] + [jnp.zeros((4, width), F32)], axis=0
    )
    pl.semaphore_wait(sem, 3 + wide_count - 1)

    def r_send(k):
        return remote(rall.at[z], rall.at[z], rs.at[k - 1], rr.at[k - 1], peer(k))

    def a_send(k):
        return remote(aall.at[z], aall.at[z], as_.at[k - 1], ar.at[k - 1], peer(k))

    def c_send(k):
        return remote(call.at[w], call.at[w], cs.at[k - 1], cr.at[k - 1], wide_peer(k))

    def p_send(k):
        return remote(pcol_ref.at[z], pcol_ref.at[z], ps.at[k - 1], pr.at[k - 1], peer(k))

    def b_send(k):
        return remote(ball.at[w], ball.at[w], bs.at[k - 1], br.at[k - 1], wide_peer(k))

    for k in (1, 2, 3):
        r_send(k).start()
        a_send(k).start()
    wide_loop(lambda k: c_send(k).start())

    for k in (1, 2, 3):
        frm = lax.rem(z + 4 - k, 4)
        remote(rall.at[frm], rall.at[frm], rs.at[k - 1], rr.at[k - 1], peer(k)).wait_recv()
        remote(aall.at[frm], aall.at[frm], as_.at[k - 1], ar.at[k - 1], peer(k)).wait_recv()
    rsum = rall[0] + rall[1] + rall[2] + rall[3]
    rsum_ref[...] = rsum
    asum = aall[0] + aall[1] + aall[2] + aall[3]
    zero = jnp.zeros((1, width - 128), F32)
    ball[w] = jnp.concatenate(
        [
            asum[0:4],
            jnp.concatenate([rsum[1:2], zero], axis=1),
            jnp.concatenate([rsum[9:10], zero], axis=1),
            jnp.zeros((2, width), F32),
        ],
        axis=0,
    )
    wide_loop(lambda k: b_send(k).start())

    def c_wait(k):
        frm = lax.rem(w + wide_count - k, wide_count)
        remote(call.at[frm], call.at[frm], cs.at[k - 1], cr.at[k - 1], wide_peer(k)).wait_recv()

    wide_loop(c_wait)
    csum = lax.fori_loop(1, wide_count, lambda i, v: v + call[i], call[0])
    csum_ref[...] = csum
    pcol_ref[z] = csum
    for k in (1, 2, 3):
        p_send(k).start()

    def b_wait(k):
        frm = lax.rem(w + wide_count - k, wide_count)
        remote(ball.at[frm], ball.at[frm], bs.at[k - 1], br.at[k - 1], wide_peer(k)).wait_recv()

    wide_loop(b_wait)
    asum_ref[...] = lax.fori_loop(1, wide_count, lambda i, v: v + ball[i], ball[0])
    prow_ref[...] = ball[:, :, 0:128]
    for k in (1, 2, 3):
        frm = lax.rem(z + 4 - k, 4)
        remote(pcol_ref.at[frm], pcol_ref.at[frm], ps.at[k - 1], pr.at[k - 1], peer(k)).wait_recv()
    for k in (1, 2, 3):
        r_send(k).wait_send()
        a_send(k).wait_send()
        p_send(k).wait_send()

    def sent(k):
        c_send(k).wait_send()
        b_send(k).wait_send()

    wide_loop(sent)


def reduce_stats(wide_count, final, small):
    width = final.shape[2]
    vmem = pl.BlockSpec(memory_space=pltpu.VMEM)
    dma = pltpu.SemaphoreType.DMA
    return pl.pallas_call(
        functools.partial(stats_kernel, wide_count),
        name="stats",
        in_specs=[vmem] * 2,
        out_specs=[vmem] * 5,
        out_shape=[
            jax.ShapeDtypeStruct((24, 128), F32),
            jax.ShapeDtypeStruct((8, width), F32),
            jax.ShapeDtypeStruct((8, width), F32),
            jax.ShapeDtypeStruct((wide_count, 8, 128), F32),
            jax.ShapeDtypeStruct((4, 8, width), F32),
        ],
        scratch_shapes=[
            pltpu.VMEM((4, 24, 128), F32), pltpu.VMEM((4, 8, width), F32),
            pltpu.VMEM((wide_count, 8, width), F32), pltpu.VMEM((wide_count, 8, width), F32),
            dma((3,)), dma((3,)), dma((3,)), dma((3,)),
            dma((wide_count - 1,)), dma((wide_count - 1,)), dma((wide_count - 1,)), dma((wide_count - 1,)),
            dma((3,)), dma((3,)),
        ],
        compiler_params=pltpu.CompilerParams(collective_id=2, has_side_effects=True),
    )(final, small)


def local(
    tokens, memory, segments, valid_rows, norm_gains, rel_table,
    self_weights, cross_weights, ffn_weights, cotangent,
):
    wide_count = lax.axis_size("wide")
    assert lax.axis_size("narrow") == 4 and wide_count % 8 == 0 and segments.shape[0] == 1
    z = lax.axis_index("narrow")
    rows, width = tokens.shape
    mem_own = memory.shape[1]
    mem_len = 4 * mem_own
    hw = self_weights.shape[2]
    fw = ffn_weights.shape[2]
    heads = rel_table.shape[1] // 4
    ext = 3 * rows
    span = 2 * rows + 128
    groups = wide_count // 8
    eighth = width // 8

    def qokv(w):
        return jnp.concatenate([w[0], w[3], w[1], w[2]], axis=1)

    ffn_packed = jnp.concatenate([ffn_weights[0], ffn_weights[1], ffn_weights[2]], axis=1)
    packed = jnp.stack([qokv(self_weights), qokv(cross_weights), ffn_packed[:, :width], ffn_packed[:, width:]])
    weights, earlier, mem_all = gather(packed.reshape(4, 16, width // 16, width), tokens, memory[0])
    weights = weights.reshape(4, 4, width, width)
    mem_full = mem_all.reshape(mem_len, width)

    buckets = bucket_table(1024, BUCKETS, MAX_DIST)
    lanes = np.arange(512)
    at_lane = np.where(lanes < 128, 128 + lanes, np.maximum(lanes - 384, 0))
    pick = jnp.asarray((buckets[at_lane][None, :] == np.arange(BUCKETS)[:, None]).astype(np.float32))
    bias_line = jnp.einsum("bl,bh->hl", pick, rel_table, precision=lax.Precision.HIGHEST)
    bias_line = bias_line.reshape(4, heads, 512)
    bias_line = lax.dynamic_slice_in_dim(jnp.concatenate([bias_line, bias_line], 0), z, 4, 0)
    seg = segments[0]
    seg_q = lax.dynamic_slice_in_dim(seg, z * rows, rows, 0).reshape(1, rows)
    seg_pad = jnp.concatenate([jnp.full((2 * rows,), -1, jnp.int32), seg])
    seg_k = lax.dynamic_slice_in_dim(seg_pad, z * rows, ext, 0).reshape(ext, 1)
    z_arr = z.reshape(1)

    sq = (width, width)
    vm = pltpu.VMEM
    x1, h1, q1, kv1, o1, bias = grid_call(
        self_fwd_kernel, "self_fwd",
        [SMEM_SPEC, full((2, rows, width)), full((rows, width)), full((3, width)), weight(0, sq),
         slot((heads, 512)), full((1, rows)), full((ext, 1))],
        [((rows, width), F32, full((rows, width))), ((ext, width), BF, full((ext, width))),
         ((4, rows, hw), BF, slot((rows, hw))), ((4, ext, 2 * hw), BF, slot((ext, 2 * hw))),
         ((4, rows, hw), BF, slot((rows, hw))), ((4, heads, 256, 128), F32, slot((heads, 256, 128)))],
        [vm((2, span, 128), F32)],
        (z_arr, earlier, tokens, norm_gains, weights, bias_line, seg_q, seg_k),
        4_000_000_000,
    )
    x2, h2, q2, kv2, o2 = grid_call(
        cross_fwd_kernel, "cross_fwd",
        [SMEM_SPEC, full((rows, width)), full((3, width)), weight(1, sq), full((mem_len, width))],
        [((rows, width), F32, full((rows, width))), ((rows, width), BF, full((rows, width))),
         ((4, rows, hw), BF, slot((rows, hw))), ((4, mem_len, 2 * hw), BF, slot((mem_len, 2 * hw))),
         ((4, rows, hw), BF, slot((rows, hw)))],
        [],
        (valid_rows, x1, norm_gains, weights, mem_full),
        3_000_000_000,
    )
    output, g2, grad_f, gain3 = grid_call(
        ffn_kernel, "ffn",
        [full((rows, width)), full((rows, width)), full((3, width)), weight(2, sq), weight(3, sq)],
        [((rows, width), BF, full((rows, width))), ((rows, width), F32, full((rows, width))),
         ((4, 2, width, width), BF, slot((2, width, width))), ((8, width), F32, full((8, width)))],
        [vm((rows, width), BF), vm((rows, width), F32), vm((rows, width), F32)],
        (x2, cotangent, norm_gains, weights, weights),
        8_000_000_000,
    )
    grad_c, g1, dmem, gain2 = grid_call(
        cross_bwd_kernel, "cross_bwd",
        [SMEM_SPEC, full((rows, width)), full((rows, width)), full((3, width)), weight(1, sq),
         full((mem_len, width)), full((rows, width)), slot((rows, hw)), slot((mem_len, 2 * hw)), slot((rows, hw))],
        [((4, width, width), BF, slot((width, width))), ((rows, width), F32, full((rows, width))),
         ((mem_len, width), BF, full((mem_len, width))), ((8, width), F32, full((8, width)))],
        [vm((rows, width), BF), vm((rows, width), F32), vm((mem_len, width), F32)],
        (valid_rows, g2, x1, norm_gains, weights, mem_full, h2, q2, kv2, o2),
        6_000_000_000,
    )
    grad_s, dh1, dx, rel = grid_call(
        self_bwd_kernel, "self_bwd",
        [full((rows, width)), full((3, width)), weight(0, sq), full((ext, width)),
         slot((rows, hw)), slot((ext, 2 * hw)), slot((rows, hw)), slot((heads, 256, 128)),
         slot((heads, 512)), full((1, rows)), full((ext, 1))],
        [((4, width, width), BF, slot((width, width))), ((rows, width), F32, full((rows, width))),
         ((2, rows, width), BF, full((2, rows, width))), ((4, heads, 512), F32, slot((heads, 512)))],
        [vm((2, span, 128), F32), vm((rows, width), BF), vm((256, 256), BF), vm((ext, width), F32)],
        (g1, norm_gains, weights, h1, q1, kv1, o1, bias, bias_line, seg_q, seg_k),
        8_000_000_000,
    )

    def by_owner(g):
        lead = g.shape[:-2]
        if groups > 1:
            g = g.reshape(lead + (groups, 8, eighth // groups, width))
            g = jnp.swapaxes(g, -4, -3)
        return g.reshape(lead + (4, 2, eighth, width))

    final, tokens_grad, memory_grad, gain1 = reduce_grads(
        by_owner(grad_f), by_owner(grad_c), by_owner(grad_s), dx, dmem.reshape(4, mem_own, width),
        dh1, tokens, g1, norm_gains,
    )
    if groups > 1:
        final = lax.psum_scatter(
            final, "wide", scatter_dimension=1, tiled=True,
            axis_index_groups=[[s + 8 * g for g in range(groups)] for s in range(8)],
        )
    own = final.shape[1]

    rel_pick = jnp.asarray(
        (buckets[np.maximum(lanes - 127, 0)][:, None] == np.arange(BUCKETS)[None, :]).astype(np.float32)
    )
    rel = lax.dynamic_slice_in_dim(jnp.concatenate([rel, rel], 0), 4 - z, 4, 0)
    rel = jnp.einsum("hl,lb->bh", rel.reshape(4 * heads, 512), rel_pick, precision=lax.Precision.HIGHEST)
    rel_row = jnp.pad(rel.reshape(1, -1), ((0, 0), (0, width - BUCKETS * 4 * heads)))
    small = jnp.concatenate([gain1[:1], gain2[:1], gain3[:1], rel_row, jnp.zeros((4, width), F32)], 0)
    rsum, csum, asum, prow, pcol = reduce_stats(wide_count, final, small)

    def split(g):
        return jnp.stack([g[:, 0:hw], g[:, 2 * hw : 3 * hw], g[:, 3 * hw :], g[:, hw : 2 * hw]])

    ffn_flat = jnp.concatenate([final[2], final[3]], axis=1)
    ffn_grad = jnp.stack([ffn_flat[:, 0:fw], ffn_flat[:, fw : 2 * fw], ffn_flat[:, 2 * fw :]])
    attn_row = jnp.concatenate([rsum[0:1], rsum[2:4], rsum[8:9], rsum[10:12]], 0)[:, :own] / width
    ffn_row = rsum[16:19, :own] / (4 * fw)
    attn_col = jnp.stack(
        [csum[i, a * hw : (a + 1) * hw] for i in range(2) for a in (0, 2, 3)]
    ) / width
    ffn_cols = jnp.concatenate([csum[2], csum[3]])
    ffn_col = ffn_cols.reshape(3, fw) / width
    proj_rows = prow[:, 4:6, :own].transpose(1, 0, 2).reshape(2, width) / width
    proj_cols = pcol[:, 0:2, hw : 2 * hw].transpose(1, 0, 2).reshape(2, width) / width
    return (
        output,
        tokens_grad,
        memory_grad.reshape(1, mem_own, width),
        asum[0:3],
        asum[3, : BUCKETS * 4 * heads].reshape(BUCKETS, 4 * heads),
        split(final[0]),
        split(final[1]),
        ffn_grad,
        attn_row,
        attn_col,
        jnp.concatenate([proj_rows, proj_cols], 1),
        ffn_row,
        ffn_col,
    )


def solution(mesh):
    in_specs = (
        P(("wide", "narrow"), None),
        P("wide", "narrow", None),
        P("wide", None),
        P("wide"),
        P(),
        P(),
        P(None, None, "narrow"),
        P(None, None, "narrow"),
        P(None, None, "narrow"),
        P(("wide", "narrow"), None),
    )
    out_specs = (
        P(("wide", "narrow"), None),
        P(("wide", "narrow"), None),
        P("wide", "narrow", None),
        P(),
        P(),
        P(None, "wide", "narrow"),
        P(None, "wide", "narrow"),
        P(None, "wide", "narrow"),
        P(None, "wide"),
        P(None, "narrow"),
        P(),
        P(None, "wide"),
        P(None, "narrow"),
    )
    return jax.shard_map(local, mesh=mesh, in_specs=in_specs, out_specs=out_specs, check_vma=False)
```

time: 1070 us -> 386 us (0.36)
  waiting for transfers between devices: 517 us -> 0 us
  Pallas kernels: 0 us -> 337 us
  other arithmetic: 219 us -> 13.1 us
  matrix products: 168 us -> 2.53 us
  blocking collectives: 85.5 us -> 0 us
  local copies, waits for them, and re-layouts: 52.6 us -> 30.7 us
  between operations: 17.6 us -> 1.52 us
    pallas_call x0 -> x8, Pallas kernels: none -> 337 us  [the longest x1 118 us: gather(): pl.pallas_call(gather_kernel, name='gather', in_specs=[any_spec] * 3, out...]
    reduce_scatter x7 -> x0, waiting for transfers between devices: 308 us -> none  [the longest x6 308 us: reduce_rows(): lax.psum_scatter(partial_sum, 'narrow', scatter_dimension=0, tiled=True)]
    dot_general x59 -> x2, matrix products: 168 us -> 2.53 us  [the longest x1 1.52 us: local(): jnp.einsum('hl,lb->bh', rel.reshape(4 * heads, 512), rel_pick, precision=...]
    all_gather x6 -> x0, waiting for transfers between devices: 136 us -> none  [gather_rows(): return lax.all_gather(row_values, 'narrow', axis=0, tiled=True)]
    eq x16 -> x0, other arithmetic: 126 us -> none  [self_geometry(): bucket_tile[None] == bucket_number]
    psum x1 -> x0, waiting for transfers between devices: 72.4 us -> none  [local(): summed = lax.psum((self_local, cross_local, ffn_local_grads), 'wide')]
    psum x2 -> x0, blocking collectives: 61.2 us -> none  [the longest x1 40.6 us: local(): lax.psum((jnp.stack([gain_one, gain_two, gain_three]), rel_full), ('wide'...]
    reduce_sum x14 -> x0, other arithmetic: 25.7 us -> none  [the longest x3 8.87 us: attend_block(): totals = jnp.sum(weights_exp, axis=-1, keepdims=True)]
  transfers between devices with their start and end apart: 14 -> 0, of which waited for: 12 -> 0; matrix products, arithmetic and copies ran while one was open for 28% -> 0% of each run, Pallas kernels for 0% -> 0%
where the time goes in v1:
time: 386 us; the launch traced here: 385 us
  Pallas kernels  337 us (87%)
  local copies, waits for them, and re-layouts  30.7 us (8%)
  other arithmetic  13.1 us (3%)
    pallas_call x1, Pallas kernels, gather(): pl.pallas_call(gather_kernel, name='gather', in_specs=[any_spec] * 3, out...  118 us
    pallas_call x1, Pallas kernels, reduce_grads(): pl.pallas_call(reduce_kernel, name='reduce', in_specs=[any_spec] * 3 + [v...  118 us
    pallas_call x5, Pallas kernels, grid_call(): pl.pallas_call(kernel, name=name, grid=(4,), in_specs=in_specs, out_specs...  89 us
    slice x10, local copies, waits for them, and re-layouts, qokv(): return jnp.concatenate([w[0], w[3], w[1], w[2]], axis=1)  15.4 us
    pallas_call x1, Pallas kernels, reduce_stats(): pl.pallas_call(functools.partial(stats_kernel, wide_count), name='stats',...  13 us

profile of v1, /device:TPU:0, one launch (start us, length us, event | category | flops | bytes accessed | tf_op | source)
XLA Modules:
  0.0 384.9 jit_solution(786132825106877398)
XLA Ops:
  1.3 1.2 constant_dynamic-slice_fusion.segq_ref
  3.3 1.0 convolution_bitcast_fusion
  5.0 0.9 reshape.111.segk_ref
  5.9 2.3 fusion.3
  8.5 1.1 copy.38
  9.6 1.9 copy.37
  11.5 2.2 fusion.4
  13.8 1.9 copy.39
  15.7 1.9 copy.40
  17.5 1.9 copy.42
  19.4 1.9 copy.41
  22.8 4.4 %pad_maximum_fusion.p_ref = bf16[4,16,48,768]{3,2,1,0:T(8,128)(2,1)} fusion(bf16[1,16,48,768]{3,2,1,0:T(8,128)(2,1)S(1)} %bitcast.74, bf16[1,16,48,768]{3,2,1,0:T(8,128)(2,1)S(1)} %bitcast.73, bf16[1,16,48,192]{3,2,1,0:T(8,128)(2,1)S(1)} %bitcast.85, bf16[1,16,48,192]{3,2,1,0:T(8,128)(2,1)S(1)} %bitcast.86, bf16[1,16,48,192]{3,2,1,0:T(8,128)(2,1)S(1)} %bitcast.84, ...), kind=kLoop, calls=%fused_computation | loop fusion | flops 47185920 | bytes 9437184 | tf_op jit(solution)/shard_map/stack | solution.py:991
  27.1 117.5 %gather.1 = (bf16[4,4,16,48,768]{4,3,2,1,0:T(8,128)(2,1)}, bf16[2,256,768]{2,1,0:T(8,128)(2,1)}, bf16[4,128,768]{2,1,0:T(8,128)(2,1)}) custom-call(bf16[4,16,48,768]{3,2,1,0:T(8,128)(2,1)} %pad_maximum_fusion.p_ref, bf16[256,768]{1,0:T(8,128)(2,1)} %tok_ref.5, bf16[128,768]{1,0:T(8,128)(2,1)} %bitcast.89), custom_call_target="tpu_custom_call" | custom-call | tf_op jit(solution)/shard_map/gather/pallas_call | solution.py:588
  144.7 16.4 %self_fwd.1 = (f32[256,768]{1,0:T(8,128)}, bf16[768,768]{1,0:T(8,128)(2,1)}, bf16[4,256,192]{2,1,0:T(8,128)(2,1)}, bf16[4,768,384]{2,1,0:T(8,128)(2,1)}, bf16[4,...) custom-call(s32[1]{0:T(128)} %bitcast.z_ref, bf16[2,256,768]{2,1,0:T(8,128)(2,1)} %get-tuple-element.48.xt_ref, ...), custom_call_target="tpu_custom_call" | custom-call | flops 4000000000 | bytes 11403264 | tf_op jit(solution)/shard_map/self_fwd/pallas_call | solution.py:351
  161.1 11.2 %cross_fwd.1 = (f32[256,768]{1,0:T(8,128)}, bf16[256,768]{1,0:T(8,128)(2,1)}, bf16[4,256,192]{2,1,0:T(8,128)(2,1)}, bf16[4,512,384]{2,1,0:T(8,128)(2,1)}, bf16[4,256,192]{2,1,0:T(8,128)(2,1)}) custom-call(s32[1]{0:T(128)S(6)} %copy.52.valid_ref, f32[256,768]{1,0:T(8,128)} %get-tuple-element.50.x1_ref, f32[3,768]{1,0:T(4,128)} %gain_ref.11, ...), custom_call_target="tpu_custom_call" | custom-call | flops 3000000000 | bytes 8257536 | tf_op jit(solution)/shard_map/cross_fwd/pallas_call | solution.py:351
  172.4 14.1 %ffn.1 = (bf16[256,768]{1,0:T(8,128)(2,1)}, f32[256,768]{1,0:T(8,128)}, bf16[4,2,768,768]{3,2,1,0:T(8,128)(2,1)}, f32[8,768]{1,0:T(8,128)}) custom-call(f32[256,768]{1,0:T(8,128)} %get-tuple-element.52.x2_ref, bf16[256,768]{1,0:T(8,128)(2,1)} %cot_ref.1, f32[3,768]{1,0:T(4,128)} %gain_ref.11, bf16[4,4,768,768]{3,2,1,0:T(8,128)(2,1)} %bitcast.68, ...), custom_call_target="tpu_custom_call" | custom-call | flops 8000000000 | bytes 15360000 | tf_op jit(solution)/shard_map/ffn/pallas_call | solution.py:351
  186.4 1.3 slice.164
  187.8 19.9 %cross_bwd.1 = (bf16[4,768,768]{2,1,0:T(8,128)(2,1)}, f32[256,768]{1,0:T(8,128)}, bf16[512,768]{1,0:T(8,128)(2,1)}, f32[8,768]{1,0:T(8,128)}) custom-call(s32[1]{0:T(128)S(6)} %copy.52.valid_ref, f32[256,768]{1,0:T(8,128)} %get-tuple-element.55.g2_ref, f32[256,768]{1,0:T(8,128)} %get-tuple-element.50.x1_ref, f32[3,768]{1,0:T(4,128)} %gain_ref.11, ...), custom_call_target="tpu_custom_call" | custom-call | flops 6000000000 | bytes 11034624 | tf_op jit(solution)/shard_map/cross_bwd/pallas_call | solution.py:351
  207.7 27.3 %self_bwd.1 = (bf16[4,768,768]{2,1,0:T(8,128)(2,1)}, f32[256,768]{1,0:T(8,128)}, bf16[2,256,768]{2,1,0:T(8,128)(2,1)}, f32[4,3,512]{2,1,0:T(4,128)}) custom-call(f32[256,768]{1,0:T(8,128)} %get-tuple-element.61.g1_ref, f32[3,768]{1,0:T(4,128)} %gain_ref.11, bf16[4,4,768,768]{3,2,1,0:T(8,128)(2,1)} %bitcast.71, bf16[768,768]{1,0:T(8,128)(2,1)} %get-tuple-element.62.h1_ref, ...), custom_call_target="tpu_custom_call" | custom-call | flops 8000000000 | bytes 11034624 | tf_op jit(solution)/shard_map/self_bwd/pallas_call | solution.py:351
  235.0 117.5 %reduce.7 = (f32[4,96,768]{2,1,0:T(8,128)}, f32[256,768]{1,0:T(8,128)}, f32[128,768]{1,0:T(8,128)}, f32[8,768]{1,0:T(8,128)}) custom-call(bf16[4,2,4,2,96,768]{5,4,3,2,1,0:T(8,128)(2,1)} %bitcast.72, bf16[4,4,2,96,768]{4,3,2,1,0:T(8,128)(2,1)} %bitcast.75, bf16[4,4,2,96,768]{4,3,2,1,0:T(8,128)(2,1)} %bitcast.76, ...), custom_call_target="tpu_custom_call" | custom-call | tf_op jit(solution)/shard_map/reduce/pallas_call | solution.py:790
  354.0 0.8 fusion.1
  354.8 1.5 fusion.8
  356.4 1.3 concatenate.71.a_ref
  357.8 13.0 %stats.1 = (f32[24,128]{1,0:T(8,128)}, f32[8,768]{1,0:T(8,128)}, f32[8,768]{1,0:T(8,128)}, f32[8,8,128]{2,1,0:T(8,128)}, f32[4,8,768]{2,1,0:T(8,128)}) custom-call(f32[4,96,768]{2,1,0:T(8,128)} %get-tuple-element.73.f_ref, f32[8,768]{1,0:T(8,128)} %concatenate.71.a_ref), custom_call_target="tpu_custom_call" | custom-call | tf_op jit(solution)/shard_map/stats/pallas_call | solution.py:946
  370.8 0.8 multiply_bitcast_fusion.1
  371.6 1.4 slice_bitcast_fusion.4
  373.1 0.9 pad_maximum_fusion.3
  375.3 1.3 slice_multiply_fusion.1
  379.2 0.9 multiply_bitcast_fusion
  381.7 0.8 pad_maximum_fusion.5
  382.5 0.8 pad_maximum_fusion.4
  383.3 0.9 copy.53
  (55 shorter events, 11.3 us)
Async XLA Ops:
  5.9 15.4 %copy-start = (bf16[3,768,512]{2,1,0:T(8,128)(2,1)S(1)}, bf16[3,768,512]{2,1,0:T(8,128)(2,1)}, u32[]{:S(2)}) copy-start(bf16[3,768,512]{2,1,0:T(8,128)(2,1)} %param.20) | copy-start | bytes 7077892
  21.3 1.0 copy-start.1
  21.3 1.1 copy-start.2
  21.3 1.2 copy-start.3
  21.3 1.3 copy-start.4
  21.3 1.5 copy-start.5
  357.8 25.5 %copy-start.6 = (f32[256,768]{1,0:T(8,128)S(1)}, f32[256,768]{1,0:T(8,128)}, u32[]{:S(2)}) copy-start(f32[256,768]{1,0:T(8,128)} %get-tuple-element.167) | copy-start | bytes 2359300
  370.8 3.9 %copy-start.8 = (f32[8,768]{1,0:T(8,128)S(1)}, f32[8,768]{1,0:T(8,128)}, u32[]{:S(2)}) copy-start(f32[8,768]{1,0:T(8,128)} %get-tuple-element.78) | copy-start | bytes 73732
  370.8 7.0 %copy-start.9 = (f32[8,768]{1,0:T(8,128)S(1)}, f32[8,768]{1,0:T(8,128)}, u32[]{:S(2)}) copy-start(f32[8,768]{1,0:T(8,128)} %get-tuple-element.80) | copy-start | bytes 73732
  371.6 12.5 %copy-start.7 = (f32[128,768]{1,0:T(8,128)S(1)}, f32[128,768]{1,0:T(8,128)}, u32[]{:S(2)}) copy-start(f32[128,768]{1,0:T(8,128)} %get-tuple-element.72) | copy-start | bytes 1179652

commit v2 on v1

--- a/solution.py
+++ b/solution.py
@@ -72,55 +72,6 @@
             segk_ref[b * 128 : b * 128 + span, :] == segq_ref[:, b * 128 : b * 128 + 128]
         )
         mask_ref[b] = jnp.where(allowed, 1.0, 0.0)
-
-
-def self_fwd_kernel(
-    z_ref, xt_ref, tok_ref, gain_ref, w_ref, bd_ref, segq_ref, segk_ref,
-    x1_ref, h1_ref, q_ref, kv_ref, o_ref, bias_ref,
-    mask_ref,
-):
-    rows = tok_ref.shape[0]
-    ext = 3 * rows
-    span = 2 * rows + 128
-    hw = q_ref.shape[2]
-    heads = hw // 64
-    j = pl.program_id(0)
-
-    @pl.when(j == 0)
-    def _():
-        g = gain_ref[0:1, :]
-        for t in range(2):
-            v = jnp.where(z_ref[0] >= 2 - t, xt_ref[t].astype(F32), 0.0)
-            h1_ref[t * rows : (t + 1) * rows, :] = (v * inv_rms(v) * g).astype(BF)
-        x = tok_ref[...].astype(F32)
-        x1_ref[...] = x
-        h1_ref[2 * rows : ext, :] = (x * inv_rms(x) * g).astype(BF)
-        self_mask_store(mask_ref, segk_ref, segq_ref, rows, span)
-
-    q = mm(h1_ref[2 * rows : ext, :], w_ref[:, 0:hw]).astype(BF)
-    kv = mm(h1_ref[...], w_ref[:, 2 * hw : 4 * hw]).astype(BF)
-    q_ref[0] = q
-    kv_ref[0] = kv
-    parts = []
-    for hh in range(heads):
-        line = jnp.broadcast_to(bd_ref[0, hh : hh + 1, :], (256, 512))
-        bias = pltpu.roll(line, 0, 1, stride=1, stride_axis=0)[:, 0:128]
-        bias_ref[0, hh] = bias
-        far = bd_ref[0, hh : hh + 1, 127:128]
-        cols = []
-        for b in range(2):
-            k = kv[b * 128 : b * 128 + span, hh * 64 : hh * 64 + 64]
-            v = kv[b * 128 : b * 128 + span, hw + hh * 64 : hw + hh * 64 + 64]
-            qb = q[b * 128 : b * 128 + 128, hh * 64 : hh * 64 + 64]
-            s = mm_nt(k, qb)
-            s = jnp.concatenate([s[: span - 256] + far, s[span - 256 :] + bias], axis=0)
-            s = jnp.where(mask_ref[b] > 0.5, s, MASKED)
-            p = soft_cols(s).astype(BF)
-            cols.append(mm_tn(v, p))
-        parts.append(jnp.concatenate(cols, axis=1))
-    o = jnp.concatenate(parts, axis=0).T.astype(BF)
-    o_ref[0] = o
-    x1_ref[...] += mm_nt(o, w_ref[:, hw : 2 * hw])
 
 
 def self_bwd_kernel(
@@ -199,35 +150,6 @@
             dx_ref[t] = acc_ref[t * rows : (t + 1) * rows, :].astype(BF)
 
 
-def cross_fwd_kernel(valid_ref, x1_ref, gain_ref, w_ref, mem_ref, x2_ref, h2_ref, q_ref, kv_ref, o_ref):
-    rows = x1_ref.shape[0]
-    mem = mem_ref.shape[0]
-    hw = q_ref.shape[2]
-    heads = hw // 64
-    j = pl.program_id(0)
-
-    @pl.when(j == 0)
-    def _():
-        x1 = x1_ref[...]
-        x2_ref[...] = x1
-        h2_ref[...] = (x1 * inv_rms(x1) * gain_ref[1:2, :]).astype(BF)
-
-    q = mm(h2_ref[...], w_ref[:, 0:hw]).astype(BF)
-    kv = mm(mem_ref[...], w_ref[:, 2 * hw : 4 * hw]).astype(BF)
-    q_ref[0] = q
-    kv_ref[0] = kv
-    allowed = lax.broadcasted_iota(jnp.int32, (mem, rows), 0) < valid_ref[0]
-    parts = []
-    for hh in range(heads):
-        k = kv[:, hh * 64 : hh * 64 + 64]
-        v = kv[:, hw + hh * 64 : hw + hh * 64 + 64]
-        s = jnp.where(allowed, mm_nt(k, q[:, hh * 64 : hh * 64 + 64]), MASKED)
-        parts.append(mm_tn(v, soft_cols(s).astype(BF)))
-    o = jnp.concatenate(parts, axis=0).T.astype(BF)
-    o_ref[0] = o
-    x2_ref[...] += mm_nt(o, w_ref[:, hw : 2 * hw])
-
-
 def cross_bwd_kernel(
     valid_ref, g2_ref, x1_ref, gain_ref, w_ref, mem_ref, h2_ref, q_ref, kv_ref, o_ref,
     grad_ref, g1_ref, dmem_ref, gsum_ref,
@@ -396,216 +318,351 @@
     )
 
 
-def gather_kernel(
-    p_ref, tok_ref, mem_ref,
-    w_ref, xt_ref, mt_ref,
-    stage, mstage, zs, zr, ps, pr, ts, tr, ms, mr, ls, lm,
+RANKS = ((0, 1, 2, 3), (1, 0, 2, 3), (2, 3, 1, 0), (3, 2, 1, 0))
+
+
+def forward_kernel(
+    valid_ref, tok_ref, mem_ref, gain_ref, bd_ref, segq_ref, segk_ref, ws_ref, wc_ref, wf_ref,
+    w_ref, x1_ref, h1_ref, q_ref, kv_ref, o_ref, bias_ref, mfull_ref, x2_ref, h2_ref, q2_ref, kv2_ref, o2_ref,
+    wv, raw, xt, mt, mask_ref, zs, zr, ps, pr, ts, tr, ms, mr, ls, fs, os_,
 ):
     at = Place()
     z, s = at.z, at.s
-    chunks = p_ref.shape[0]
-    at.barrier()
-
-    def own(c):
-        return p_ref.at[c, pl.ds(2 * s, 2)]
-
-    def up0(c):
-        return remote(own(c), w_ref.at[c, 3, pl.ds(2 * s, 2)], zs.at[c, 0], zr.at[c, 3], {"narrow": z + 1})
-
-    def down0(c):
-        return remote(own(c), w_ref.at[c, 1, pl.ds(2 * s, 2)], zs.at[c, 1], zr.at[c, 1], {"narrow": z - 1})
-
-    def tok1():
-        return remote(tok_ref, xt_ref.at[1], ts.at[0], tr.at[1], {"narrow": z + 1})
-
-    def tok2():
-        return remote(tok_ref, xt_ref.at[0], ts.at[1], tr.at[0], {"narrow": z + 2})
-
-    def memk(k):
-        return remote(mem_ref, mt_ref.at[z], ms.at[k - 1], mr.at[k - 1], at.narrow_dev(k))
-
-    def start_z(c):
-        @pl.when(z < 3)
+    j = pl.program_id(0)
+    units = 4
+    rows, width = tok_ref.shape
+    ext = 3 * rows
+    span = 2 * rows + 128
+    hw = q_ref.shape[2]
+    fw = wf_ref.shape[3]
+    heads = hw // 64
+    part = rows // 4
+    mine = pl.ds(2 * s, 2)
+
+    def edge(k):
+        return [(d, RANKS[k + d].index(k)) for d in (1, -1) if 0 <= k + d < 4]
+
+    def own_send(u, k, d, rank):
+        return remote(
+            wv.at[u, 0, mine], wv.at[u, rank, mine], zs.at[u, 0 if d > 0 else 1], zr.at[u, rank], {"narrow": k + d}
+        )
+
+    def own_sends(u, act):
+        for k in range(4):
+            @pl.when(z == k)
+            def _():
+                for d, rank in edge(k):
+                    act(own_send(u, k, d, rank))
+
+    def forwards(u, r, act):
+        for k in (1, 2):
+            quarter = RANKS[k][r]
+            d = 1 if quarter < k else -1
+            there = RANKS[k + d].index(quarter)
+
+            @pl.when(z == k)
+            def _():
+                act(remote(wv.at[u, r, mine], wv.at[u, there, mine], zs.at[u, 1 + r], zr.at[u, there], {"narrow": k + d}))
+
+    def tok_copy(hop, p):
+        part_rows = pl.ds(p * part, part)
+        return remote(
+            tok_ref.at[part_rows], xt.at[2 - hop, part_rows], ts.at[hop - 1, p], tr.at[hop - 1, p], {"narrow": z + hop}
+        )
+
+    def tok_send(hop, parts):
+        @pl.when(z < 4 - hop)
         def _():
-            up0(c).start()
-
-        @pl.when(z > 0)
-        def _():
-            down0(c).start()
-
-    start_z(0)
-
-    @pl.when(z < 3)
-    def _():
-        tok1().start()
-
-    @pl.when(z < 2)
-    def _():
-        tok2().start()
-
-    for c in range(1, chunks):
-        start_z(c)
-    for k in (1, 2, 3):
-        memk(k).start()
-
-    mem_in = pltpu.make_async_copy(mem_ref, mstage, lm.at[0])
-    mem_in.start()
-    loads = [pltpu.make_async_copy(p_ref.at[c], stage.at[c], ls.at[c]) for c in range(chunks)]
-    for copy in loads:
-        copy.start()
-    mem_in.wait()
-    mem_out = pltpu.make_async_copy(mstage, mt_ref.at[z], lm.at[1])
-    mem_out.start()
-    stores = [pltpu.make_async_copy(stage.at[c], w_ref.at[c, 0], ls.at[chunks + c]) for c in range(chunks)]
-    for load, store in zip(loads, stores):
-        load.wait()
-        store.start()
-
-    e0 = 1 - (z + 3) // 4
-    e3 = z // 3
-    e1 = (1 - z // 2) * lax.rem(z, 2)
-    e2 = (z // 2) * (1 - lax.rem(z, 2))
-    order = [e0 * 1 + e1 * 3 + e2 * 1 + e3 * 3, e0 * 2 + e1 * 1 + e2 * 3 + e3 * 2, e0 * 3 + e1 * 2 + e2 * 2 + e3 * 1]
-    onward = {1: [(3, 2, 1), (1, 2, -1), (2, 3, -1)], 2: [(1, 2, -1), (3, 2, 1), (2, 1, 1)]}
-
-    def forward(c, r, k):
-        here, there, step = onward[k][r]
-        return remote(
-            w_ref.at[c, here, pl.ds(2 * s, 2)], w_ref.at[c, there, pl.ds(2 * s, 2)],
-            zs.at[c, 2 + r], zr.at[c, there], {"narrow": k + step},
-        )
-
-    def piece(c, r, kind):
-        sl = order[r]
-        i = c * 3 + r
-        table = {
+            for p in parts:
+                tok_copy(hop, p).start()
+
+    def mem_copy(k):
+        return remote(mem_ref, mt.at[z], ms.at[k - 1], mr.at[k - 1], at.narrow_dev(k))
+
+    def piece(u, r, kind):
+        first, n, dev = {
             0: (2 * s, 1, at.x_dev), 1: (2 * s + 1, 1, at.x_dev), 2: (2 * at.sy + 1, 1, at.x_dev),
             3: (2 * s + 1, 1, at.y_dev), 4: (2 * s, 1, at.y_dev), 5: (2 * at.sx, 1, at.y_dev),
             6: (2 * s, 2, at.core_dev), 7: (2 * at.sx, 2, at.core_dev),
             8: (2 * at.sy, 2, at.core_dev), 9: (2 * at.sxy, 2, at.core_dev),
-        }
-        first, n, dev = table[kind]
-        region = w_ref.at[c, sl, pl.ds(first, n)]
+        }[kind]
+        region = wv.at[u, r, pl.ds(first, n)]
+        i = u * 3 + r - 1
         return remote(region, region, ps.at[i, kind], pr.at[i, kind], dev)
 
-    def arrived(c, r, kind):
-        sl = order[r]
-        i = c * 3 + r
-        table = {
+    def arrived(u, r, kind):
+        first, n = {
             0: (2 * at.sx, 1), 1: (2 * at.sx + 1, 1), 2: (2 * at.sxy + 1, 1),
             3: (2 * at.sy + 1, 1), 4: (2 * at.sy, 1), 5: (2 * at.sxy, 1),
             6: (2 * (s + at.dc), 2), 7: (2 * (at.sx + at.dc), 2),
             8: (2 * (at.sy + at.dc), 2), 9: (2 * (at.sxy + at.dc), 2),
-        }
-        first, n = table[kind]
-        region = w_ref.at[c, sl, pl.ds(first, n)]
+        }[kind]
+        region = wv.at[u, r, pl.ds(first, n)]
+        i = u * 3 + r - 1
         remote(region, region, ps.at[i, kind], pr.at[i, kind], at.x_dev).wait_recv()
 
-    def step0(c, r):
-        sl = order[r]
-        region = w_ref.at[c, sl, pl.ds(2 * s, 2)]
-        remote(region, region, zs.at[c, 0], zr.at[c, sl], at.x_dev).wait_recv()
-        for k in (1, 2):
-            @pl.when(z == k)
+    pieces = [(u, r) for u in range(units) for r in (1, 2, 3)]
+
+    def step0(t):
+        if not 0 <= t < len(pieces):
+            return
+        u, r = pieces[t]
+        region = wv.at[u, r, mine]
+        remote(region, region, zs.at[u, 0], zr.at[u, r], at.x_dev).wait_recv()
+        forwards(u, r, lambda copy: copy.start())
+        for kind in (0, 3, 4, 1, 6):
+            piece(u, r, kind).start()
+        if t == 0:
+            tok_send(1, (2, 3))
+        if t == 1:
+            tok_send(2, (0, 1))
+        if t == 2:
+            tok_send(2, (2, 3))
+            own_sends(2, lambda copy: copy.start())
+        if t in (3, 4, 5):
+            mem_copy(t - 2).start()
+        if t == 5:
+            own_sends(3, lambda copy: copy.start())
+
+    def step1(t):
+        if not 0 <= t < len(pieces):
+            return
+        u, r = pieces[t]
+        arrived(u, r, 0)
+        piece(u, r, 5).start()
+        arrived(u, r, 3)
+        piece(u, r, 2).start()
+        arrived(u, r, 1)
+        piece(u, r, 7).start()
+        arrived(u, r, 4)
+        piece(u, r, 8).start()
+
+    def step2(t):
+        if not 0 <= t < len(pieces):
+            return
+        u, r = pieces[t]
+        arrived(u, r, 5)
+        arrived(u, r, 2)
+        piece(u, r, 9).start()
+
+    def keep(u, k):
+        return pltpu.make_async_copy(wv.at[u, k], w_ref.at[u, k], os_.at[u, k])
+
+    def step3(t):
+        if not 0 <= t < len(pieces):
+            return
+        u, r = pieces[t]
+        for kind in (6, 7, 8, 9):
+            arrived(u, r, kind)
+        keep(u, r).start()
+
+    def load_raw(i):
+        src = (ws_ref, wc_ref)[i]
+        return pltpu.make_async_copy(src, raw.at[i], ls.at[i])
+
+    def ffn_loads():
+        cut = width - fw
+        return [
+            pltpu.make_async_copy(wf_ref.at[0], wv.at[2, 0, :, :, 0:fw], fs.at[0]),
+            pltpu.make_async_copy(wf_ref.at[1, :, :, 0:cut], wv.at[2, 0, :, :, fw:width], fs.at[1]),
+            pltpu.make_async_copy(wf_ref.at[1, :, :, cut:fw], wv.at[3, 0, :, :, 0 : fw - cut], fs.at[2]),
+            pltpu.make_async_copy(wf_ref.at[2], wv.at[3, 0, :, :, fw - cut : width], fs.at[3]),
+        ]
+
+    def pack(i):
+        load_raw(i).wait()
+        for b in range(16):
+            wv[i, 0, b] = jnp.concatenate([raw[i, 0, b], raw[i, 3, b], raw[i, 1, b], raw[i, 2, b]], axis=1)
+
+    @pl.when(j == 0)
+    def _():
+        load_raw(0).start()
+        load_raw(1).start()
+        for copy in ffn_loads():
+            copy.start()
+        at.barrier()
+        pack(0)
+        own_sends(0, lambda copy: copy.start())
+        tok_send(1, (0, 1))
+        pack(1)
+        own_sends(1, lambda copy: copy.start())
+        for copy in ffn_loads():
+            copy.wait()
+        for u in range(units):
+            keep(u, 0).start()
+        x = tok_ref[...].astype(F32)
+        x1_ref[...] = x
+        h1_ref[2 * rows : ext, :] = (x * inv_rms(x) * gain_ref[0:1, :]).astype(BF)
+        self_mask_store(mask_ref, segk_ref, segq_ref, rows, span)
+        step0(0)
+        step0(1)
+        step1(0)
+        step0(2)
+        step1(1)
+        step2(0)
+        step3(0)
+        step0(3)
+        step1(2)
+        step2(1)
+        for hop in (1, 2):
+            @pl.when(z >= hop)
             def _():
-                forward(c, r, k).start()
-        for kind in (0, 3, 4, 1, 6):
-            piece(c, r, kind).start()
-
-    def step1(c, r):
-        arrived(c, r, 0)
-        piece(c, r, 5).start()
-        arrived(c, r, 3)
-        piece(c, r, 2).start()
-        arrived(c, r, 1)
-        piece(c, r, 7).start()
-        arrived(c, r, 4)
-        piece(c, r, 8).start()
-
-    def step2(c, r):
-        arrived(c, r, 5)
-        arrived(c, r, 2)
-        piece(c, r, 9).start()
-
-    pieces = [(c, r) for c in range(chunks) for r in range(3)]
-    for t in range(len(pieces) + 2):
-        if t < len(pieces):
-            step0(*pieces[t])
-        if 0 <= t - 1 < len(pieces):
-            step1(*pieces[t - 1])
-        if 0 <= t - 2 < len(pieces):
-            step2(*pieces[t - 2])
-
-    for c, r in pieces:
-        for kind in (6, 7, 8, 9):
-            arrived(c, r, kind)
-        for kind in range(10):
-            piece(c, r, kind).wait_send()
-        for k in (1, 2):
-            @pl.when(z == k)
+                for p in range(4):
+                    tok_copy(hop, p).wait_recv()
+        for t in range(2):
+            v = jnp.where(z >= 2 - t, xt[t].astype(F32), 0.0)
+            h1_ref[t * rows : (t + 1) * rows, :] = (v * inv_rms(v) * gain_ref[0:1, :]).astype(BF)
+
+    def hook(i, first, last):
+        for jj in range(first, last):
+            t = 4 + jj
+
+            @pl.when(j == jj)
             def _():
-                forward(c, r, k).wait_send()
-    for c in range(chunks):
-        stores[c].wait()
-
-        @pl.when(z < 3)
-        def _():
-            up0(c).wait_send()
-
-        @pl.when(z > 0)
-        def _():
-            down0(c).wait_send()
-
-    mem_out.wait()
-    for k in (1, 2, 3):
-        memk(k).wait_send()
-        here = mt_ref.at[lax.rem(z + 4 - k, 4)]
-        remote(here, here, ms.at[k - 1], mr.at[k - 1], at.x_dev).wait_recv()
-
-    @pl.when(z < 3)
+                if i == 0:
+                    step3(t - 3)
+                    step0(t)
+                if i == 1:
+                    step1(t - 1)
+                if i == 2:
+                    step2(t - 2)
+
+    def flat(u, k, lo, hi):
+        return wv[u, k, :, :, lo:hi].reshape(width, hi - lo)
+
+    @pl.when(j < 4)
     def _():
-        tok1().wait_send()
-
-    @pl.when(z < 2)
+        hook(0, 0, 4)
+        q = mm(h1_ref[2 * rows : ext, :], flat(0, j, 0, hw)).astype(BF)
+        kv = mm(h1_ref[...], flat(0, j, 2 * hw, 4 * hw)).astype(BF)
+        q_ref[0] = q
+        kv_ref[0] = kv
+        parts = []
+        for hh in range(heads):
+            line = jnp.broadcast_to(bd_ref[j, hh : hh + 1, :], (256, 512))
+            bias = pltpu.roll(line, 0, 1, stride=1, stride_axis=0)[:, 0:128]
+            bias_ref[0, hh] = bias
+            far = bd_ref[j, hh : hh + 1, 127:128]
+            cols = []
+            for b in range(2):
+                k = kv[b * 128 : b * 128 + span, hh * 64 : hh * 64 + 64]
+                v = kv[b * 128 : b * 128 + span, hw + hh * 64 : hw + hh * 64 + 64]
+                qb = q[b * 128 : b * 128 + 128, hh * 64 : hh * 64 + 64]
+                sc = mm_nt(k, qb)
+                sc = jnp.concatenate([sc[: span - 256] + far, sc[span - 256 :] + bias], axis=0)
+                sc = jnp.where(mask_ref[b] > 0.5, sc, MASKED)
+                cols.append(mm_tn(v, soft_cols(sc).astype(BF)))
+            parts.append(jnp.concatenate(cols, axis=1))
+            if hh < 2:
+                hook(1 + hh, 0, 4)
+        o = jnp.concatenate(parts, axis=0).T.astype(BF)
+        o_ref[0] = o
+        x1_ref[...] += mm_nt(o, flat(0, j, hw, 2 * hw))
+
+    @pl.when(j == 4)
     def _():
-        tok2().wait_send()
-
-    @pl.when(z > 0)
+        x1 = x1_ref[...]
+        x2_ref[...] = x1
+        h2_ref[...] = (x1 * inv_rms(x1) * gain_ref[1:2, :]).astype(BF)
+        mfull_ref[z] = mem_ref[...]
+        for k in (1, 2, 3):
+            frm = lax.rem(z + 4 - k, 4)
+            remote(mt.at[frm], mt.at[frm], ms.at[k - 1], mr.at[k - 1], at.x_dev).wait_recv()
+            mfull_ref[frm] = mt[frm]
+
+    @pl.when(j >= 4)
     def _():
-        tok1().wait_recv()
-
-    @pl.when(z > 1)
+        hook(0, 4, 8)
+        mem = mfull_ref.shape[0] * mfull_ref.shape[1]
+        q = mm(h2_ref[...], flat(1, j - 4, 0, hw)).astype(BF)
+        kv = mm(mfull_ref[...].reshape(mem, width), flat(1, j - 4, 2 * hw, 4 * hw)).astype(BF)
+        q2_ref[0] = q
+        kv2_ref[0] = kv
+        allowed = lax.broadcasted_iota(jnp.int32, (mem, rows), 0) < valid_ref[0]
+        parts = []
+        for hh in range(heads):
+            k = kv[:, hh * 64 : hh * 64 + 64]
+            v = kv[:, hw + hh * 64 : hw + hh * 64 + 64]
+            sc = jnp.where(allowed, mm_nt(k, q[:, hh * 64 : hh * 64 + 64]), MASKED)
+            parts.append(mm_tn(v, soft_cols(sc).astype(BF)))
+            if hh < 2:
+                hook(1 + hh, 4, 8)
+        o = jnp.concatenate(parts, axis=0).T.astype(BF)
+        o2_ref[0] = o
+        x2_ref[...] += mm_nt(o, flat(1, j - 4, hw, 2 * hw))
+
+    @pl.when(j == 7)
     def _():
-        tok2().wait_recv()
-
-
-def gather(packed, tokens, memory):
+        for t in range(12, len(pieces) + 3):
+            step0(t)
+            step1(t - 1)
+            step2(t - 2)
+            step3(t - 3)
+        for u, r in pieces:
+            for kind in range(10):
+                piece(u, r, kind).wait_send()
+            forwards(u, r, lambda copy: copy.wait_send())
+        for u in range(units):
+            own_sends(u, lambda copy: copy.wait_send())
+            for k in range(4):
+                keep(u, k).wait()
+        for hop in (1, 2):
+            @pl.when(z < 4 - hop)
+            def _():
+                for p in range(4):
+                    tok_copy(hop, p).wait_send()
+        for k in (1, 2, 3):
+            mem_copy(k).wait_send()
+
+
+def forward(valid_rows, tokens, memory, gains, bias_line, seg_q, seg_k, ws, wc, wf):
     rows, width = tokens.shape
-    chunks = packed.shape[0]
-    half = packed.shape[2]
+    mem_own = memory.shape[0]
+    hw = ws.shape[3]
+    heads = hw // 64
+    ext = 3 * rows
+    mem = 4 * mem_own
+    half = width // 16
     any_spec = pl.BlockSpec(memory_space=pl.ANY)
     dma = pltpu.SemaphoreType.DMA
+
+    def early(shape):
+        return pl.BlockSpec((1,) + shape, lambda j: (jnp.minimum(j, 3),) + (0,) * len(shape))
+
+    def late(shape):
+        return pl.BlockSpec((1,) + shape, lambda j: (jnp.maximum(j - 4, 0),) + (0,) * len(shape))
+
+    out = [
+        ((4, 4, 16, half, width), BF, any_spec),
+        ((rows, width), F32, full((rows, width))), ((ext, width), BF, full((ext, width))),
+        ((4, rows, hw), BF, early((rows, hw))), ((4, ext, 2 * hw), BF, early((ext, 2 * hw))),
+        ((4, rows, hw), BF, early((rows, hw))), ((4, heads, 256, 128), F32, early((heads, 256, 128))),
+        ((4, mem_own, width), BF, full((4, mem_own, width))),
+        ((rows, width), F32, full((rows, width))), ((rows, width), BF, full((rows, width))),
+        ((4, rows, hw), BF, late((rows, hw))), ((4, mem, 2 * hw), BF, late((mem, 2 * hw))),
+        ((4, rows, hw), BF, late((rows, hw))),
+    ]
     return pl.pallas_call(
-        gather_kernel,
-        name="gather",
-        in_specs=[any_spec] * 3,
-        out_specs=[any_spec] * 3,
-        out_shape=[
-            jax.ShapeDtypeStruct((chunks, 4) + packed.shape[1:], BF),
-            jax.ShapeDtypeStruct((2, rows, width), BF),
-            jax.ShapeDtypeStruct((4,) + memory.shape, BF),
+        forward_kernel,
+        name="forward",
+        grid=(8,),
+        in_specs=[
+            SMEM_SPEC, full((rows, width)), full((mem_own, width)), full((3, width)), full((4, heads, 512)),
+            full((1, rows)), full((ext, 1)), any_spec, any_spec, any_spec,
         ],
+        out_specs=[spec for _, _, spec in out],
+        out_shape=[jax.ShapeDtypeStruct(shape, dtype) for shape, dtype, _ in out],
         scratch_shapes=[
-            pltpu.VMEM((chunks, 16, half, width), BF),
-            pltpu.VMEM(memory.shape, BF),
-            dma((chunks, 5)), dma((chunks, 4)),
-            dma((chunks * 3, 10)), dma((chunks * 3, 10)),
-            dma((2,)), dma((2,)), dma((3,)), dma((3,)), dma((2 * chunks,)), dma((2,)),
+            pltpu.VMEM((4, 4, 16, half, width), BF), pltpu.VMEM((2,) + ws.shape, BF),
+            pltpu.VMEM((2, rows, width), BF), pltpu.VMEM((4, mem_own, width), BF),
+            pltpu.VMEM((2, 2 * rows + 128, 128), F32),
+            dma((4, 5)), dma((4, 4)), dma((12, 10)), dma((12, 10)),
+            dma((2, 4)), dma((2, 4)), dma((3,)), dma((3,)), dma((2,)), dma((4,)), dma((4, 4)),
         ],
         compiler_params=pltpu.CompilerParams(
-            collective_id=0, has_side_effects=True, vmem_limit_bytes=VMEM_LIMIT
+            collective_id=0, has_side_effects=True, vmem_limit_bytes=VMEM_LIMIT, dimension_semantics=("arbitrary",)
         ),
-    )(packed, tokens, memory)
+    )(valid_rows, tokens, memory, gains, bias_line, seg_q, seg_k, ws, wc, wf)
 
 
 QUARTERS = (3, 0, 2, 1)
@@ -634,14 +691,22 @@
     def dm_send(k):
         return remote(dm_ref.at[lax.rem(z + k, 4)], dmr.at[k - 1], dms.at[k - 1], dmrs.at[k - 1], at.narrow_dev(k))
 
+    e0 = 1 - (z + 3) // 4
+    e3 = z // 3
+    e1 = (1 - z // 2) * lax.rem(z, 2)
+    e2 = (z // 2) * (1 - lax.rem(z, 2))
+
+    def rank(q):
+        return sum(e * row.index(q) for e, row in zip((e0, e1, e2, e3), RANKS))
+
     def core_send(i):
         _, get, q = chunks[i]
-        src = get(lax.rem(q + 4 - z, 4)).at[:, pl.ds(1 - at.c, 1)]
+        src = get(rank(q)).at[:, pl.ds(1 - at.c, 1)]
         return remote(src, rc.at[i], cs.at[i], cr.at[i], at.core_dev)
 
     def load(i):
         _, get, q = chunks[i]
-        src = get(lax.rem(q + 4 - z, 4)).at[:, pl.ds(at.c, 1)]
+        src = get(rank(q)).at[:, pl.ds(at.c, 1)]
         return pltpu.make_async_copy(src, own.at[i], lsem.at[i])
 
     for i in range(n):
@@ -984,51 +1049,29 @@
     groups = wide_count // 8
     eighth = width // 8
 
-    def qokv(w):
-        return jnp.concatenate([w[0], w[3], w[1], w[2]], axis=1)
-
-    ffn_packed = jnp.concatenate([ffn_weights[0], ffn_weights[1], ffn_weights[2]], axis=1)
-    packed = jnp.stack([qokv(self_weights), qokv(cross_weights), ffn_packed[:, :width], ffn_packed[:, width:]])
-    weights, earlier, mem_all = gather(packed.reshape(4, 16, width // 16, width), tokens, memory[0])
-    weights = weights.reshape(4, 4, width, width)
-    mem_full = mem_all.reshape(mem_len, width)
-
     buckets = bucket_table(1024, BUCKETS, MAX_DIST)
     lanes = np.arange(512)
     at_lane = np.where(lanes < 128, 128 + lanes, np.maximum(lanes - 384, 0))
     pick = jnp.asarray((buckets[at_lane][None, :] == np.arange(BUCKETS)[:, None]).astype(np.float32))
     bias_line = jnp.einsum("bl,bh->hl", pick, rel_table, precision=lax.Precision.HIGHEST)
     bias_line = bias_line.reshape(4, heads, 512)
-    bias_line = lax.dynamic_slice_in_dim(jnp.concatenate([bias_line, bias_line], 0), z, 4, 0)
+    ranks = jnp.asarray(RANKS, jnp.int32)
+    bias_line = jnp.take(bias_line, ranks[z], axis=0)
     seg = segments[0]
     seg_q = lax.dynamic_slice_in_dim(seg, z * rows, rows, 0).reshape(1, rows)
     seg_pad = jnp.concatenate([jnp.full((2 * rows,), -1, jnp.int32), seg])
     seg_k = lax.dynamic_slice_in_dim(seg_pad, z * rows, ext, 0).reshape(ext, 1)
-    z_arr = z.reshape(1)
 
     sq = (width, width)
     vm = pltpu.VMEM
-    x1, h1, q1, kv1, o1, bias = grid_call(
-        self_fwd_kernel, "self_fwd",
-        [SMEM_SPEC, full((2, rows, width)), full((rows, width)), full((3, width)), weight(0, sq),
-         slot((heads, 512)), full((1, rows)), full((ext, 1))],
-        [((rows, width), F32, full((rows, width))), ((ext, width), BF, full((ext, width))),
-         ((4, rows, hw), BF, slot((rows, hw))), ((4, ext, 2 * hw), BF, slot((ext, 2 * hw))),
-         ((4, rows, hw), BF, slot((rows, hw))), ((4, heads, 256, 128), F32, slot((heads, 256, 128)))],
-        [vm((2, span, 128), F32)],
-        (z_arr, earlier, tokens, norm_gains, weights, bias_line, seg_q, seg_k),
-        4_000_000_000,
-    )
-    x2, h2, q2, kv2, o2 = grid_call(
-        cross_fwd_kernel, "cross_fwd",
-        [SMEM_SPEC, full((rows, width)), full((3, width)), weight(1, sq), full((mem_len, width))],
-        [((rows, width), F32, full((rows, width))), ((rows, width), BF, full((rows, width))),
-         ((4, rows, hw), BF, slot((rows, hw))), ((4, mem_len, 2 * hw), BF, slot((mem_len, 2 * hw))),
-         ((4, rows, hw), BF, slot((rows, hw)))],
-        [],
-        (valid_rows, x1, norm_gains, weights, mem_full),
-        3_000_000_000,
-    )
+    half = width // 16
+    weights, x1, h1, q1, kv1, o1, bias, mem_full, x2, h2, q2, kv2, o2 = forward(
+        valid_rows, tokens, memory[0], norm_gains, bias_line, seg_q, seg_k,
+        self_weights.reshape(4, 16, half, hw), cross_weights.reshape(4, 16, half, hw),
+        ffn_weights.reshape(3, 16, half, fw),
+    )
+    weights = weights.reshape(4, 4, width, width)
+    mem_full = mem_full.reshape(mem_len, width)
     output, g2, grad_f, gain3 = grid_call(
         ffn_kernel, "ffn",
         [full((rows, width)), full((rows, width)), full((3, width)), weight(2, sq), weight(3, sq)],
@@ -1081,7 +1124,8 @@
     rel_pick = jnp.asarray(
         (buckets[np.maximum(lanes - 127, 0)][:, None] == np.arange(BUCKETS)[None, :]).astype(np.float32)
     )
-    rel = lax.dynamic_slice_in_dim(jnp.concatenate([rel, rel], 0), 4 - z, 4, 0)
+    places = jnp.asarray([[row.index(q) for q in range(4)] for row in RANKS], jnp.int32)
+    rel = jnp.take(rel, places[z], axis=0)
     rel = jnp.einsum("hl,lb->bh", rel.reshape(4 * heads, 512), rel_pick, precision=lax.Precision.HIGHEST)
     rel_row = jnp.pad(rel.reshape(1, -1), ((0, 0), (0, width - BUCKETS * 4 * heads)))
     small = jnp.concatenate([gain1[:1], gain2[:1], gain3[:1], rel_row, jnp.zeros((4, width), F32)], 0)

time: 386 us -> 331 us (0.86)
  Pallas kernels: 337 us -> 296 us
  local copies, waits for them, and re-layouts: 30.7 us -> 19 us
    pallas_call x5 -> x3, Pallas kernels: 89 us -> 61.4 us  [grid_call(): pl.pallas_call(kernel, name=name, grid=(4,), in_specs=in_specs, out_specs...]
    pallas_call x1, Pallas kernels: 118 us -> 101 us  [forward(): pl.pallas_call(forward_kernel, name='forward', grid=(8,), in_specs=[SMEM_...]
    slice x10 -> x0, local copies, waits for them, and re-layouts: 15.4 us -> none  [qokv(): return jnp.concatenate([w[0], w[3], w[1], w[2]], axis=1)]
    another operation x1 -> x0, other arithmetic: 4.35 us -> none  [local(): jnp.stack([qokv(self_weights), qokv(cross_weights), ffn_packed[:, :width]...]
where the time goes in v2:
time: 331 us; the launch traced here: 330 us
  Pallas kernels  296 us (89%)
  local copies, waits for them, and re-layouts  19 us (6%)
  other arithmetic  10.4 us (3%)
    pallas_call x1, Pallas kernels, reduce_grads(): pl.pallas_call(reduce_kernel, name='reduce', in_specs=[any_spec] * 3 + [v...  121 us
    pallas_call x1, Pallas kernels, forward(): pl.pallas_call(forward_kernel, name='forward', grid=(8,), in_specs=[SMEM_...  101 us
    pallas_call x3, Pallas kernels, grid_call(): pl.pallas_call(kernel, name=name, grid=(4,), in_specs=in_specs, out_specs...  61.4 us
    pallas_call x1, Pallas kernels, reduce_stats(): pl.pallas_call(functools.partial(stats_kernel, wide_count), name='stats',...  12.9 us

profile of v2, /device:TPU:0, one launch (start us, length us, event | category | flops | bytes accessed | tf_op | source)
XLA Modules:
  0.0 329.6 jit_solution(8929546833852667020)
XLA Ops:
  1.3 1.2 constant_dynamic-slice_fusion.1.segq_ref
  2.5 1.2 compare_and_fusion
  3.8 0.8 pad_dynamic-slice_fusion
  5.1 1.0 convolution_bitcast_fusion
  6.7 0.7 broadcast_select_fusion.1.bd_ref
  7.4 0.9 reshape.121.segk_ref
  8.3 2.5 copy.31
  10.8 1.6 copy.32
  12.4 101.3 %forward.1 = (bf16[4,4,16,48,768]{4,3,2,1,0:T(8,128)(2,1)}, f32[256,768]{1,0:T(8,128)}, bf16[768,768]{1,0:T(8,128)(2,1)}, bf16[4,256,192]{2,1,0:T(8,128)(2,1)}, ...) custom-call(s32[1]{0:T(128)S(6)} %copy.42.valid_ref, ...), custom_call_target="tpu_custom_call" | custom-call | tf_op jit(solution)/shard_map/forward/pallas_call | solution.py:645
  113.8 14.1 %ffn.1 = (bf16[256,768]{1,0:T(8,128)(2,1)}, f32[256,768]{1,0:T(8,128)}, bf16[4,2,768,768]{3,2,1,0:T(8,128)(2,1)}, f32[8,768]{1,0:T(8,128)}) custom-call(f32[256,768]{1,0:T(8,128)} %get-tuple-element.48.x2_ref, bf16[256,768]{1,0:T(8,128)(2,1)} %cot_ref.1, f32[3,768]{1,0:T(4,128)} %gain_ref.9, bf16[4,4,768,768]{3,2,1,0:T(8,128)(2,1)} %bitcast.62, ...), custom_call_target="tpu_custom_call" | custom-call | flops 8000000000 | bytes 15360000 | tf_op jit(solution)/shard_map/ffn/pallas_call | solution.py:273
  127.9 1.3 slice.110
  129.3 19.9 %cross_bwd.1 = (bf16[4,768,768]{2,1,0:T(8,128)(2,1)}, f32[256,768]{1,0:T(8,128)}, bf16[512,768]{1,0:T(8,128)(2,1)}, f32[8,768]{1,0:T(8,128)}) custom-call(s32[1]{0:T(128)S(6)} %copy.42.valid_ref, f32[256,768]{1,0:T(8,128)} %get-tuple-element.52.g2_ref, f32[256,768]{1,0:T(8,128)} %get-tuple-element.53.x1_ref, f32[3,768]{1,0:T(4,128)} %gain_ref.9, ...), custom_call_target="tpu_custom_call" | custom-call | flops 6000000000 | bytes 11034624 | tf_op jit(solution)/shard_map/cross_bwd/pallas_call | solution.py:273
  149.2 27.3 %self_bwd.1 = (bf16[4,768,768]{2,1,0:T(8,128)(2,1)}, f32[256,768]{1,0:T(8,128)}, bf16[2,256,768]{2,1,0:T(8,128)(2,1)}, f32[4,3,512]{2,1,0:T(4,128)}) custom-call(f32[256,768]{1,0:T(8,128)} %get-tuple-element.60.g1_ref, f32[3,768]{1,0:T(4,128)} %gain_ref.9, bf16[4,4,768,768]{3,2,1,0:T(8,128)(2,1)} %bitcast.65, bf16[768,768]{1,0:T(8,128)(2,1)} %get-tuple-element.61.h1_ref, ...), custom_call_target="tpu_custom_call" | custom-call | flops 8000000000 | bytes 11034624 | tf_op jit(solution)/shard_map/self_bwd/pallas_call | solution.py:273
  176.5 120.6 %reduce.7 = (f32[4,96,768]{2,1,0:T(8,128)}, f32[256,768]{1,0:T(8,128)}, f32[128,768]{1,0:T(8,128)}, f32[8,768]{1,0:T(8,128)}) custom-call(bf16[4,2,4,2,96,768]{5,4,3,2,1,0:T(8,128)(2,1)} %bitcast.66, bf16[4,4,2,96,768]{4,3,2,1,0:T(8,128)(2,1)} %bitcast.69, bf16[4,4,2,96,768]{4,3,2,1,0:T(8,128)(2,1)} %bitcast.70, ...), custom_call_target="tpu_custom_call" | custom-call | tf_op jit(solution)/shard_map/reduce/pallas_call | solution.py:855
  297.1 0.8 slice.108
  297.9 0.7 slice.109
  298.6 1.5 gather_fusion.1
  300.1 0.7 broadcast_select_fusion
  300.8 1.5 fusion.6
  302.5 1.3 concatenate.19.a_ref
  303.8 12.9 %stats.1 = (f32[24,128]{1,0:T(8,128)}, f32[8,768]{1,0:T(8,128)}, f32[8,768]{1,0:T(8,128)}, f32[8,8,128]{2,1,0:T(8,128)}, f32[4,8,768]{2,1,0:T(8,128)}) custom-call(f32[4,96,768]{2,1,0:T(8,128)} %get-tuple-element.72.f_ref, f32[8,768]{1,0:T(8,128)} %concatenate.19.a_ref), custom_call_target="tpu_custom_call" | custom-call | tf_op jit(solution)/shard_map/stats/pallas_call | solution.py:1011
  316.7 0.8 multiply_bitcast_fusion.1
  317.8 0.9 pad_maximum_fusion
  318.6 0.7 fusion.4
  319.9 1.3 slice_multiply_fusion.1
  321.2 0.7 fusion.5
  323.9 0.9 multiply_bitcast_fusion
  325.5 0.7 copy.38
  326.3 0.8 pad_maximum_fusion.2
  327.2 0.8 pad_maximum_fusion.1
  328.0 0.9 copy.43
  328.9 0.7 copy.44
  (40 shorter events, 5.2 us)
Async XLA Ops:
  7.4 3.4 %copy-start.1 = (bf16[4,768,192]{1,2,0:T(8,128)(2,1)S(1)}, bf16[4,768,192]{1,2,0:T(8,128)(2,1)}, u32[]{:S(2)}) copy-start(bf16[4,768,192]{1,2,0:T(8,128)(2,1)} %param.23) | copy-start | bytes 3538948
  297.0 20.5 %copy-start = (f32[4,96,768]{2,1,0:T(8,128)S(1)}, f32[4,96,768]{2,1,0:T(8,128)}, u32[]{:S(2)}) copy-start(f32[4,96,768]{2,1,0:T(8,128)} %get-tuple-element.72.f_ref) | copy-start | bytes 3538948
  317.7 1.6 copy-start.4
  317.7 4.8 %copy-start.5 = (f32[8,768]{1,0:T(8,128)S(1)}, f32[8,768]{1,0:T(8,128)}, u32[]{:S(2)}) copy-start(f32[8,768]{1,0:T(8,128)} %get-tuple-element.79) | copy-start | bytes 73732
  326.2 1.8 copy-start.2
  327.1 1.8 copy-start.3

commit v3 on v2

--- a/solution.py
+++ b/solution.py
@@ -74,215 +74,15 @@
         mask_ref[b] = jnp.where(allowed, 1.0, 0.0)
 
 
-def self_bwd_kernel(
-    g1_ref, gain_ref, w_ref, h1_ref, q_ref, kv_ref, o_ref, bias_ref, bd_ref, segq_ref, segk_ref,
-    grad_ref, dh_ref, dx_ref, rel_ref,
-    mask_ref, da_ref, flip_ref, acc_ref,
-):
-    rows = g1_ref.shape[0]
-    ext = 3 * rows
-    span = 2 * rows + 128
-    hw = q_ref.shape[2]
-    heads = hw // 64
-    j = pl.program_id(0)
-
-    @pl.when(j == 0)
-    def _():
-        da_ref[...] = g1_ref[...].astype(BF)
-        self_mask_store(mask_ref, segk_ref, segq_ref, rows, span)
-        r = lax.broadcasted_iota(jnp.int32, (256, 256), 0)
-        c = lax.broadcasted_iota(jnp.int32, (256, 256), 1)
-        flip_ref[...] = jnp.where(r + c == 255, 1.0, 0.0).astype(BF)
-        acc_ref[...] = jnp.zeros_like(acc_ref)
-
-    da = da_ref[...]
-    q = q_ref[0]
-    kv = kv_ref[0]
-    do = mm(da, w_ref[:, hw : 2 * hw]).astype(BF)
-    dq_parts, dk_parts, dv_parts = [], [], []
-    for hh in range(heads):
-        far = bd_ref[0, hh : hh + 1, 127:128]
-        dq_cols, dks, dvs = [], [], []
-        band = jnp.zeros((256, 128), F32)
-        total = jnp.zeros((1, 128), F32)
-        for b in range(2):
-            k = kv[b * 128 : b * 128 + span, hh * 64 : hh * 64 + 64]
-            v = kv[b * 128 : b * 128 + span, hw + hh * 64 : hw + hh * 64 + 64]
-            qb = q[b * 128 : b * 128 + 128, hh * 64 : hh * 64 + 64]
-            dob = do[b * 128 : b * 128 + 128, hh * 64 : hh * 64 + 64]
-            s = mm_nt(k, qb)
-            s = jnp.concatenate([s[: span - 256] + far, s[span - 256 :] + bias_ref[0, hh]], axis=0)
-            s = jnp.where(mask_ref[b] > 0.5, s, MASKED)
-            p = soft_cols(s)
-            dp = mm_nt(v, dob)
-            ds = (p * (dp - jnp.sum(p * dp, axis=0, keepdims=True))).astype(BF)
-            dvs.append(mm(p.astype(BF), dob))
-            dks.append(mm(ds, qb))
-            dq_cols.append(mm_tn(k, ds))
-            band = band + mm(flip_ref[...], ds[span - 256 :])
-            total = total + jnp.sum(ds[: span - 256].astype(F32), axis=0, keepdims=True)
-        gap = jnp.zeros((128, 64), F32)
-        dk_parts.append(jnp.concatenate([dks[0], gap], 0) + jnp.concatenate([gap, dks[1]], 0))
-        dv_parts.append(jnp.concatenate([dvs[0], gap], 0) + jnp.concatenate([gap, dvs[1]], 0))
-        dq_parts.append(jnp.concatenate(dq_cols, axis=1))
-        wide_band = jnp.concatenate([band, jnp.zeros((256, 384), F32)], axis=1)
-        aligned = pltpu.roll(wide_band, 0, 1, stride=1, stride_axis=0)
-        line = jnp.sum(aligned, axis=0, keepdims=True)
-        lane = lax.broadcasted_iota(jnp.int32, (1, 512), 1)
-        far_sum = jnp.sum(total, axis=1, keepdims=True)
-        rel_ref[0, hh : hh + 1, :] = jnp.where(lane == 511, far_sum, line)
-    dq = jnp.concatenate(dq_parts, axis=0).T.astype(BF)
-    dkv = jnp.concatenate(dk_parts + dv_parts, axis=1).astype(BF)
-    zero = jnp.zeros((rows, hw), BF)
-    left = jnp.concatenate([h1_ref[2 * rows : ext, :], da], axis=0)
-    right = jnp.concatenate(
-        [jnp.concatenate([dq, zero], axis=1), jnp.concatenate([zero, o_ref[0]], axis=1)], axis=0
-    )
-    grad_ref[0, :, 0 : 2 * hw] = mm_tn(left, right).astype(BF)
-    grad_ref[0, :, 2 * hw : 4 * hw] = mm_tn(h1_ref[...], dkv).astype(BF)
-    acc_ref[...] += mm_nt(dkv, w_ref[:, 2 * hw : 4 * hw])
-    acc_ref[2 * rows : ext, :] += mm_nt(dq, w_ref[:, 0:hw])
-
-    @pl.when(j == 3)
-    def _():
-        dh_ref[...] = acc_ref[2 * rows : ext, :]
-        for t in range(2):
-            dx_ref[t] = acc_ref[t * rows : (t + 1) * rows, :].astype(BF)
-
-
-def cross_bwd_kernel(
-    valid_ref, g2_ref, x1_ref, gain_ref, w_ref, mem_ref, h2_ref, q_ref, kv_ref, o_ref,
-    grad_ref, g1_ref, dmem_ref, gsum_ref,
-    dc_ref, dh_ref, macc_ref,
-):
-    rows = g2_ref.shape[0]
-    mem = mem_ref.shape[0]
-    hw = q_ref.shape[2]
-    heads = hw // 64
-    j = pl.program_id(0)
-
-    @pl.when(j == 0)
-    def _():
-        dc_ref[...] = g2_ref[...].astype(BF)
-        dh_ref[...] = jnp.zeros_like(dh_ref)
-        macc_ref[...] = jnp.zeros_like(macc_ref)
-
-    dc = dc_ref[...]
-    q = q_ref[0]
-    kv = kv_ref[0]
-    do = mm(dc, w_ref[:, hw : 2 * hw]).astype(BF)
-    allowed = lax.broadcasted_iota(jnp.int32, (mem, rows), 0) < valid_ref[0]
-    dq_parts, dk_parts, dv_parts = [], [], []
-    for hh in range(heads):
-        k = kv[:, hh * 64 : hh * 64 + 64]
-        v = kv[:, hw + hh * 64 : hw + hh * 64 + 64]
-        qh = q[:, hh * 64 : hh * 64 + 64]
-        doh = do[:, hh * 64 : hh * 64 + 64]
-        p = soft_cols(jnp.where(allowed, mm_nt(k, qh), MASKED))
-        dp = mm_nt(v, doh)
-        ds = (p * (dp - jnp.sum(p * dp, axis=0, keepdims=True))).astype(BF)
-        dv_parts.append(mm(p.astype(BF), doh))
-        dk_parts.append(mm(ds, qh))
-        dq_parts.append(mm_tn(k, ds))
-    dq = jnp.concatenate(dq_parts, axis=0).T.astype(BF)
-    dkv = jnp.concatenate(dk_parts + dv_parts, axis=1).astype(BF)
-    zero = jnp.zeros((rows, hw), BF)
-    left = jnp.concatenate([h2_ref[...], dc], axis=0)
-    right = jnp.concatenate(
-        [jnp.concatenate([dq, zero], axis=1), jnp.concatenate([zero, o_ref[0]], axis=1)], axis=0
-    )
-    grad_ref[0, :, 0 : 2 * hw] = mm_tn(left, right).astype(BF)
-    grad_ref[0, :, 2 * hw : 4 * hw] = mm_tn(mem_ref[...], dkv).astype(BF)
-    dh_ref[...] += mm_nt(dq, w_ref[:, 0:hw])
-    macc_ref[...] += mm_nt(dkv, w_ref[:, 2 * hw : 4 * hw])
-
-    @pl.when(j == 3)
-    def _():
-        gain_part, dv = norm_back(x1_ref[...], gain_ref[1:2, :], dh_ref[...])
-        gsum_ref[...] = jnp.broadcast_to(gain_part, gsum_ref.shape)
-        g1_ref[...] = g2_ref[...] + dv
-        dmem_ref[...] = macc_ref[...].astype(BF)
-
-
-def ffn_kernel(
-    x2_ref, cot_ref, gain_ref, wa_ref, wb_ref,
-    out_ref, g2_ref, grad_ref, gsum_ref,
-    h3_ref, acc_ref, dh_ref,
-):
-    fw = wa_ref.shape[1] * 2 // 3
-    j = pl.program_id(0)
-
-    @pl.when(j == 0)
-    def _():
-        x2 = x2_ref[...]
-        acc_ref[...] = x2
-        h3_ref[...] = (x2 * inv_rms(x2) * gain_ref[2:3, :]).astype(BF)
-        dh_ref[...] = jnp.zeros_like(dh_ref)
-
-    h3 = h3_ref[...]
-    df = cot_ref[...]
-    wg = wa_ref[:, 0:fw]
-    wu = jnp.concatenate([wa_ref[:, fw:], wb_ref[:, 0 : fw // 2]], axis=1)
-    wd = wb_ref[:, fw // 2 :]
-    gate = mm(h3, wg)
-    up = mm(h3, wu)
-    c0 = math.sqrt(2.0 / math.pi)
-    gate2 = gate * gate
-    t = jnp.tanh(c0 * (gate + 0.044715 * gate2 * gate))
-    half = 0.5 * (1.0 + t)
-    gelu = gate * half
-    slope = half + 0.5 * gate * (1.0 - t * t) * (c0 * (1.0 + 3.0 * 0.044715 * gate2))
-    act = (gelu * up).astype(BF)
-    acc_ref[...] += mm_nt(act, wd)
-    da = mm(df, wd)
-    dgate = (da * up * slope).astype(BF)
-    dup = (da * gelu).astype(BF)
-    dgu = jnp.concatenate([dgate, dup], axis=1)
-    ggu = mm_tn(h3, dgu).astype(BF)
-    grad_ref[0, 0] = ggu[:, 0 : fw * 3 // 2]
-    grad_ref[0, 1, :, 0 : fw // 2] = ggu[:, fw * 3 // 2 :]
-    grad_ref[0, 1, :, fw // 2 :] = mm_tn(df, act).astype(BF)
-    dh_ref[...] += mm_nt(dgate, wg) + mm_nt(dup, wu)
-
-    @pl.when(j == 3)
-    def _():
-        out_ref[...] = acc_ref[...].astype(BF)
-        gain_part, dv = norm_back(x2_ref[...], gain_ref[2:3, :], dh_ref[...])
-        gsum_ref[...] = jnp.broadcast_to(gain_part, gsum_ref.shape)
-        g2_ref[...] = df.astype(F32) + dv
-
-
 def full(shape):
     return pl.BlockSpec(shape, lambda j: (0,) * len(shape))
 
 
-def slot(shape):
-    return pl.BlockSpec((1,) + shape, lambda j: (j,) + (0,) * len(shape))
-
-
-def weight(chunk, shape):
-    return pl.BlockSpec((None, None) + shape, lambda j: (chunk, j, 0, 0))
+def once(shape):
+    return pl.BlockSpec(shape, lambda j: (0,) * len(shape), pipeline_mode=pl.Buffered(1))
 
 
 SMEM_SPEC = pl.BlockSpec(memory_space=pltpu.SMEM)
-
-
-def grid_call(kernel, name, in_specs, out, scratch, args, flops):
-    shapes = [jax.ShapeDtypeStruct(s, d) for s, d, _ in out]
-    nbytes = sum(math.prod(s) * jnp.dtype(d).itemsize for s, d, _ in out) + 4 * 768 * 768 * 2
-    return pl.pallas_call(
-        kernel,
-        name=name,
-        grid=(4,),
-        in_specs=in_specs,
-        out_specs=[spec for _, _, spec in out],
-        out_shape=shapes,
-        scratch_shapes=scratch,
-        compiler_params=pltpu.CompilerParams(
-            dimension_semantics=("arbitrary",), vmem_limit_bytes=VMEM_LIMIT
-        ),
-        cost_estimate=pl.CostEstimate(flops=flops, bytes_accessed=nbytes, transcendentals=0),
-    )(*args)
 
 
 class Place:
@@ -304,12 +104,19 @@
     def narrow_dev(self, k):
         return {"narrow": lax.rem(self.z + k, 4)}
 
+    def devices(self):
+        return [self.core_dev, self.x_dev, self.y_dev] + [self.narrow_dev(k) for k in (1, 2, 3)]
+
+    def signal_all(self):
+        for dev in self.devices():
+            pl.semaphore_signal(pltpu.get_barrier_semaphore(), inc=1, device_id=dev, device_id_type=MESH)
+
+    def wait_all(self):
+        pl.semaphore_wait(pltpu.get_barrier_semaphore(), len(self.devices()))
+
     def barrier(self):
-        sem = pltpu.get_barrier_semaphore()
-        devs = [self.core_dev, self.x_dev, self.y_dev] + [self.narrow_dev(k) for k in (1, 2, 3)]
-        for dev in devs:
-            pl.semaphore_signal(sem, inc=1, device_id=dev, device_id_type=MESH)
-        pl.semaphore_wait(sem, len(devs))
+        self.signal_all()
+        self.wait_all()
 
 
 def remote(src, dst, send_sem, recv_sem, dev):
@@ -665,82 +472,76 @@
     )(valid_rows, tokens, memory, gains, bias_line, seg_q, seg_k, ws, wc, wf)
 
 
-QUARTERS = (3, 0, 2, 1)
-
-
-def reduce_kernel(
-    gf_ref, gc_ref, gs_ref, dx_ref, dm_ref, dh_ref, tok_ref, g1_ref, gain_ref,
-    f_ref, tg_ref, mg_ref, gsum_ref,
-    own, rc, xr, yr, x2, y2, zu, zd, dxr, dmr,
-    lsem, cs, cr, xs, xrs, ys, yrs, x2s, x2r, y2s, y2r, us, ur, ds_, dr, dxs, dxrs, dms, dmrs,
+CHUNKS = [(2 + i % 2, i // 2) for i in range(8)] + [(1, i) for i in range(4)] + [(0, i) for i in range(4)]
+HELD = 12
+TICKS = [(1, 0), (2, 0), (3, 0), (4, 1), (5, 1), (6, 1), (7, 1), (8, 0), (8, 2), (9, 1), (10, 0), (10, 2), (11, 1)]
+
+
+def backward_kernel(
+    valid_ref, x2_ref, cot_ref, x1_ref, mem_ref, h2_ref, h1_ref, tok_ref, gain_ref, bd_ref, segq_ref, segk_ref,
+    w_ref, q2_ref, kv2_ref, o2_ref, q1_ref, kv1_ref, o1_ref, bias_ref,
+    out_ref, f_ref, tg_ref, mg_ref, gsum_ref, rel_ref,
+    g, wbuf, acc, act_in, res, do_ref, dqt_ref, dkv_ref, mask_ref, flip_ref, dxo, dmo, rc, xr, yr, xr2, yr2, zb, dxr, dmr,
+    wsem, cs, cr, xs, xrs, ys, yrs, x2s, x2r, y2s, y2r, zs, zr, dxs, dxrs, dms, dmrs,
 ):
     at = Place()
     z = at.z
-    half = own.shape[3] // 2
-    at.barrier()
-    groups = [
-        (2, lambda j: gf_ref.at[j, 0]), (3, lambda j: gf_ref.at[j, 1]),
-        (1, lambda j: gc_ref.at[j]), (0, lambda j: gs_ref.at[j]),
-    ]
-    chunks = [(out, get, q) for out, get in groups for q in QUARTERS]
-    n = len(chunks)
-
-    def dx_send(t):
-        return remote(dx_ref.at[t], dxr.at[t], dxs.at[t], dxrs.at[t], {"narrow": z - 2 + t})
-
-    def dm_send(k):
-        return remote(dm_ref.at[lax.rem(z + k, 4)], dmr.at[k - 1], dms.at[k - 1], dmrs.at[k - 1], at.narrow_dev(k))
-
-    e0 = 1 - (z + 3) // 4
-    e3 = z // 3
-    e1 = (1 - z // 2) * lax.rem(z, 2)
-    e2 = (z // 2) * (1 - lax.rem(z, 2))
-
-    def rank(q):
-        return sum(e * row.index(q) for e, row in zip((e0, e1, e2, e3), RANKS))
-
-    def core_send(i):
-        _, get, q = chunks[i]
-        src = get(rank(q)).at[:, pl.ds(1 - at.c, 1)]
-        return remote(src, rc.at[i], cs.at[i], cr.at[i], at.core_dev)
-
-    def load(i):
-        _, get, q = chunks[i]
-        src = get(rank(q)).at[:, pl.ds(at.c, 1)]
-        return pltpu.make_async_copy(src, own.at[i], lsem.at[i])
-
-    for i in range(n):
-        load(i).start()
-        core_send(i).start()
-    for t in range(2):
-        @pl.when(z >= 2 - t)
-        def _():
-            dx_send(t).start()
-    for k in (1, 2, 3):
-        dm_send(k).start()
-
+    j = pl.program_id(0)
+    rows, width = x2_ref.shape
+    mem = mem_ref.shape[0]
+    ext = 3 * rows
+    span = 2 * rows + 128
+    hw = q1_ref.shape[2]
+    heads = hw // 64
+    fw = wbuf.shape[2] * 2 // 3
+    own_rows = g.shape[3]
+    half = own_rows // 2
+    n = len(CHUNKS)
     lo, hi = pl.ds(0, half), pl.ds(half, half)
     yx = 2 * at.y + at.x
+    top, bottom = pl.ds(0, rows), pl.ds(2 * rows, rows)
+
+    def w_load(unit, slot, k):
+        return pltpu.make_async_copy(w_ref.at[unit, slot], wbuf.at[k], wsem.at[k])
+
+    def held(i):
+        return g.at[i % HELD]
 
     def add(ref, other):
-        ref[...] = (ref[...].astype(F32) + other[...].astype(F32)).astype(BF)
+        ref[...] = ref[...] + other[...]
+
+    def core_send(i):
+        return remote(held(i).at[:, pl.ds(1 - at.c, 1)], rc.at[i], cs.at[i], cr.at[i], at.core_dev)
 
     def x_send(i, yb):
-        return remote(own.at[i, 2 * yb + 1 - at.x, 0, lo], xr.at[i, yb], xs.at[i, yb], xrs.at[i, yb], at.x_dev)
+        src = held(i).at[2 * yb + 1 - at.x, at.c, lo]
+        return remote(src, xr.at[i, yb], xs.at[i, yb], xrs.at[i, yb], at.x_dev)
 
     def y_send(i, xb):
-        return remote(own.at[i, 2 * (1 - at.y) + xb, 0, hi], yr.at[i, xb], ys.at[i, xb], yrs.at[i, xb], at.y_dev)
+        src = held(i).at[2 * (1 - at.y) + xb, at.c, hi]
+        return remote(src, yr.at[i, xb], ys.at[i, xb], yrs.at[i, xb], at.y_dev)
 
     def y2_send(i):
-        return remote(own.at[i, 2 * (1 - at.y) + at.x, 0, lo], y2.at[i], y2s.at[i], y2r.at[i], at.y_dev)
+        return remote(held(i).at[2 * (1 - at.y) + at.x, at.c, lo], yr2.at[i], y2s.at[i], y2r.at[i], at.y_dev)
 
     def x2_send(i):
-        return remote(own.at[i, 2 * at.y + 1 - at.x, 0, hi], x2.at[i], x2s.at[i], x2r.at[i], at.x_dev)
+        return remote(held(i).at[2 * at.y + 1 - at.x, at.c, hi], xr2.at[i], x2s.at[i], x2r.at[i], at.x_dev)
+
+    d = 1 - 2 * (z // 2)
+    is_end = jnp.logical_or(z == 0, z == 3)
+    is_inner = jnp.logical_or(z == 1, z == 2)
+
+    def z_send(i, dst, step):
+        unit = CHUNKS[i][0]
+        return remote(held(i).at[yx, at.c], zb.at[unit, dst], zs.at[i], zr.at[unit, dst], {"narrow": z + step})
+
+    def z_wait(i, k):
+        unit = CHUNKS[i][0]
+        remote(zb.at[unit, k], zb.at[unit, k], zs.at[i], zr.at[unit, k], at.x_dev).wait_recv()
 
     def step_b(i):
-        load(i).wait()
         core_send(i).wait_recv()
-        add(own.at[i], rc.at[i])
+        add(held(i).at[:, pl.ds(at.c, 1)], rc.at[i])
         for b in range(2):
             x_send(i, b).start()
             y_send(i, b).start()
@@ -749,136 +550,374 @@
         for b in range(2):
             x_send(i, b).wait_recv()
             y_send(i, b).wait_recv()
-            add(own.at[i, 2 * b + at.x, 0, lo], xr.at[i, b])
-            add(own.at[i, 2 * at.y + b, 0, hi], yr.at[i, b])
+            add(held(i).at[2 * b + at.x, at.c, lo], xr.at[i, b])
+            add(held(i).at[2 * at.y + b, at.c, hi], yr.at[i, b])
         y2_send(i).start()
         x2_send(i).start()
 
     def step_d(i):
         y2_send(i).wait_recv()
-        add(own.at[i, yx, 0, lo], y2.at[i])
+        add(held(i).at[yx, at.c, lo], yr2.at[i])
         x2_send(i).wait_recv()
-        add(own.at[i, yx, 0, hi], x2.at[i])
-
-    def up(i, k):
-        return remote(own.at[i, yx, 0], zu.at[i], us.at[i], ur.at[i], {"narrow": k + 1})
-
-    def down(i, k):
-        return remote(own.at[i, yx, 0], zd.at[i], ds_.at[i], dr.at[i], {"narrow": k - 1})
-
-    def step_e(i, h):
-        out, _, q = chunks[i]
-        if h < q:
-            @pl.when(z == h)
+        add(held(i).at[yx, at.c, hi], xr2.at[i])
+
+    def step_e(i):
+        @pl.when(is_end)
+        def _():
+            if CHUNKS[i][1] < 3:
+                z_send(i, CHUNKS[i][1], d).start()
+
+    def step_f(i):
+        unit, s = CHUNKS[i]
+
+        @pl.when(is_inner)
+        def _():
+            if s < 2:
+                z_wait(i, s)
+                add(held(i).at[yx, at.c], zb.at[unit, s])
+                z_send(i, 3 + s, d).start()
+            if s == 2:
+                z_wait(i, 3)
+                add(held(i).at[yx, at.c], zb.at[unit, 3])
+                z_send(i, 2, -d).start()
+            if s == 3:
+                z_wait(i, 2)
+                z_wait(i, 4)
+                f_ref[unit] = (
+                    held(i)[yx, at.c].astype(F32) + zb[unit, 2].astype(F32) + zb[unit, 4].astype(F32)
+                )
+
+        if s == 3:
+            @pl.when(is_end)
             def _():
-                if h > 0:
-                    up(i, 0).wait_recv()
-                    add(own.at[i, yx, 0], zu.at[i])
-                up(i, h).start()
-        k = 3 - h
-        if k > q:
-            @pl.when(z == k)
-            def _():
-                if k < 3:
-                    down(i, 3).wait_recv()
-                    add(own.at[i, yx, 0], zd.at[i])
-                down(i, k).start()
-        if h == max(q, 3 - q):
-            @pl.when(z == q)
-            def _():
-                total = own[i, yx, 0].astype(F32)
-                if q > 0:
-                    up(i, 0).wait_recv()
-                    total = total + zu[i].astype(F32)
-                if q < 3:
-                    down(i, 3).wait_recv()
-                    total = total + zd[i].astype(F32)
-                f_ref[out] = total
-
-    for t in range(n + 6):
-        if t < n:
-            step_b(t)
-        if 0 <= t - 1 < n:
-            step_c(t - 1)
-        if 0 <= t - 2 < n:
-            step_d(t - 2)
-        for h in range(4):
-            if 0 <= t - 3 - h < n:
-                step_e(t - 3 - h, h)
-        if t == 8:
-            mg_ref[...] = dm_ref[z].astype(F32)
-            for k in (1, 2, 3):
-                dm_send(k).wait_recv()
-                mg_ref[...] += dmr[k - 1].astype(F32)
-            tg_ref[...] = dh_ref[...]
-            for d in range(2):
-                @pl.when(z < 2 + d)
-                def _():
-                    dx_send(d).wait_recv()
-                    tg_ref[...] += dxr[d].astype(F32)
-            gain_part, dv = norm_back(tok_ref[...].astype(F32), gain_ref[0:1, :], tg_ref[...])
-            gsum_ref[...] = jnp.broadcast_to(gain_part, gsum_ref.shape)
-            tg_ref[...] = g1_ref[...] + dv
-
-    for i in range(n):
-        q = chunks[i][2]
+                z_wait(i, 2)
+                f_ref[unit] = held(i)[yx, at.c].astype(F32) + zb[unit, 2].astype(F32)
+
+    def sent(i):
         core_send(i).wait_send()
         for b in range(2):
             x_send(i, b).wait_send()
             y_send(i, b).wait_send()
         y2_send(i).wait_send()
         x2_send(i).wait_send()
-
-        @pl.when(z < q)
+        if CHUNKS[i][1] < 3:
+            z_send(i, 0, d).wait_send()
+
+    def tick(t):
+        for k, step in enumerate((step_b, step_c, step_d, step_e, step_f)):
+            if 0 <= t - k < n:
+                step(t - k)
+
+    def hook(place, first, last):
+        for t, (jj, p) in enumerate(TICKS):
+            if p == place and first <= jj < last:
+                @pl.when(j == jj)
+                def _():
+                    tick(t)
+
+    def dx_send(t):
+        return remote(dxo.at[t], dxr.at[t], dxs.at[t], dxrs.at[t], {"narrow": z - 2 + t})
+
+    def dm_send(k):
+        return remote(dmo.at[lax.rem(z + k, 4)], dmr.at[k - 1], dms.at[k - 1], dmrs.at[k - 1], at.narrow_dev(k))
+
+    @pl.when(j == 0)
+    def _():
+        for b in range(2):
+            w_load(2 + b, 3, b).start()
+        at.signal_all()
+        x2 = x2_ref[...]
+        acc[0:rows, :] = x2
+        acc[rows : 2 * rows, :] = jnp.zeros((rows, width), F32)
+        act_in[...] = (x2 * inv_rms(x2) * gain_ref[2:3, :]).astype(BF)
+
+    @pl.when(j < 4)
+    def _():
+        k = 2 * lax.rem(j, 2)
+        for b in range(2):
+            w_load(2 + b, 3 - j, k + b).wait()
+
+        @pl.when(j < 3)
         def _():
-            up(i, 0).wait_send()
-
-        @pl.when(z > q)
+            for b in range(2):
+                w_load(2 + b, 2 - j, 2 - k + b).start()
+
+        @pl.when(j == 3)
         def _():
-            down(i, 3).wait_send()
-    for t in range(2):
-        @pl.when(z >= 2 - t)
+            w_load(1, 3, 0).start()
+
+        @pl.when(j == 0)
         def _():
-            dx_send(t).wait_send()
-    for k in (1, 2, 3):
-        dm_send(k).wait_send()
-
-
-def reduce_grads(gf, gc, gs, dx, dm, dh, tok, g1, gains):
-    own, width = gs.shape[3:]
+            at.wait_all()
+
+        hook(0, 0, 4)
+        h3 = act_in[...]
+        df = cot_ref[...]
+        wg = wbuf[k, :, 0:fw]
+        wu = jnp.concatenate([wbuf[k, :, fw:], wbuf[k + 1, :, 0 : fw // 2]], axis=1)
+        wd = wbuf[k + 1, :, fw // 2 :]
+        gate = mm(h3, wg)
+        up = mm(h3, wu)
+        c0 = math.sqrt(2.0 / math.pi)
+        gate2 = gate * gate
+        t = jnp.tanh(c0 * (gate + 0.044715 * gate2 * gate))
+        part = 0.5 * (1.0 + t)
+        gelu = gate * part
+        slope = part + 0.5 * gate * (1.0 - t * t) * (c0 * (1.0 + 3.0 * 0.044715 * gate2))
+        act = (gelu * up).astype(BF)
+        acc[0:rows, :] += mm_nt(act, wd)
+        da = mm(df, wd)
+        dgate = (da * up * slope).astype(BF)
+        dup = (da * gelu).astype(BF)
+        dgu = jnp.concatenate([dgate, dup], axis=1)
+        ggu = mm_tn(h3, dgu).astype(BF)
+        blocks = (4, 2, own_rows)
+        g[2 * j] = ggu[:, 0 : fw * 3 // 2].reshape(blocks + (width,))
+        g[2 * j + 1, :, :, :, 0 : fw // 2] = ggu[:, fw * 3 // 2 :].reshape(blocks + (fw // 2,))
+        g[2 * j + 1, :, :, :, fw // 2 :] = mm_tn(df, act).astype(BF).reshape(blocks + (fw,))
+        acc[rows : 2 * rows, :] += mm_nt(dgate, wg) + mm_nt(dup, wu)
+        for jj in range(4):
+            @pl.when(j == jj)
+            def _():
+                core_send(2 * jj).start()
+                core_send(2 * jj + 1).start()
+
+    @pl.when(j == 3)
+    def _():
+        out_ref[...] = acc[0:rows, :].astype(BF)
+        gain_part, dv = norm_back(x2_ref[...], gain_ref[2:3, :], acc[rows : 2 * rows, :])
+        gsum_ref[16:24, :] = jnp.broadcast_to(gain_part, (8, width))
+        g2 = cot_ref[...].astype(F32) + dv
+        res[...] = g2
+        act_in[...] = g2.astype(BF)
+        acc[...] = jnp.zeros_like(acc)
+
+    @pl.when(jnp.logical_and(j >= 4, j < 8))
+    def _():
+        k0 = j - 4
+        w_load(1, 7 - j, k0).wait()
+
+        @pl.when(j < 7)
+        def _():
+            w_load(1, 6 - j, k0 + 1).start()
+
+        @pl.when(j == 7)
+        def _():
+            w_load(0, 3, 0).start()
+
+        do_ref[...] = mm(act_in[...], wbuf[k0, :, hw : 2 * hw]).astype(BF)
+        for hh in range(heads):
+            h_cols, v_cols = slice(hh * 64, hh * 64 + 64), slice(hw + hh * 64, hw + hh * 64 + 64)
+            k = kv2_ref[0, :, h_cols]
+            v = kv2_ref[0, :, v_cols]
+            qh = q2_ref[0, :, h_cols]
+            doh = do_ref[:, h_cols]
+            allowed = lax.broadcasted_iota(jnp.int32, (mem, rows), 0) < valid_ref[0]
+            p = soft_cols(jnp.where(allowed, mm_nt(k, qh), MASKED))
+            dp = mm_nt(v, doh)
+            ds = (p * (dp - jnp.sum(p * dp, axis=0, keepdims=True))).astype(BF)
+            dkv_ref[0:mem, v_cols] = mm(p.astype(BF), doh).astype(BF)
+            dkv_ref[0:mem, h_cols] = mm(ds, qh).astype(BF)
+            dqt_ref[h_cols, :] = mm_tn(k, ds)
+            hook(hh, 4, 8)
+        dc = act_in[...]
+        dq = dqt_ref[...].T.astype(BF)
+        dkv = dkv_ref[0:mem, :]
+        zero = jnp.zeros((rows, hw), BF)
+        left = jnp.concatenate([h2_ref[...], dc], axis=0)
+        right = jnp.concatenate(
+            [jnp.concatenate([dq, zero], axis=1), jnp.concatenate([zero, o2_ref[0]], axis=1)], axis=0
+        )
+        blocks = (4, 2, own_rows, 2 * hw)
+        g[4 + j, :, :, :, 0 : 2 * hw] = mm_tn(left, right).astype(BF).reshape(blocks)
+        g[4 + j, :, :, :, 2 * hw : 4 * hw] = mm_tn(mem_ref[...], dkv).astype(BF).reshape(blocks)
+        for jj in range(4, 8):
+            @pl.when(j == jj)
+            def _():
+                core_send(4 + jj).start()
+        acc[0:rows, :] += mm_nt(dq, wbuf[k0, :, 0:hw])
+        acc[rows : rows + mem, :] += mm_nt(dkv, wbuf[k0, :, 2 * hw : 4 * hw])
+
+    @pl.when(j == 7)
+    def _():
+        for k in range(4):
+            dmo[k] = acc[rows + k * (mem // 4) : rows + (k + 1) * (mem // 4), :].astype(BF)
+        for k in (1, 2, 3):
+            dm_send(k).start()
+        gain_part, dv = norm_back(x1_ref[...], gain_ref[1:2, :], acc[0:rows, :])
+        gsum_ref[8:16, :] = jnp.broadcast_to(gain_part, (8, width))
+        g1 = res[...] + dv
+        res[...] = g1
+        act_in[...] = g1.astype(BF)
+        acc[...] = jnp.zeros_like(acc)
+        self_mask_store(mask_ref, segk_ref, segq_ref, rows, span)
+        r = lax.broadcasted_iota(jnp.int32, (256, 256), 0)
+        c = lax.broadcasted_iota(jnp.int32, (256, 256), 1)
+        flip_ref[...] = jnp.where(r + c == 255, 1.0, 0.0).astype(BF)
+
+    @pl.when(j >= 8)
+    def _():
+        k0 = j - 8
+        w_load(0, 11 - j, k0).wait()
+
+        @pl.when(j < 11)
+        def _():
+            w_load(0, 10 - j, k0 + 1).start()
+
+        do_ref[...] = mm(act_in[...], wbuf[k0, :, hw : 2 * hw]).astype(BF)
+        for hh in range(heads):
+            h_cols, v_cols = slice(hh * 64, hh * 64 + 64), slice(hw + hh * 64, hw + hh * 64 + 64)
+            far = bd_ref[11 - j, hh : hh + 1, 127:128]
+            dq_cols, dks, dvs = [], [], []
+            band = jnp.zeros((256, 128), F32)
+            total = jnp.zeros((1, 128), F32)
+            for b in range(2):
+                k = kv1_ref[0, b * 128 : b * 128 + span, h_cols]
+                v = kv1_ref[0, b * 128 : b * 128 + span, v_cols]
+                qb = q1_ref[0, b * 128 : b * 128 + 128, h_cols]
+                dob = do_ref[b * 128 : b * 128 + 128, h_cols]
+                s = mm_nt(k, qb)
+                s = jnp.concatenate([s[: span - 256] + far, s[span - 256 :] + bias_ref[0, hh]], axis=0)
+                s = jnp.where(mask_ref[b] > 0.5, s, MASKED)
+                p = soft_cols(s)
+                dp = mm_nt(v, dob)
+                ds = (p * (dp - jnp.sum(p * dp, axis=0, keepdims=True))).astype(BF)
+                dvs.append(mm(p.astype(BF), dob))
+                dks.append(mm(ds, qb))
+                dq_cols.append(mm_tn(k, ds))
+                band = band + mm(flip_ref[...], ds[span - 256 :])
+                total = total + jnp.sum(ds[: span - 256].astype(F32), axis=0, keepdims=True)
+            gap = jnp.zeros((128, 64), F32)
+            dk = jnp.concatenate([dks[0], gap], 0) + jnp.concatenate([gap, dks[1]], 0)
+            dv = jnp.concatenate([dvs[0], gap], 0) + jnp.concatenate([gap, dvs[1]], 0)
+            dkv_ref[:, h_cols] = dk.astype(BF)
+            dkv_ref[:, v_cols] = dv.astype(BF)
+            dqt_ref[h_cols, :] = jnp.concatenate(dq_cols, axis=1)
+            wide_band = jnp.concatenate([band, jnp.zeros((256, 384), F32)], axis=1)
+            aligned = pltpu.roll(wide_band, 0, 1, stride=1, stride_axis=0)
+            line = jnp.sum(aligned, axis=0, keepdims=True)
+            lane = lax.broadcasted_iota(jnp.int32, (1, 512), 1)
+            far_sum = jnp.sum(total, axis=1, keepdims=True)
+            rel_ref[0, hh : hh + 1, :] = jnp.where(lane == 511, far_sum, line)
+            hook(hh, 8, 12)
+        da = act_in[...]
+        dq = dqt_ref[...].T.astype(BF)
+        dkv = dkv_ref[...]
+        zero = jnp.zeros((rows, hw), BF)
+        left = jnp.concatenate([h1_ref[2 * rows : ext, :], da], axis=0)
+        right = jnp.concatenate(
+            [jnp.concatenate([dq, zero], axis=1), jnp.concatenate([zero, o1_ref[0]], axis=1)], axis=0
+        )
+        for jj in range(8, 12):
+            @pl.when(j == jj)
+            def _():
+                sent(jj - 8)
+        blocks = (4, 2, own_rows, 2 * hw)
+        g[j - 8, :, :, :, 0 : 2 * hw] = mm_tn(left, right).astype(BF).reshape(blocks)
+        g[j - 8, :, :, :, 2 * hw : 4 * hw] = mm_tn(h1_ref[...], dkv).astype(BF).reshape(blocks)
+        for jj in range(8, 12):
+            @pl.when(j == jj)
+            def _():
+                core_send(4 + jj).start()
+        acc[...] += mm_nt(dkv, wbuf[k0, :, 2 * hw : 4 * hw])
+        acc[2 * rows : ext, :] += mm_nt(dq, wbuf[k0, :, 0:hw])
+
+    @pl.when(j == 11)
+    def _():
+        for t in range(2):
+            dxo[t] = acc[t * rows : (t + 1) * rows, :].astype(BF)
+
+            @pl.when(z >= 2 - t)
+            def _():
+                dx_send(t).start()
+        last = n + 4
+        for t in range(len(TICKS), last):
+            tick(t)
+            if t == len(TICKS):
+                mg_ref[...] = dmo[z].astype(F32)
+                for k in (1, 2, 3):
+                    dm_send(k).wait_recv()
+                    mg_ref[...] += dmr[k - 1].astype(F32)
+            if t == last - 2:
+                for k in range(2):
+                    @pl.when(z < 2 + k)
+                    def _():
+                        dx_send(k).wait_recv()
+                        acc[2 * rows : ext, :] += dxr[k].astype(F32)
+                gain_part, dv = norm_back(tok_ref[...].astype(F32), gain_ref[0:1, :], acc[2 * rows : ext, :])
+                gsum_ref[0:8, :] = jnp.broadcast_to(gain_part, (8, width))
+                tg_ref[...] = res[...] + dv
+        for i in range(n - HELD, n):
+            sent(i)
+        for t in range(2):
+            @pl.when(z >= 2 - t)
+            def _():
+                dx_send(t).wait_send()
+        for k in (1, 2, 3):
+            dm_send(k).wait_send()
+
+
+def backward(
+    valid_rows, x2, cot, x1, mem_full, h2, h1, tokens, gains, bias_line, seg_q, seg_k,
+    weights, q2, kv2, o2, q1, kv1, o1, bias,
+):
+    rows, width = x2.shape
+    mem = mem_full.shape[0]
+    hw = q1.shape[2]
+    heads = bias_line.shape[1]
+    ext = 3 * rows
+    own = width // 8
     half = own // 2
-    rows = tok.shape[0]
-    n = 16
-    any_spec = pl.BlockSpec(memory_space=pl.ANY)
-    vmem = pl.BlockSpec(memory_space=pltpu.VMEM)
+    n = len(CHUNKS)
     dma = pltpu.SemaphoreType.DMA
+
+    def slot(last, a):
+        shape = a.shape[1:]
+        return pl.BlockSpec(
+            (1,) + shape, lambda j: (jnp.clip(last - j, 0, 3),) + (0,) * len(shape)
+        )
+
+    out = [
+        ((rows, width), BF), ((4, own, width), F32), ((rows, width), F32), ((mem // 4, width), F32),
+        ((24, width), F32), ((4, heads, 512), F32),
+    ]
+    shapes = [jax.ShapeDtypeStruct(s, d) for s, d in out]
     return pl.pallas_call(
-        reduce_kernel,
-        name="reduce",
-        in_specs=[any_spec] * 3 + [vmem] * 6,
-        out_specs=[vmem] * 4,
-        out_shape=[
-            jax.ShapeDtypeStruct((4, own, width), F32),
-            jax.ShapeDtypeStruct((rows, width), F32),
-            jax.ShapeDtypeStruct(dm.shape[1:], F32),
-            jax.ShapeDtypeStruct((8, width), F32),
+        backward_kernel,
+        name="backward",
+        grid=(12,),
+        in_specs=[
+            SMEM_SPEC, *[once(a.shape) for a in (x2, cot, x1, mem_full, h2, h1, tokens)],
+            full(gains.shape), full(bias_line.shape), full(seg_q.shape), full(seg_k.shape),
+            pl.BlockSpec(memory_space=pl.ANY),
+            slot(7, q2), slot(7, kv2), slot(7, o2), slot(11, q1), slot(11, kv1), slot(11, o1), slot(11, bias),
         ],
+        out_specs=[*[once(s) for s, _ in out[:5]], slot(11, shapes[5])],
+        out_shape=shapes,
         scratch_shapes=[
-            pltpu.VMEM((n, 4, 1, own, width), BF), pltpu.VMEM((n, 4, 1, own, width), BF),
+            pltpu.VMEM((HELD, 4, 2, own, width), BF), pltpu.VMEM((4, width, width), BF),
+            pltpu.VMEM((ext, width), F32), pltpu.VMEM((rows, width), BF), pltpu.VMEM((rows, width), F32),
+            pltpu.VMEM((rows, hw), BF), pltpu.VMEM((hw, rows), F32), pltpu.VMEM((ext, 2 * hw), BF),
+            pltpu.VMEM((2, 2 * rows + 128, 128), F32), pltpu.VMEM((256, 256), BF),
+            pltpu.VMEM((2, rows, width), BF), pltpu.VMEM((4, mem // 4, width), BF),
+            pltpu.VMEM((n, 4, 1, own, width), BF),
             pltpu.VMEM((n, 2, half, width), BF), pltpu.VMEM((n, 2, half, width), BF),
             pltpu.VMEM((n, half, width), BF), pltpu.VMEM((n, half, width), BF),
-            pltpu.VMEM((n, own, width), BF), pltpu.VMEM((n, own, width), BF),
-            pltpu.VMEM(dx.shape, BF), pltpu.VMEM((3,) + dm.shape[1:], BF),
-            dma((n,)), dma((n,)), dma((n,)),
+            pltpu.VMEM((4, 5, own, width), BF),
+            pltpu.VMEM((2, rows, width), BF), pltpu.VMEM((3, mem // 4, width), BF),
+            dma((4,)), dma((n,)), dma((n,)),
             dma((n, 2)), dma((n, 2)), dma((n, 2)), dma((n, 2)),
             dma((n,)), dma((n,)), dma((n,)), dma((n,)),
-            dma((n,)), dma((n,)), dma((n,)), dma((n,)),
+            dma((n,)), dma((4, 5)),
             dma((2,)), dma((2,)), dma((3,)), dma((3,)),
         ],
         compiler_params=pltpu.CompilerParams(
-            collective_id=1, has_side_effects=True, vmem_limit_bytes=VMEM_LIMIT
+            collective_id=1, has_side_effects=True, vmem_limit_bytes=VMEM_LIMIT, dimension_semantics=("arbitrary",)
         ),
-    )(gf, gc, gs, dx, dm, dh, tok, g1, gains)
+    )(
+        valid_rows, x2, cot, x1, mem_full, h2, h1, tokens, gains, bias_line, seg_q, seg_k,
+        weights, q2, kv2, o2, q1, kv1, o1, bias,
+    )
 
 
 def stats_kernel(
@@ -1062,8 +1101,6 @@
     seg_pad = jnp.concatenate([jnp.full((2 * rows,), -1, jnp.int32), seg])
     seg_k = lax.dynamic_slice_in_dim(seg_pad, z * rows, ext, 0).reshape(ext, 1)
 
-    sq = (width, width)
-    vm = pltpu.VMEM
     half = width // 16
     weights, x1, h1, q1, kv1, o1, bias, mem_full, x2, h2, q2, kv2, o2 = forward(
         valid_rows, tokens, memory[0], norm_gains, bias_line, seg_q, seg_k,
@@ -1072,53 +1109,16 @@
     )
     weights = weights.reshape(4, 4, width, width)
     mem_full = mem_full.reshape(mem_len, width)
-    output, g2, grad_f, gain3 = grid_call(
-        ffn_kernel, "ffn",
-        [full((rows, width)), full((rows, width)), full((3, width)), weight(2, sq), weight(3, sq)],
-        [((rows, width), BF, full((rows, width))), ((rows, width), F32, full((rows, width))),
-         ((4, 2, width, width), BF, slot((2, width, width))), ((8, width), F32, full((8, width)))],
-        [vm((rows, width), BF), vm((rows, width), F32), vm((rows, width), F32)],
-        (x2, cotangent, norm_gains, weights, weights),
-        8_000_000_000,
-    )
-    grad_c, g1, dmem, gain2 = grid_call(
-        cross_bwd_kernel, "cross_bwd",
-        [SMEM_SPEC, full((rows, width)), full((rows, width)), full((3, width)), weight(1, sq),
-         full((mem_len, width)), full((rows, width)), slot((rows, hw)), slot((mem_len, 2 * hw)), slot((rows, hw))],
-        [((4, width, width), BF, slot((width, width))), ((rows, width), F32, full((rows, width))),
-         ((mem_len, width), BF, full((mem_len, width))), ((8, width), F32, full((8, width)))],
-        [vm((rows, width), BF), vm((rows, width), F32), vm((mem_len, width), F32)],
-        (valid_rows, g2, x1, norm_gains, weights, mem_full, h2, q2, kv2, o2),
-        6_000_000_000,
-    )
-    grad_s, dh1, dx, rel = grid_call(
-        self_bwd_kernel, "self_bwd",
-        [full((rows, width)), full((3, width)), weight(0, sq), full((ext, width)),
-         slot((rows, hw)), slot((ext, 2 * hw)), slot((rows, hw)), slot((heads, 256, 128)),
-         slot((heads, 512)), full((1, rows)), full((ext, 1))],
-        [((4, width, width), BF, slot((width, width))), ((rows, width), F32, full((rows, width))),
-         ((2, rows, width), BF, full((2, rows, width))), ((4, heads, 512), F32, slot((heads, 512)))],
-        [vm((2, span, 128), F32), vm((rows, width), BF), vm((256, 256), BF), vm((ext, width), F32)],
-        (g1, norm_gains, weights, h1, q1, kv1, o1, bias, bias_line, seg_q, seg_k),
-        8_000_000_000,
-    )
-
-    def by_owner(g):
-        lead = g.shape[:-2]
-        if groups > 1:
-            g = g.reshape(lead + (groups, 8, eighth // groups, width))
-            g = jnp.swapaxes(g, -4, -3)
-        return g.reshape(lead + (4, 2, eighth, width))
-
-    final, tokens_grad, memory_grad, gain1 = reduce_grads(
-        by_owner(grad_f), by_owner(grad_c), by_owner(grad_s), dx, dmem.reshape(4, mem_own, width),
-        dh1, tokens, g1, norm_gains,
+    output, final, tokens_grad, memory_grad, gain_sums, rel = backward(
+        valid_rows, x2, cotangent, x1, mem_full, h2, h1, tokens, norm_gains, bias_line, seg_q, seg_k,
+        weights, q2, kv2, o2, q1, kv1, o1, bias,
     )
     if groups > 1:
-        final = lax.psum_scatter(
-            final, "wide", scatter_dimension=1, tiled=True,
-            axis_index_groups=[[s + 8 * g for g in range(groups)] for s in range(8)],
+        w = lax.axis_index("wide")
+        mine = lax.dynamic_update_slice_in_dim(
+            jnp.zeros((4, width, width), F32), final, lax.rem(w, 8) * eighth, 1
         )
+        final = lax.psum_scatter(mine, "wide", scatter_dimension=1, tiled=True)
     own = final.shape[1]
 
     rel_pick = jnp.asarray(
@@ -1128,7 +1128,7 @@
     rel = jnp.take(rel, places[z], axis=0)
     rel = jnp.einsum("hl,lb->bh", rel.reshape(4 * heads, 512), rel_pick, precision=lax.Precision.HIGHEST)
     rel_row = jnp.pad(rel.reshape(1, -1), ((0, 0), (0, width - BUCKETS * 4 * heads)))
-    small = jnp.concatenate([gain1[:1], gain2[:1], gain3[:1], rel_row, jnp.zeros((4, width), F32)], 0)
+    small = jnp.concatenate([gain_sums[::8], rel_row, jnp.zeros((4, width), F32)], 0)
     rsum, csum, asum, prow, pcol = reduce_stats(wide_count, final, small)
 
     def split(g):

time: 331 us -> 280 us (0.85)
  Pallas kernels: 296 us -> 246 us
    pallas_call x4 -> x1, Pallas kernels: 182 us -> 131 us  [backward(): pl.pallas_call(backward_kernel, name='backward', grid=(12,), in_specs=[SM...]
    unnamed x17 -> x18, local copies, waits for them, and re-layouts: 6.43 us -> 7.2 us
where the time goes in v3:
time: 280 us
  Pallas kernels  246 us (88%)
  local copies, waits for them, and re-layouts  18.1 us (6%)
  other arithmetic  11.3 us (4%)
    pallas_call x1, Pallas kernels, backward(): pl.pallas_call(backward_kernel, name='backward', grid=(12,), in_specs=[SM...  131 us
    pallas_call x1, Pallas kernels, forward(): pl.pallas_call(forward_kernel, name='forward', grid=(8,), in_specs=[SMEM_...  101 us
    pallas_call x1, Pallas kernels, reduce_stats(): pl.pallas_call(functools.partial(stats_kernel, wide_count), name='stats',...  13.5 us
    unnamed x18, local copies, waits for them, and re-layouts  7.2 us

profile of v3, /device:TPU:0, one launch (start us, length us, event | category | flops | bytes accessed | tf_op | source)
XLA Modules:
  0.0 279.5 jit_solution(14105228963438493021)
XLA Ops:
  0.6 1.2 compare_and_fusion
  1.9 1.0 convolution_bitcast_fusion
  3.5 0.7 broadcast_select_fusion.1.bd_ref
  4.2 0.8 pad_dynamic-slice_fusion
  5.0 0.9 reshape.105.segk_ref
  5.9 1.2 constant_dynamic-slice_fusion.1.segq_ref
  7.8 2.6 copy.31
  10.3 1.5 copy.32
  11.9 101.5 %forward.1 = (bf16[4,4,16,48,768]{4,3,2,1,0:T(8,128)(2,1)}, f32[256,768]{1,0:T(8,128)}, bf16[768,768]{1,0:T(8,128)(2,1)}, bf16[4,256,192]{2,1,0:T(8,128)(2,1)}, ...) custom-call(s32[1]{0:T(128)S(6)} %copy.43.valid_ref, ...), custom_call_target="tpu_custom_call" | custom-call | tf_op jit(solution)/shard_map/forward/pallas_call | solution.py:452
  113.4 131.2 %backward.1 = (bf16[256,768]{1,0:T(8,128)(2,1)}, f32[4,96,768]{2,1,0:T(8,128)}, f32[256,768]{1,0:T(8,128)}, f32[128,768]{1,0:T(8,128)}, f32[24,768]{1,0:T(8,128)}, /*index=5*/f32[4,3,512]{2,1,0:T(4,128)}) custom-call(s32[1]{0:T(128)S(6)} %copy.43.valid_ref, f32[256,768]{1,0:T(8,128)} %get-tuple-element.38.x2_ref, bf16[256,768]{1,0:T(8,128)(2,1)} %cot_ref.1, ...), custom_call_target="tpu_custom_call" | custom-call | tf_op jit(solution)/shard_map/backward/pallas_call | solution.py:885
  244.6 0.8 pad_clamp_fusion
  245.4 1.3 gather_fusion.1
  246.7 0.7 broadcast_select_fusion
  247.4 1.5 fusion.8
  249.1 0.9 slice.102
  250.1 0.7 fusion.1.a_ref
  250.8 13.5 %stats.1 = (f32[24,128]{1,0:T(8,128)}, f32[8,768]{1,0:T(8,128)}, f32[8,768]{1,0:T(8,128)}, f32[8,8,128]{2,1,0:T(8,128)}, f32[4,8,768]{2,1,0:T(8,128)}) custom-call(f32[4,96,768]{2,1,0:T(8,128)} %get-tuple-element.54.f_ref, f32[8,768]{1,0:T(8,128)} %fusion.1.a_ref), custom_call_target="tpu_custom_call" | custom-call | tf_op jit(solution)/shard_map/stats/pallas_call | solution.py:1050
  264.2 0.8 slice_reduce_fusion.1
  265.7 0.8 multiply_bitcast_fusion.1
  266.5 0.9 multiply_bitcast_fusion
  267.5 0.6 pad_maximum_fusion.4
  268.1 0.9 fusion.5
  269.7 0.7 fusion.7
  270.4 0.7 fusion.6
  271.8 0.9 pad_maximum_fusion
  272.8 0.8 pad_maximum_fusion.2
  273.7 0.8 pad_maximum_fusion.1
  274.6 0.7 copy.38
  275.9 1.3 slice_multiply_fusion.1
  277.2 0.7 copy.44
  277.9 0.9 copy.45
  278.8 0.7 copy.46
  (36 shorter events, 3.9 us)
Async XLA Ops:
  4.9 5.4 %copy-start.1 = (bf16[4,768,192]{1,2,0:T(8,128)(2,1)S(1)}, bf16[4,768,192]{1,2,0:T(8,128)(2,1)}, u32[]{:S(2)}) copy-start(bf16[4,768,192]{1,2,0:T(8,128)(2,1)} %param.23) | copy-start | bytes 3538948
  244.6 27.1 %copy-start = (f32[4,96,768]{2,1,0:T(8,128)S(1)}, f32[4,96,768]{2,1,0:T(8,128)}, u32[]{:S(2)}) copy-start(f32[4,96,768]{2,1,0:T(8,128)} %get-tuple-element.54.f_ref) | copy-start | bytes 3538948
  272.7 1.8 copy-start.5
  272.7 4.5 %copy-start.4 = (bf16[256,768]{1,0:T(8,128)(2,1)S(1)}, bf16[256,768]{1,0:T(8,128)(2,1)}, u32[]{:S(2)}) copy-start(bf16[256,768]{1,0:T(8,128)(2,1)} %get-tuple-element.134) | copy-start | bytes 1179652
  272.8 5.1 %copy-start.2 = (f32[256,768]{1,0:T(8,128)S(1)}, f32[256,768]{1,0:T(8,128)}, u32[]{:S(2)}) copy-start(f32[256,768]{1,0:T(8,128)} %get-tuple-element.135) | copy-start | bytes 2359300
  273.7 5.1 %copy-start.3 = (f32[128,768]{1,0:T(8,128)S(1)}, f32[128,768]{1,0:T(8,128)}, u32[]{:S(2)}) copy-start(f32[128,768]{1,0:T(8,128)} %get-tuple-element.53) | copy-start | bytes 1179652

commit v4 on v3

--- a/solution.py
+++ b/solution.py
@@ -64,13 +64,20 @@
     return e * (1.0 / jnp.sum(e, axis=0, keepdims=True))
 
 
-def self_mask_store(mask_ref, segk_ref, segq_ref, rows, span):
+def self_mask_store(mask_ref, seg_ref, z, rows, span):
+    def quarter(k):
+        out = jnp.full((1, rows), -1, jnp.int32)
+        for kk in range(4):
+            out = jnp.where(k == kk, seg_ref[:, kk * rows : (kk + 1) * rows], out)
+        return out.astype(F32)
+
+    own = quarter(z)
+    keys = jnp.concatenate([quarter(z - 2), quarter(z - 1), own], axis=1)
+    keys = jnp.broadcast_to(keys, (128, 3 * rows)).T
     for b in range(2):
         r = lax.broadcasted_iota(jnp.int32, (span, 128), 0)
         c = lax.broadcasted_iota(jnp.int32, (span, 128), 1)
-        allowed = (c + 2 * rows >= r) & (
-            segk_ref[b * 128 : b * 128 + span, :] == segq_ref[:, b * 128 : b * 128 + 128]
-        )
+        allowed = (c + 2 * rows >= r) & (keys[b * 128 : b * 128 + span] == own[:, b * 128 : b * 128 + 128])
         mask_ref[b] = jnp.where(allowed, 1.0, 0.0)
 
 
@@ -101,6 +108,15 @@
         self.sx, self.sy, self.sxy = s + dx, s + dy, s + dx + dy
         self.dc = dc
 
+    def quarter(self, k):
+        z = self.z
+        e0, e3 = 1 - (z + 3) // 4, z // 3
+        e1, e2 = (1 - z // 2) * lax.rem(z, 2), (z // 2) * (1 - lax.rem(z, 2))
+        return sum(e * row[k] for e, row in zip((e0, e1, e2, e3), RANKS))
+
+    def quarter_of(self, slot):
+        return sum(jnp.where(slot == k, self.quarter(k), 0) for k in range(4))
+
     def narrow_dev(self, k):
         return {"narrow": lax.rem(self.z + k, 4)}
 
@@ -129,9 +145,9 @@
 
 
 def forward_kernel(
-    valid_ref, tok_ref, mem_ref, gain_ref, bd_ref, segq_ref, segk_ref, ws_ref, wc_ref, wf_ref,
-    w_ref, x1_ref, h1_ref, q_ref, kv_ref, o_ref, bias_ref, mfull_ref, x2_ref, h2_ref, q2_ref, kv2_ref, o2_ref,
-    wv, raw, xt, mt, mask_ref, zs, zr, ps, pr, ts, tr, ms, mr, ls, fs, os_,
+    valid_ref, tok_ref, mem_ref, gain_ref, rel_ref, pick_ref, seg_ref, ws_ref, wc_ref, wf_ref,
+    w_ref, bd_ref, x1_ref, h1_ref, q_ref, kv_ref, o_ref, bias_ref, mfull_ref, x2_ref, h2_ref, q2_ref, kv2_ref, o2_ref,
+    wv, lines, xt, mt, mask_ref, zs, zr, ps, pr, ts, tr, ms, mr, ls, fs, os_,
 ):
     at = Place()
     z, s = at.z, at.s
@@ -144,6 +160,7 @@
     fw = wf_ref.shape[3]
     heads = hw // 64
     part = rows // 4
+    half = width // 16
     mine = pl.ds(2 * s, 2)
 
     def edge(k):
@@ -263,9 +280,12 @@
             arrived(u, r, kind)
         keep(u, r).start()
 
-    def load_raw(i):
+    def attn_loads(i):
         src = (ws_ref, wc_ref)[i]
-        return pltpu.make_async_copy(src, raw.at[i], ls.at[i])
+        return [
+            pltpu.make_async_copy(src.at[part], wv.at[i, 0, pl.ds(4 * k, 4)], ls.at[i, k])
+            for k, part in enumerate((0, 3, 1, 2))
+        ]
 
     def ffn_loads():
         cut = width - fw
@@ -276,22 +296,18 @@
             pltpu.make_async_copy(wf_ref.at[2], wv.at[3, 0, :, :, fw - cut : width], fs.at[3]),
         ]
 
-    def pack(i):
-        load_raw(i).wait()
-        for b in range(16):
-            wv[i, 0, b] = jnp.concatenate([raw[i, 0, b], raw[i, 3, b], raw[i, 1, b], raw[i, 2, b]], axis=1)
-
     @pl.when(j == 0)
     def _():
-        load_raw(0).start()
-        load_raw(1).start()
-        for copy in ffn_loads():
+        at.signal_all()
+        for copy in attn_loads(0) + attn_loads(1) + ffn_loads():
             copy.start()
-        at.barrier()
-        pack(0)
+        at.wait_all()
+        for copy in attn_loads(0):
+            copy.wait()
         own_sends(0, lambda copy: copy.start())
         tok_send(1, (0, 1))
-        pack(1)
+        for copy in attn_loads(1):
+            copy.wait()
         own_sends(1, lambda copy: copy.start())
         for copy in ffn_loads():
             copy.wait()
@@ -300,7 +316,15 @@
         x = tok_ref[...].astype(F32)
         x1_ref[...] = x
         h1_ref[2 * rows : ext, :] = (x * inv_rms(x) * gain_ref[0:1, :]).astype(BF)
-        self_mask_store(mask_ref, segk_ref, segq_ref, rows, span)
+        self_mask_store(mask_ref, seg_ref, z, rows, span)
+        lines[...] = lax.dot_general(
+            rel_ref[...], pick_ref[...], (((1,), (0,)), ((), ())),
+            preferred_element_type=F32, precision=lax.Precision.HIGHEST,
+        )
+        for k in range(4):
+            first = at.quarter(k) * heads
+            for hh in range(heads):
+                bd_ref[k, hh : hh + 1, :] = lines[pl.ds(first + hh, 1), :]
         step0(0)
         step0(1)
         step1(0)
@@ -335,13 +359,13 @@
                     step2(t - 2)
 
     def flat(u, k, lo, hi):
-        return wv[u, k, :, :, lo:hi].reshape(width, hi - lo)
+        return wv[u, k, lo // half : hi // half].reshape(hi - lo, width)
 
     @pl.when(j < 4)
     def _():
         hook(0, 0, 4)
-        q = mm(h1_ref[2 * rows : ext, :], flat(0, j, 0, hw)).astype(BF)
-        kv = mm(h1_ref[...], flat(0, j, 2 * hw, 4 * hw)).astype(BF)
+        q = mm_nt(h1_ref[2 * rows : ext, :], flat(0, j, 0, hw)).astype(BF)
+        kv = mm_nt(h1_ref[...], flat(0, j, 2 * hw, 4 * hw)).astype(BF)
         q_ref[0] = q
         kv_ref[0] = kv
         parts = []
@@ -364,7 +388,7 @@
                 hook(1 + hh, 0, 4)
         o = jnp.concatenate(parts, axis=0).T.astype(BF)
         o_ref[0] = o
-        x1_ref[...] += mm_nt(o, flat(0, j, hw, 2 * hw))
+        x1_ref[...] += mm(o, flat(0, j, hw, 2 * hw))
 
     @pl.when(j == 4)
     def _():
@@ -381,8 +405,8 @@
     def _():
         hook(0, 4, 8)
         mem = mfull_ref.shape[0] * mfull_ref.shape[1]
-        q = mm(h2_ref[...], flat(1, j - 4, 0, hw)).astype(BF)
-        kv = mm(mfull_ref[...].reshape(mem, width), flat(1, j - 4, 2 * hw, 4 * hw)).astype(BF)
+        q = mm_nt(h2_ref[...], flat(1, j - 4, 0, hw)).astype(BF)
+        kv = mm_nt(mfull_ref[...].reshape(mem, width), flat(1, j - 4, 2 * hw, 4 * hw)).astype(BF)
         q2_ref[0] = q
         kv2_ref[0] = kv
         allowed = lax.broadcasted_iota(jnp.int32, (mem, rows), 0) < valid_ref[0]
@@ -396,7 +420,7 @@
                 hook(1 + hh, 4, 8)
         o = jnp.concatenate(parts, axis=0).T.astype(BF)
         o2_ref[0] = o
-        x2_ref[...] += mm_nt(o, flat(1, j - 4, hw, 2 * hw))
+        x2_ref[...] += mm(o, flat(1, j - 4, hw, 2 * hw))
 
     @pl.when(j == 7)
     def _():
@@ -422,10 +446,10 @@
             mem_copy(k).wait_send()
 
 
-def forward(valid_rows, tokens, memory, gains, bias_line, seg_q, seg_k, ws, wc, wf):
+def forward(valid_rows, tokens, memory, gains, rel, pick, seg, ws, wc, wf):
     rows, width = tokens.shape
     mem_own = memory.shape[0]
-    hw = ws.shape[3]
+    hw = 4 * ws.shape[2]
     heads = hw // 64
     ext = 3 * rows
     mem = 4 * mem_own
@@ -440,7 +464,7 @@
         return pl.BlockSpec((1,) + shape, lambda j: (jnp.maximum(j - 4, 0),) + (0,) * len(shape))
 
     out = [
-        ((4, 4, 16, half, width), BF, any_spec),
+        ((4, 4, 16, half, width), BF, any_spec), ((4, heads, 512), F32, full((4, heads, 512))),
         ((rows, width), F32, full((rows, width))), ((ext, width), BF, full((ext, width))),
         ((4, rows, hw), BF, early((rows, hw))), ((4, ext, 2 * hw), BF, early((ext, 2 * hw))),
         ((4, rows, hw), BF, early((rows, hw))), ((4, heads, 256, 128), F32, early((heads, 256, 128))),
@@ -454,22 +478,22 @@
         name="forward",
         grid=(8,),
         in_specs=[
-            SMEM_SPEC, full((rows, width)), full((mem_own, width)), full((3, width)), full((4, heads, 512)),
-            full((1, rows)), full((ext, 1)), any_spec, any_spec, any_spec,
+            SMEM_SPEC, full((rows, width)), full((mem_own, width)), full((3, width)),
+            full(rel.shape), full(pick.shape), full(seg.shape), any_spec, any_spec, any_spec,
         ],
         out_specs=[spec for _, _, spec in out],
         out_shape=[jax.ShapeDtypeStruct(shape, dtype) for shape, dtype, _ in out],
         scratch_shapes=[
-            pltpu.VMEM((4, 4, 16, half, width), BF), pltpu.VMEM((2,) + ws.shape, BF),
+            pltpu.VMEM((4, 4, 16, half, width), BF), pltpu.VMEM((4 * heads, 512), F32),
             pltpu.VMEM((2, rows, width), BF), pltpu.VMEM((4, mem_own, width), BF),
             pltpu.VMEM((2, 2 * rows + 128, 128), F32),
             dma((4, 5)), dma((4, 4)), dma((12, 10)), dma((12, 10)),
-            dma((2, 4)), dma((2, 4)), dma((3,)), dma((3,)), dma((2,)), dma((4,)), dma((4, 4)),
+            dma((2, 4)), dma((2, 4)), dma((3,)), dma((3,)), dma((2, 4)), dma((4,)), dma((4, 4)),
         ],
         compiler_params=pltpu.CompilerParams(
             collective_id=0, has_side_effects=True, vmem_limit_bytes=VMEM_LIMIT, dimension_semantics=("arbitrary",)
         ),
-    )(valid_rows, tokens, memory, gains, bias_line, seg_q, seg_k, ws, wc, wf)
+    )(valid_rows, tokens, memory, gains, rel, pick, seg, ws, wc, wf)
 
 
 CHUNKS = [(2 + i % 2, i // 2) for i in range(8)] + [(1, i) for i in range(4)] + [(0, i) for i in range(4)]
@@ -478,10 +502,10 @@
 
 
 def backward_kernel(
-    valid_ref, x2_ref, cot_ref, x1_ref, mem_ref, h2_ref, h1_ref, tok_ref, gain_ref, bd_ref, segq_ref, segk_ref,
+    valid_ref, x2_ref, cot_ref, x1_ref, mem_ref, h2_ref, h1_ref, tok_ref, gain_ref, bd_ref, seg_ref, pick_ref,
     w_ref, q2_ref, kv2_ref, o2_ref, q1_ref, kv1_ref, o1_ref, bias_ref,
-    out_ref, f_ref, tg_ref, mg_ref, gsum_ref, rel_ref,
-    g, wbuf, acc, act_in, res, do_ref, dqt_ref, dkv_ref, mask_ref, flip_ref, dxo, dmo, rc, xr, yr, xr2, yr2, zb, dxr, dmr,
+    out_ref, f_ref, tg_ref, mg_ref, small_ref,
+    g, wbuf, acc, act_in, res, gsum_ref, rel_ref, do_ref, dqt_ref, dkv_ref, mask_ref, flip_ref, dxo, dmo, rc, xr, yr, xr2, yr2, zb, dxr, dmr,
     wsem, cs, cr, xs, xrs, ys, yrs, x2s, x2r, y2s, y2r, zs, zr, dxs, dxrs, dms, dmrs,
 ):
     at = Place()
@@ -705,7 +729,7 @@
         def _():
             w_load(0, 3, 0).start()
 
-        do_ref[...] = mm(act_in[...], wbuf[k0, :, hw : 2 * hw]).astype(BF)
+        do_ref[...] = mm_nt(act_in[...], wbuf[k0, hw : 2 * hw, :]).astype(BF)
         for hh in range(heads):
             h_cols, v_cols = slice(hh * 64, hh * 64 + 64), slice(hw + hh * 64, hw + hh * 64 + 64)
             k = kv2_ref[0, :, h_cols]
@@ -735,8 +759,8 @@
             @pl.when(j == jj)
             def _():
                 core_send(4 + jj).start()
-        acc[0:rows, :] += mm_nt(dq, wbuf[k0, :, 0:hw])
-        acc[rows : rows + mem, :] += mm_nt(dkv, wbuf[k0, :, 2 * hw : 4 * hw])
+        acc[0:rows, :] += mm(dq, wbuf[k0, 0:hw, :])
+        acc[rows : rows + mem, :] += mm(dkv, wbuf[k0, 2 * hw : 4 * hw, :])
 
     @pl.when(j == 7)
     def _():
@@ -750,7 +774,8 @@
         res[...] = g1
         act_in[...] = g1.astype(BF)
         acc[...] = jnp.zeros_like(acc)
-        self_mask_store(mask_ref, segk_ref, segq_ref, rows, span)
+        self_mask_store(mask_ref, seg_ref, z, rows, span)
+        rel_ref[...] = jnp.zeros_like(rel_ref)
         r = lax.broadcasted_iota(jnp.int32, (256, 256), 0)
         c = lax.broadcasted_iota(jnp.int32, (256, 256), 1)
         flip_ref[...] = jnp.where(r + c == 255, 1.0, 0.0).astype(BF)
@@ -764,7 +789,7 @@
         def _():
             w_load(0, 10 - j, k0 + 1).start()
 
-        do_ref[...] = mm(act_in[...], wbuf[k0, :, hw : 2 * hw]).astype(BF)
+        do_ref[...] = mm_nt(act_in[...], wbuf[k0, hw : 2 * hw, :]).astype(BF)
         for hh in range(heads):
             h_cols, v_cols = slice(hh * 64, hh * 64 + 64), slice(hw + hh * 64, hw + hh * 64 + 64)
             far = bd_ref[11 - j, hh : hh + 1, 127:128]
@@ -798,7 +823,7 @@
             line = jnp.sum(aligned, axis=0, keepdims=True)
             lane = lax.broadcasted_iota(jnp.int32, (1, 512), 1)
             far_sum = jnp.sum(total, axis=1, keepdims=True)
-            rel_ref[0, hh : hh + 1, :] = jnp.where(lane == 511, far_sum, line)
+            rel_ref[pl.ds(at.quarter_of(11 - j) * heads + hh, 1), :] = jnp.where(lane == 511, far_sum, line)
             hook(hh, 8, 12)
         da = act_in[...]
         dq = dqt_ref[...].T.astype(BF)
@@ -819,8 +844,8 @@
             @pl.when(j == jj)
             def _():
                 core_send(4 + jj).start()
-        acc[...] += mm_nt(dkv, wbuf[k0, :, 2 * hw : 4 * hw])
-        acc[2 * rows : ext, :] += mm_nt(dq, wbuf[k0, :, 0:hw])
+        acc[...] += mm(dkv, wbuf[k0, 2 * hw : 4 * hw, :])
+        acc[2 * rows : ext, :] += mm(dq, wbuf[k0, 0:hw, :])
 
     @pl.when(j == 11)
     def _():
@@ -845,7 +870,12 @@
                         dx_send(k).wait_recv()
                         acc[2 * rows : ext, :] += dxr[k].astype(F32)
                 gain_part, dv = norm_back(tok_ref[...].astype(F32), gain_ref[0:1, :], acc[2 * rows : ext, :])
-                gsum_ref[0:8, :] = jnp.broadcast_to(gain_part, (8, width))
+                rel = lax.dot_general(
+                    rel_ref[...], pick_ref[...], (((1,), (0,)), ((), ())),
+                    preferred_element_type=F32, precision=lax.Precision.HIGHEST,
+                )
+                gains = [gain_part, gsum_ref[8:9, :], gsum_ref[16:17, :], jnp.zeros((5, width), F32)]
+                small_ref[...] = jnp.concatenate([jnp.concatenate(gains, axis=0), rel[0:8], rel[8:16]], axis=1)
                 tg_ref[...] = res[...] + dv
         for i in range(n - HELD, n):
             sent(i)
@@ -858,13 +888,12 @@
 
 
 def backward(
-    valid_rows, x2, cot, x1, mem_full, h2, h1, tokens, gains, bias_line, seg_q, seg_k,
+    valid_rows, x2, cot, x1, mem_full, h2, h1, tokens, gains, bias_line, seg, pick,
     weights, q2, kv2, o2, q1, kv1, o1, bias,
 ):
     rows, width = x2.shape
     mem = mem_full.shape[0]
     hw = q1.shape[2]
-    heads = bias_line.shape[1]
     ext = 3 * rows
     own = width // 8
     half = own // 2
@@ -879,7 +908,7 @@
 
     out = [
         ((rows, width), BF), ((4, own, width), F32), ((rows, width), F32), ((mem // 4, width), F32),
-        ((24, width), F32), ((4, heads, 512), F32),
+        ((8, width + 256), F32),
     ]
     shapes = [jax.ShapeDtypeStruct(s, d) for s, d in out]
     return pl.pallas_call(
@@ -888,15 +917,16 @@
         grid=(12,),
         in_specs=[
             SMEM_SPEC, *[once(a.shape) for a in (x2, cot, x1, mem_full, h2, h1, tokens)],
-            full(gains.shape), full(bias_line.shape), full(seg_q.shape), full(seg_k.shape),
+            full(gains.shape), full(bias_line.shape), full(seg.shape), full(pick.shape),
             pl.BlockSpec(memory_space=pl.ANY),
             slot(7, q2), slot(7, kv2), slot(7, o2), slot(11, q1), slot(11, kv1), slot(11, o1), slot(11, bias),
         ],
-        out_specs=[*[once(s) for s, _ in out[:5]], slot(11, shapes[5])],
+        out_specs=[once(s) for s, _ in out],
         out_shape=shapes,
         scratch_shapes=[
             pltpu.VMEM((HELD, 4, 2, own, width), BF), pltpu.VMEM((4, width, width), BF),
             pltpu.VMEM((ext, width), F32), pltpu.VMEM((rows, width), BF), pltpu.VMEM((rows, width), F32),
+            pltpu.VMEM((24, width), F32), pltpu.VMEM((16, 512), F32),
             pltpu.VMEM((rows, hw), BF), pltpu.VMEM((hw, rows), F32), pltpu.VMEM((ext, 2 * hw), BF),
             pltpu.VMEM((2, 2 * rows + 128, 128), F32), pltpu.VMEM((256, 256), BF),
             pltpu.VMEM((2, rows, width), BF), pltpu.VMEM((4, mem // 4, width), BF),
@@ -915,14 +945,14 @@
             collective_id=1, has_side_effects=True, vmem_limit_bytes=VMEM_LIMIT, dimension_semantics=("arbitrary",)
         ),
     )(
-        valid_rows, x2, cot, x1, mem_full, h2, h1, tokens, gains, bias_line, seg_q, seg_k,
+        valid_rows, x2, cot, x1, mem_full, h2, h1, tokens, gains, bias_line, seg, pick,
         weights, q2, kv2, o2, q1, kv1, o1, bias,
     )
 
 
 def stats_kernel(
     wide_count, f_ref, a_ref,
-    rsum_ref, csum_ref, asum_ref, prow_ref, pcol_ref,
+    rsum_ref, csum_ref, asum_ref, pcol_ref,
     rall, aall, call, ball, rs, rr, as_, ar, cs, cr, bs, br, ps, pr,
 ):
     w = lax.axis_index("wide")
@@ -998,16 +1028,19 @@
     rsum = rall[0] + rall[1] + rall[2] + rall[3]
     rsum_ref[...] = rsum
     asum = aall[0] + aall[1] + aall[2] + aall[3]
-    zero = jnp.zeros((1, width - 128), F32)
-    ball[w] = jnp.concatenate(
+    zero = jnp.zeros((8, width - 128), F32)
+    rows = jnp.concatenate([rsum[0:8], zero], axis=1)
+    more = jnp.concatenate([rsum[8:16], zero], axis=1)
+    shift = own * w
+    left = jnp.concatenate(
         [
-            asum[0:4],
-            jnp.concatenate([rsum[1:2], zero], axis=1),
-            jnp.concatenate([rsum[9:10], zero], axis=1),
-            jnp.zeros((2, width), F32),
+            asum[0:3, 0:width],
+            pltpu.roll(rows, shift, 1)[1:2], pltpu.roll(more, shift, 1)[1:2],
+            jnp.zeros((3, width), F32),
         ],
         axis=0,
     )
+    ball[w] = jnp.concatenate([left, asum[:, width:]], axis=1)
     wide_loop(lambda k: b_send(k).start())
 
     def c_wait(k):
@@ -1027,7 +1060,6 @@
 
     wide_loop(b_wait)
     asum_ref[...] = lax.fori_loop(1, wide_count, lambda i, v: v + ball[i], ball[0])
-    prow_ref[...] = ball[:, :, 0:128]
     for k in (1, 2, 3):
         frm = lax.rem(z + 4 - k, 4)
         remote(pcol_ref.at[frm], pcol_ref.at[frm], ps.at[k - 1], pr.at[k - 1], peer(k)).wait_recv()
@@ -1051,17 +1083,16 @@
         functools.partial(stats_kernel, wide_count),
         name="stats",
         in_specs=[vmem] * 2,
-        out_specs=[vmem] * 5,
+        out_specs=[vmem] * 4,
         out_shape=[
             jax.ShapeDtypeStruct((24, 128), F32),
             jax.ShapeDtypeStruct((8, width), F32),
-            jax.ShapeDtypeStruct((8, width), F32),
-            jax.ShapeDtypeStruct((wide_count, 8, 128), F32),
+            jax.ShapeDtypeStruct(small.shape, F32),
             jax.ShapeDtypeStruct((4, 8, width), F32),
         ],
         scratch_shapes=[
-            pltpu.VMEM((4, 24, 128), F32), pltpu.VMEM((4, 8, width), F32),
-            pltpu.VMEM((wide_count, 8, width), F32), pltpu.VMEM((wide_count, 8, width), F32),
+            pltpu.VMEM((4, 24, 128), F32), pltpu.VMEM((4,) + small.shape, F32),
+            pltpu.VMEM((wide_count, 8, width), F32), pltpu.VMEM((wide_count,) + small.shape, F32),
             dma((3,)), dma((3,)), dma((3,)), dma((3,)),
             dma((wide_count - 1,)), dma((wide_count - 1,)), dma((wide_count - 1,)), dma((wide_count - 1,)),
             dma((3,)), dma((3,)),
@@ -1070,21 +1101,68 @@
     )(final, small)
 
 
+def finish_kernel(
+    out_ref, tg_ref, mg_ref, f_ref, rsum_ref, csum_ref, asum_ref, pcol_ref,
+    out_o, tg_o, mg_o, gains_o, rel_o, self_o, cross_o, ffn_o, arow_o, acol_o, proj_o, frow_o, fcol_o,
+):
+    own, width = f_ref.shape[1:]
+    hw = self_o.shape[2]
+    fw = ffn_o.shape[2]
+    out_o[...] = out_ref[...]
+    tg_o[...] = tg_ref[...]
+    mg_o[...] = mg_ref[...]
+    gains_o[...] = asum_ref[0:3, 0:width]
+    rel = jnp.concatenate([asum_ref[:, width : width + 128], asum_ref[:, width + 128 : width + 256]], axis=0)
+    rel_o[...] = rel[0 : rel_o.shape[0], 0 : rel_o.shape[1]]
+    for ref, i in ((self_o, 0), (cross_o, 1)):
+        for m, part in enumerate((0, 2, 3, 1)):
+            ref[m] = f_ref[i, :, part * hw : (part + 1) * hw]
+    cut = width - fw
+    ffn_o[0] = f_ref[2, :, 0:fw]
+    ffn_o[1, :, 0:cut] = f_ref[2, :, fw:width]
+    ffn_o[1, :, cut:fw] = f_ref[3, :, 0 : fw - cut]
+    ffn_o[2] = f_ref[3, :, fw - cut : width]
+    rsum = rsum_ref[...]
+    arow = jnp.concatenate([rsum[0:1], rsum[2:4], rsum[8:9], rsum[10:12]], axis=0)
+    arow_o[...] = arow[:, 0:own] * (1.0 / width)
+    frow_o[...] = rsum[16:19, 0:own] * (1.0 / (4 * fw))
+    scale = 1.0 / width
+    for i in range(2):
+        for m, part in enumerate((0, 2, 3)):
+            acol_o[3 * i + m : 3 * i + m + 1, :] = csum_ref[i : i + 1, part * hw : (part + 1) * hw] * scale
+    fcol_o[0:1, :] = csum_ref[2:3, 0:fw] * scale
+    fcol_o[1:2, 0:cut] = csum_ref[2:3, fw:width] * scale
+    fcol_o[1:2, cut:fw] = csum_ref[3:4, 0 : fw - cut] * scale
+    fcol_o[2:3, :] = csum_ref[3:4, fw - cut : width] * scale
+    for i in range(2):
+        cols = jnp.concatenate([pcol_ref[k, i : i + 1, hw : 2 * hw] for k in range(4)], axis=1)
+        proj_o[i : i + 1, 0:width] = asum_ref[3 + i : 4 + i, 0:width] * scale
+        proj_o[i : i + 1, width : 2 * width] = cols * scale
+
+
+def finish(shapes, *args):
+    vmem = pl.BlockSpec(memory_space=pltpu.VMEM)
+    return pl.pallas_call(
+        finish_kernel,
+        name="finish",
+        in_specs=[vmem] * len(args),
+        out_specs=[vmem] * len(shapes),
+        out_shape=[jax.ShapeDtypeStruct(s, d) for s, d in shapes],
+    )(*args)
+
+
 def local(
     tokens, memory, segments, valid_rows, norm_gains, rel_table,
     self_weights, cross_weights, ffn_weights, cotangent,
 ):
     wide_count = lax.axis_size("wide")
     assert lax.axis_size("narrow") == 4 and wide_count % 8 == 0 and segments.shape[0] == 1
-    z = lax.axis_index("narrow")
     rows, width = tokens.shape
     mem_own = memory.shape[1]
     mem_len = 4 * mem_own
     hw = self_weights.shape[2]
     fw = ffn_weights.shape[2]
-    heads = rel_table.shape[1] // 4
-    ext = 3 * rows
-    span = 2 * rows + 128
+    heads = rel_table.shape[1]
     groups = wide_count // 8
     eighth = width // 8
 
@@ -1092,25 +1170,21 @@
     lanes = np.arange(512)
     at_lane = np.where(lanes < 128, 128 + lanes, np.maximum(lanes - 384, 0))
     pick = jnp.asarray((buckets[at_lane][None, :] == np.arange(BUCKETS)[:, None]).astype(np.float32))
-    bias_line = jnp.einsum("bl,bh->hl", pick, rel_table, precision=lax.Precision.HIGHEST)
-    bias_line = bias_line.reshape(4, heads, 512)
-    ranks = jnp.asarray(RANKS, jnp.int32)
-    bias_line = jnp.take(bias_line, ranks[z], axis=0)
-    seg = segments[0]
-    seg_q = lax.dynamic_slice_in_dim(seg, z * rows, rows, 0).reshape(1, rows)
-    seg_pad = jnp.concatenate([jnp.full((2 * rows,), -1, jnp.int32), seg])
-    seg_k = lax.dynamic_slice_in_dim(seg_pad, z * rows, ext, 0).reshape(ext, 1)
+    rel_pick = jnp.asarray(
+        (buckets[np.maximum(lanes - 127, 0)][:, None] == np.arange(128)[None, :]).astype(np.float32)
+    )
 
     half = width // 16
-    weights, x1, h1, q1, kv1, o1, bias, mem_full, x2, h2, q2, kv2, o2 = forward(
-        valid_rows, tokens, memory[0], norm_gains, bias_line, seg_q, seg_k,
-        self_weights.reshape(4, 16, half, hw), cross_weights.reshape(4, 16, half, hw),
+    weights, bias_line, x1, h1, q1, kv1, o1, bias, mem_full, x2, h2, q2, kv2, o2 = forward(
+        valid_rows, tokens, memory[0], norm_gains, rel_table.T, pick, segments,
+        jnp.swapaxes(self_weights, 1, 2).reshape(4, 4, hw // 4, width),
+        jnp.swapaxes(cross_weights, 1, 2).reshape(4, 4, hw // 4, width),
         ffn_weights.reshape(3, 16, half, fw),
     )
     weights = weights.reshape(4, 4, width, width)
     mem_full = mem_full.reshape(mem_len, width)
-    output, final, tokens_grad, memory_grad, gain_sums, rel = backward(
-        valid_rows, x2, cotangent, x1, mem_full, h2, h1, tokens, norm_gains, bias_line, seg_q, seg_k,
+    output, final, tokens_grad, memory_grad, small = backward(
+        valid_rows, x2, cotangent, x1, mem_full, h2, h1, tokens, norm_gains, bias_line, segments, rel_pick,
         weights, q2, kv2, o2, q1, kv1, o1, bias,
     )
     if groups > 1:
@@ -1120,46 +1194,16 @@
         )
         final = lax.psum_scatter(mine, "wide", scatter_dimension=1, tiled=True)
     own = final.shape[1]
-
-    rel_pick = jnp.asarray(
-        (buckets[np.maximum(lanes - 127, 0)][:, None] == np.arange(BUCKETS)[None, :]).astype(np.float32)
-    )
-    places = jnp.asarray([[row.index(q) for q in range(4)] for row in RANKS], jnp.int32)
-    rel = jnp.take(rel, places[z], axis=0)
-    rel = jnp.einsum("hl,lb->bh", rel.reshape(4 * heads, 512), rel_pick, precision=lax.Precision.HIGHEST)
-    rel_row = jnp.pad(rel.reshape(1, -1), ((0, 0), (0, width - BUCKETS * 4 * heads)))
-    small = jnp.concatenate([gain_sums[::8], rel_row, jnp.zeros((4, width), F32)], 0)
-    rsum, csum, asum, prow, pcol = reduce_stats(wide_count, final, small)
-
-    def split(g):
-        return jnp.stack([g[:, 0:hw], g[:, 2 * hw : 3 * hw], g[:, 3 * hw :], g[:, hw : 2 * hw]])
-
-    ffn_flat = jnp.concatenate([final[2], final[3]], axis=1)
-    ffn_grad = jnp.stack([ffn_flat[:, 0:fw], ffn_flat[:, fw : 2 * fw], ffn_flat[:, 2 * fw :]])
-    attn_row = jnp.concatenate([rsum[0:1], rsum[2:4], rsum[8:9], rsum[10:12]], 0)[:, :own] / width
-    ffn_row = rsum[16:19, :own] / (4 * fw)
-    attn_col = jnp.stack(
-        [csum[i, a * hw : (a + 1) * hw] for i in range(2) for a in (0, 2, 3)]
-    ) / width
-    ffn_cols = jnp.concatenate([csum[2], csum[3]])
-    ffn_col = ffn_cols.reshape(3, fw) / width
-    proj_rows = prow[:, 4:6, :own].transpose(1, 0, 2).reshape(2, width) / width
-    proj_cols = pcol[:, 0:2, hw : 2 * hw].transpose(1, 0, 2).reshape(2, width) / width
-    return (
-        output,
-        tokens_grad,
-        memory_grad.reshape(1, mem_own, width),
-        asum[0:3],
-        asum[3, : BUCKETS * 4 * heads].reshape(BUCKETS, 4 * heads),
-        split(final[0]),
-        split(final[1]),
-        ffn_grad,
-        attn_row,
-        attn_col,
-        jnp.concatenate([proj_rows, proj_cols], 1),
-        ffn_row,
-        ffn_col,
-    )
+    sums = reduce_stats(wide_count, final, small)
+    shapes = [
+        ((rows, width), BF), ((rows, width), F32), ((mem_own, width), F32), ((3, width), F32), ((heads, BUCKETS), F32),
+        ((4, own, hw), F32), ((4, own, hw), F32), ((3, own, fw), F32),
+        ((6, own), F32), ((6, hw), F32), ((2, 2 * width), F32), ((3, own), F32), ((3, fw), F32),
+    ]
+    outs = list(finish(shapes, output, tokens_grad, memory_grad, final, *sums))
+    outs[2] = outs[2].reshape(1, mem_own, width)
+    outs[4] = outs[4].T
+    return tuple(outs)
 
 
 def solution(mesh):

time: 280 us -> 251 us (0.90)
  local copies, waits for them, and re-layouts: 18.1 us -> 0 us
  other arithmetic: 11.3 us -> 0 us
  Pallas kernels: 246 us -> 250 us
    unnamed x18 -> x0, local copies, waits for them, and re-layouts: 7.2 us -> none
    slice x7 -> x0, local copies, waits for them, and re-layouts: 4.66 us -> none  [the longest x1 0.94 us: local(): csum[i, a * hw:(a + 1) * hw]]
    div x6 -> x0, other arithmetic: 4.11 us -> none  [the longest x1 1.26 us: local(): ffn_row = rsum[16:19, :own] / (4 * fw)]
    pallas_call x0 -> x1, Pallas kernels: none -> 3.54 us  [finish(): pl.pallas_call(finish_kernel, name='finish', in_specs=[vmem] * len(args),...]
where the time goes in v4:
time: 251 us
  Pallas kernels  250 us (100%)
    pallas_call x1, Pallas kernels, backward(): pl.pallas_call(backward_kernel, name='backward', grid=(12,), in_specs=[SM...  130 us
    pallas_call x1, Pallas kernels, forward(): pl.pallas_call(forward_kernel, name='forward', grid=(8,), in_specs=[SMEM_...  101 us
    pallas_call x1, Pallas kernels, reduce_stats(): pl.pallas_call(functools.partial(stats_kernel, wide_count), name='stats',...  14.3 us

profile of v4, /device:TPU:0, one launch (start us, length us, event | category | flops | bytes accessed | tf_op | source)
XLA Modules:
  0.0 251.1 jit_solution(8045832165872176184)
XLA Ops:
  1.3 101.4 %forward.1 = (bf16[4,4,16,48,768]{4,3,2,1,0:T(8,128)(2,1)}, f32[4,3,512]{2,1,0:T(4,128)}, f32[256,768]{1,0:T(8,128)}, bf16[768,768]{1,0:T(8,128)(2,1)}, bf16[4,2...) custom-call(s32[1]{0:T(128)S(6)} %copy.25.valid_ref, ...), custom_call_target="tpu_custom_call" | custom-call | tf_op jit(solution)/shard_map/forward/pallas_call | solution.py:476
  102.7 130.5 %backward.1 = (bf16[256,768]{1,0:T(8,128)(2,1)}, f32[4,96,768]{2,1,0:T(8,128)}, f32[256,768]{1,0:T(8,128)}, f32[128,768]{1,0:T(8,128)}, f32[8,1024]{1,0:T(8,128)}) custom-call(s32[1]{0:T(128)S(6)} %copy.25.valid_ref, f32[256,768]{1,0:T(8,128)} %get-tuple-element.49.x2_ref, bf16[256,768]{1,0:T(8,128)(2,1)} %cot_ref.1, f32[256,768]{1,0:T(8,128)} %get-tuple-element.50.x1_ref, ...), custom_call_target="tpu_custom_call" | custom-call | tf_op jit(solution)/shard_map/backward/pallas_call | solution.py:914
  233.2 14.3 %stats.1 = (f32[24,128]{1,0:T(8,128)}, f32[8,768]{1,0:T(8,128)}, f32[8,1024]{1,0:T(8,128)}, f32[4,8,768]{2,1,0:T(8,128)}) custom-call(f32[4,96,768]{2,1,0:T(8,128)} %get-tuple-element.66.f_ref, f32[8,1024]{1,0:T(8,128)} %get-tuple-element.67.a_ref), custom_call_target="tpu_custom_call" | custom-call | tf_op jit(solution)/shard_map/stats/pallas_call | solution.py:1082
  247.4 3.5 %finish.1 = (bf16[256,768]{1,0:T(8,128)(2,1)}, f32[256,768]{1,0:T(8,128)}, f32[128,768]{1,0:T(8,128)}, f32[3,768]{1,0:T(4,128)}, f32[12,32]{1,0:T(8,128)}, /*ind...) custom-call(bf16[256,768]{1,0:T(8,128)(2,1)} %get-tuple-element.63.o, ...), custom_call_target="tpu_custom_call" | custom-call | tf_op jit(solution)/shard_map/finish/pallas_call | solution.py:1145

commit v5 on v4

--- a/solution.py
+++ b/solution.py
@@ -142,6 +142,7 @@
 
 
 RANKS = ((0, 1, 2, 3), (1, 0, 2, 3), (2, 3, 1, 0), (3, 2, 1, 0))
+EARLY = 6
 
 
 def forward_kernel(
@@ -190,18 +191,46 @@
 
     def tok_copy(hop, p):
         part_rows = pl.ds(p * part, part)
-        return remote(
-            tok_ref.at[part_rows], xt.at[2 - hop, part_rows], ts.at[hop - 1, p], tr.at[hop - 1, p], {"narrow": z + hop}
-        )
+        src = tok_ref.at[part_rows] if hop == 1 else xt.at[1, part_rows]
+        return remote(src, xt.at[2 - hop, part_rows], ts.at[hop - 1, p], tr.at[hop - 1, p], {"narrow": z + 1})
+
+    def tok_senders(hop):
+        return z < 3 if hop == 1 else jnp.logical_and(z >= 1, z < 3)
 
     def tok_send(hop, parts):
-        @pl.when(z < 4 - hop)
+        if hop == 2:
+            @pl.when(z >= 1)
+            def _():
+                for p in parts:
+                    tok_copy(1, p).wait_recv()
+
+        @pl.when(tok_senders(hop))
         def _():
             for p in parts:
                 tok_copy(hop, p).start()
 
-    def mem_copy(k):
-        return remote(mem_ref, mt.at[z], ms.at[k - 1], mr.at[k - 1], at.narrow_dev(k))
+    def mem_copy(i, d):
+        k = z - d * i
+        src = mem_ref if i == 0 else mt.at[k]
+        place = i if d > 0 else 3 + i
+        return remote(src, mt.at[k], ms.at[place], mr.at[place], {"narrow": z + d})
+
+    def mem_sends(i, act):
+        @pl.when(jnp.logical_and(z >= i, z < 3))
+        def _():
+            act(mem_copy(i, 1))
+
+        @pl.when(jnp.logical_and(z >= 1, z < 4 - i))
+        def _():
+            act(mem_copy(i, -1))
+
+    def mem_arrived(i):
+        for d in (1, -1):
+            @pl.when(z > i if d > 0 else z < 3 - i)
+            def _():
+                here = mt.at[z - d * (1 + i)]
+                place = i if d > 0 else 3 + i
+                remote(here, here, ms.at[place], mr.at[place], at.x_dev).wait_recv()
 
     def piece(u, r, kind):
         first, n, dev = {
@@ -237,16 +266,22 @@
         for kind in (0, 3, 4, 1, 6):
             piece(u, r, kind).start()
         if t == 0:
+            tok_send(1, (0, 1))
+        if t == 1:
             tok_send(1, (2, 3))
-        if t == 1:
+        if t == 2:
+            own_sends(2, lambda copy: copy.start())
+        if t == 3:
             tok_send(2, (0, 1))
-        if t == 2:
+        if t == 4:
             tok_send(2, (2, 3))
-            own_sends(2, lambda copy: copy.start())
-        if t in (3, 4, 5):
-            mem_copy(t - 2).start()
         if t == 5:
             own_sends(3, lambda copy: copy.start())
+            mem_sends(0, lambda copy: copy.start())
+        if t in (7, 9):
+            i = (t - 5) // 2
+            mem_arrived(i - 1)
+            mem_sends(i, lambda copy: copy.start())
 
     def step1(t):
         if not 0 <= t < len(pieces):
@@ -305,7 +340,6 @@
         for copy in attn_loads(0):
             copy.wait()
         own_sends(0, lambda copy: copy.start())
-        tok_send(1, (0, 1))
         for copy in attn_loads(1):
             copy.wait()
         own_sends(1, lambda copy: copy.start())
@@ -325,28 +359,24 @@
             first = at.quarter(k) * heads
             for hh in range(heads):
                 bd_ref[k, hh : hh + 1, :] = lines[pl.ds(first + hh, 1), :]
-        step0(0)
-        step0(1)
-        step1(0)
-        step0(2)
-        step1(1)
-        step2(0)
-        step3(0)
-        step0(3)
-        step1(2)
-        step2(1)
-        for hop in (1, 2):
-            @pl.when(z >= hop)
-            def _():
-                for p in range(4):
-                    tok_copy(hop, p).wait_recv()
+        for t in range(EARLY):
+            step0(t)
+            step1(t - 1)
+            step2(t - 2)
+            step3(t - 3)
+
+        @pl.when(z >= 2)
+        def _():
+            for p in range(4):
+                tok_copy(2, p).wait_recv()
+
         for t in range(2):
             v = jnp.where(z >= 2 - t, xt[t].astype(F32), 0.0)
             h1_ref[t * rows : (t + 1) * rows, :] = (v * inv_rms(v) * gain_ref[0:1, :]).astype(BF)
 
     def hook(i, first, last):
         for jj in range(first, last):
-            t = 4 + jj
+            t = EARLY + jj
 
             @pl.when(j == jj)
             def _():
@@ -396,10 +426,11 @@
         x2_ref[...] = x1
         h2_ref[...] = (x1 * inv_rms(x1) * gain_ref[1:2, :]).astype(BF)
         mfull_ref[z] = mem_ref[...]
-        for k in (1, 2, 3):
-            frm = lax.rem(z + 4 - k, 4)
-            remote(mt.at[frm], mt.at[frm], ms.at[k - 1], mr.at[k - 1], at.x_dev).wait_recv()
-            mfull_ref[frm] = mt[frm]
+        mem_arrived(2)
+        for k in range(4):
+            @pl.when(z != k)
+            def _():
+                mfull_ref[k] = mt[k]
 
     @pl.when(j >= 4)
     def _():
@@ -424,7 +455,7 @@
 
     @pl.when(j == 7)
     def _():
-        for t in range(12, len(pieces) + 3):
+        for t in range(EARLY + 8, len(pieces) + 3):
             step0(t)
             step1(t - 1)
             step2(t - 2)
@@ -438,12 +469,12 @@
             for k in range(4):
                 keep(u, k).wait()
         for hop in (1, 2):
-            @pl.when(z < 4 - hop)
+            @pl.when(tok_senders(hop))
             def _():
                 for p in range(4):
                     tok_copy(hop, p).wait_send()
-        for k in (1, 2, 3):
-            mem_copy(k).wait_send()
+        for i in range(3):
+            mem_sends(i, lambda copy: copy.wait_send())
 
 
 def forward(valid_rows, tokens, memory, gains, rel, pick, seg, ws, wc, wf):
@@ -488,7 +519,7 @@
             pltpu.VMEM((2, rows, width), BF), pltpu.VMEM((4, mem_own, width), BF),
             pltpu.VMEM((2, 2 * rows + 128, 128), F32),
             dma((4, 5)), dma((4, 4)), dma((12, 10)), dma((12, 10)),
-            dma((2, 4)), dma((2, 4)), dma((3,)), dma((3,)), dma((2, 4)), dma((4,)), dma((4, 4)),
+            dma((2, 4)), dma((2, 4)), dma((6,)), dma((6,)), dma((2, 4)), dma((4,)), dma((4, 4)),
         ],
         compiler_params=pltpu.CompilerParams(
             collective_id=0, has_side_effects=True, vmem_limit_bytes=VMEM_LIMIT, dimension_semantics=("arbitrary",)
@@ -640,7 +671,7 @@
                     tick(t)
 
     def dx_send(t):
-        return remote(dxo.at[t], dxr.at[t], dxs.at[t], dxrs.at[t], {"narrow": z - 2 + t})
+        return remote(dxo.at[t], dxr.at[t], dxs.at[t], dxrs.at[t], {"narrow": z - 1})
 
     def dm_send(k):
         return remote(dmo.at[lax.rem(z + k, 4)], dmr.at[k - 1], dms.at[k - 1], dmrs.at[k - 1], at.narrow_dev(k))
@@ -852,9 +883,13 @@
         for t in range(2):
             dxo[t] = acc[t * rows : (t + 1) * rows, :].astype(BF)
 
-            @pl.when(z >= 2 - t)
-            def _():
-                dx_send(t).start()
+        @pl.when(z >= 2)
+        def _():
+            dx_send(0).start()
+
+        @pl.when(z == 3)
+        def _():
+            dx_send(1).start()
         last = n + 4
         for t in range(len(TICKS), last):
             tick(t)
@@ -863,12 +898,17 @@
                 for k in (1, 2, 3):
                     dm_send(k).wait_recv()
                     mg_ref[...] += dmr[k - 1].astype(F32)
-            if t == last - 2:
-                for k in range(2):
-                    @pl.when(z < 2 + k)
-                    def _():
-                        dx_send(k).wait_recv()
-                        acc[2 * rows : ext, :] += dxr[k].astype(F32)
+            if t == len(TICKS) + 1:
+                @pl.when(is_inner)
+                def _():
+                    dx_send(0).wait_recv()
+                    add(dxo.at[1], dxr.at[0])
+                    dx_send(1).start()
+            if t == len(TICKS) + 3:
+                @pl.when(z < 3)
+                def _():
+                    dx_send(1).wait_recv()
+                    acc[2 * rows : ext, :] += dxr[1].astype(F32)
                 gain_part, dv = norm_back(tok_ref[...].astype(F32), gain_ref[0:1, :], acc[2 * rows : ext, :])
                 rel = lax.dot_general(
                     rel_ref[...], pick_ref[...], (((1,), (0,)), ((), ())),

time: 251 us -> 234 us (0.932)
  Pallas kernels: 250 us -> 232 us
    pallas_call x1, Pallas kernels: 101 us -> 90 us  [forward(): pl.pallas_call(forward_kernel, name='forward', grid=(8,), in_specs=[SMEM_...]
    pallas_call x1, Pallas kernels: 130 us -> 125 us  [backward(): pl.pallas_call(backward_kernel, name='backward', grid=(12,), in_specs=[SM...]
where the time goes in v5:
time: 234 us
  Pallas kernels  232 us (99%)
    pallas_call x1, Pallas kernels, backward(): pl.pallas_call(backward_kernel, name='backward', grid=(12,), in_specs=[SM...  125 us
    pallas_call x1, Pallas kernels, forward(): pl.pallas_call(forward_kernel, name='forward', grid=(8,), in_specs=[SMEM_...  90 us
    pallas_call x1, Pallas kernels, reduce_stats(): pl.pallas_call(functools.partial(stats_kernel, wide_count), name='stats',...  13.6 us

profile of v5, /device:TPU:0, one launch (start us, length us, event | category | flops | bytes accessed | tf_op | source)
XLA Modules:
  0.0 233.8 jit_solution(15799079799518344279)
XLA Ops:
  1.3 90.0 %forward.1 = (bf16[4,4,16,48,768]{4,3,2,1,0:T(8,128)(2,1)}, f32[4,3,512]{2,1,0:T(4,128)}, f32[256,768]{1,0:T(8,128)}, bf16[768,768]{1,0:T(8,128)(2,1)}, bf16[4,2...) custom-call(s32[1]{0:T(128)S(6)} %copy.25.valid_ref, ...), custom_call_target="tpu_custom_call" | custom-call | tf_op jit(solution)/shard_map/forward/pallas_call | solution.py:507
  91.3 125.2 %backward.1 = (bf16[256,768]{1,0:T(8,128)(2,1)}, f32[4,96,768]{2,1,0:T(8,128)}, f32[256,768]{1,0:T(8,128)}, f32[128,768]{1,0:T(8,128)}, f32[8,1024]{1,0:T(8,128)}) custom-call(s32[1]{0:T(128)S(6)} %copy.25.valid_ref, f32[256,768]{1,0:T(8,128)} %get-tuple-element.49.x2_ref, bf16[256,768]{1,0:T(8,128)(2,1)} %cot_ref.1, f32[256,768]{1,0:T(8,128)} %get-tuple-element.50.x1_ref, ...), custom_call_target="tpu_custom_call" | custom-call | tf_op jit(solution)/shard_map/backward/pallas_call | solution.py:954
  216.5 13.6 %stats.1 = (f32[24,128]{1,0:T(8,128)}, f32[8,768]{1,0:T(8,128)}, f32[8,1024]{1,0:T(8,128)}, f32[4,8,768]{2,1,0:T(8,128)}) custom-call(f32[4,96,768]{2,1,0:T(8,128)} %get-tuple-element.66.f_ref, f32[8,1024]{1,0:T(8,128)} %get-tuple-element.67.a_ref), custom_call_target="tpu_custom_call" | custom-call | tf_op jit(solution)/shard_map/stats/pallas_call | solution.py:1122
  230.1 3.5 %finish.1 = (bf16[256,768]{1,0:T(8,128)(2,1)}, f32[256,768]{1,0:T(8,128)}, f32[128,768]{1,0:T(8,128)}, f32[3,768]{1,0:T(4,128)}, f32[12,32]{1,0:T(8,128)}, /*ind...) custom-call(bf16[256,768]{1,0:T(8,128)(2,1)} %get-tuple-element.63.o, ...), custom_call_target="tpu_custom_call" | custom-call | tf_op jit(solution)/shard_map/finish/pallas_call | solution.py:1185

commit v6 on v5

--- a/solution.py
+++ b/solution.py
@@ -142,7 +142,7 @@
 
 
 RANKS = ((0, 1, 2, 3), (1, 0, 2, 3), (2, 3, 1, 0), (3, 2, 1, 0))
-EARLY = 6
+EARLY = 5
 
 
 def forward_kernel(
@@ -272,14 +272,13 @@
         if t == 2:
             own_sends(2, lambda copy: copy.start())
         if t == 3:
-            tok_send(2, (0, 1))
+            tok_send(2, (0, 1, 2, 3))
         if t == 4:
-            tok_send(2, (2, 3))
+            mem_sends(0, lambda copy: copy.start())
         if t == 5:
             own_sends(3, lambda copy: copy.start())
-            mem_sends(0, lambda copy: copy.start())
-        if t in (7, 9):
-            i = (t - 5) // 2
+        if t in (6, 8):
+            i = (t - 4) // 2
             mem_arrived(i - 1)
             mem_sends(i, lambda copy: copy.start())
 
@@ -529,7 +528,8 @@
 
 CHUNKS = [(2 + i % 2, i // 2) for i in range(8)] + [(1, i) for i in range(4)] + [(0, i) for i in range(4)]
 HELD = 12
-TICKS = [(1, 0), (2, 0), (3, 0), (4, 1), (5, 1), (6, 1), (7, 1), (8, 0), (8, 2), (9, 1), (10, 0), (10, 2), (11, 1)]
+LAG = 3
+TICKS = [(1, 0), (2, 0), (3, 0), (4, 0), (5, 0), (6, 0), (7, 0), (8, 0), (8, 2), (9, 1), (10, 0), (10, 2), (11, 1)]
 
 
 def backward_kernel(
@@ -659,7 +659,7 @@
             z_send(i, 0, d).wait_send()
 
     def tick(t):
-        for k, step in enumerate((step_b, step_c, step_d, step_e, step_f)):
+        for k, step in ((0, step_b), (1, step_c), (2, step_d), (2, step_e), (LAG, step_f)):
             if 0 <= t - k < n:
                 step(t - k)
 
@@ -890,7 +890,7 @@
         @pl.when(z == 3)
         def _():
             dx_send(1).start()
-        last = n + 4
+        last = n + LAG
         for t in range(len(TICKS), last):
             tick(t)
             if t == len(TICKS):
@@ -914,8 +914,13 @@
                     rel_ref[...], pick_ref[...], (((1,), (0,)), ((), ())),
                     preferred_element_type=F32, precision=lax.Precision.HIGHEST,
                 )
-                gains = [gain_part, gsum_ref[8:9, :], gsum_ref[16:17, :], jnp.zeros((5, width), F32)]
-                small_ref[...] = jnp.concatenate([jnp.concatenate(gains, axis=0), rel[0:8], rel[8:16]], axis=1)
+                gains = [gain_part, gsum_ref[8:9, :], gsum_ref[16:17, :], jnp.zeros((2, width), F32)]
+                per = width // 128
+                lines = [
+                    jnp.concatenate([rel[per * k + h : per * k + h + 1] for h in range(per)], axis=1)
+                    for k in range(2)
+                ]
+                small_ref[...] = jnp.concatenate(gains + lines + [jnp.zeros((1, width), F32)], axis=0)
                 tg_ref[...] = res[...] + dv
         for i in range(n - HELD, n):
             sent(i)
@@ -948,7 +953,7 @@
 
     out = [
         ((rows, width), BF), ((4, own, width), F32), ((rows, width), F32), ((mem // 4, width), F32),
-        ((8, width + 256), F32),
+        ((8, width), F32),
     ]
     shapes = [jax.ShapeDtypeStruct(s, d) for s, d in out]
     return pl.pallas_call(
@@ -1037,7 +1042,7 @@
     rall[z, 16:24] = sums(lane // third == row, sq[2]) + sums((lane + width) // third == row, sq[3])
     aall[z] = a_ref[...]
     call[w] = jnp.concatenate(
-        [jnp.sum(v, axis=0, keepdims=True) for v in sq] + [jnp.zeros((4, width), F32)], axis=0
+        [jnp.sum(v, axis=0, keepdims=True) for v in sq], axis=0
     )
     pl.semaphore_wait(sem, 3 + wide_count - 1)
 
@@ -1072,15 +1077,9 @@
     rows = jnp.concatenate([rsum[0:8], zero], axis=1)
     more = jnp.concatenate([rsum[8:16], zero], axis=1)
     shift = own * w
-    left = jnp.concatenate(
-        [
-            asum[0:3, 0:width],
-            pltpu.roll(rows, shift, 1)[1:2], pltpu.roll(more, shift, 1)[1:2],
-            jnp.zeros((3, width), F32),
-        ],
-        axis=0,
+    ball[w] = jnp.concatenate(
+        [asum[0:3], pltpu.roll(rows, shift, 1)[1:2], pltpu.roll(more, shift, 1)[1:2], asum[5:8]], axis=0
     )
-    ball[w] = jnp.concatenate([left, asum[:, width:]], axis=1)
     wide_loop(lambda k: b_send(k).start())
 
     def c_wait(k):
@@ -1090,7 +1089,7 @@
     wide_loop(c_wait)
     csum = lax.fori_loop(1, wide_count, lambda i, v: v + call[i], call[0])
     csum_ref[...] = csum
-    pcol_ref[z] = csum
+    pcol_ref[z] = csum[:, quarter : quarter + 256]
     for k in (1, 2, 3):
         p_send(k).start()
 
@@ -1126,13 +1125,13 @@
         out_specs=[vmem] * 4,
         out_shape=[
             jax.ShapeDtypeStruct((24, 128), F32),
-            jax.ShapeDtypeStruct((8, width), F32),
+            jax.ShapeDtypeStruct((4, width), F32),
             jax.ShapeDtypeStruct(small.shape, F32),
-            jax.ShapeDtypeStruct((4, 8, width), F32),
+            jax.ShapeDtypeStruct((4, 4, 256), F32),
         ],
         scratch_shapes=[
             pltpu.VMEM((4, 24, 128), F32), pltpu.VMEM((4,) + small.shape, F32),
-            pltpu.VMEM((wide_count, 8, width), F32), pltpu.VMEM((wide_count,) + small.shape, F32),
+            pltpu.VMEM((wide_count, 4, width), F32), pltpu.VMEM((wide_count,) + small.shape, F32),
             dma((3,)), dma((3,)), dma((3,)), dma((3,)),
             dma((wide_count - 1,)), dma((wide_count - 1,)), dma((wide_count - 1,)), dma((wide_count - 1,)),
             dma((3,)), dma((3,)),
@@ -1152,8 +1151,11 @@
     tg_o[...] = tg_ref[...]
     mg_o[...] = mg_ref[...]
     gains_o[...] = asum_ref[0:3, 0:width]
-    rel = jnp.concatenate([asum_ref[:, width : width + 128], asum_ref[:, width + 128 : width + 256]], axis=0)
-    rel_o[...] = rel[0 : rel_o.shape[0], 0 : rel_o.shape[1]]
+    heads, buckets = rel_o.shape
+    per = width // 128
+    for h in range(heads):
+        row, first = 5 + h // per, 128 * (h % per)
+        rel_o[h : h + 1, :] = asum_ref[row : row + 1, first : first + buckets]
     for ref, i in ((self_o, 0), (cross_o, 1)):
         for m, part in enumerate((0, 2, 3, 1)):
             ref[m] = f_ref[i, :, part * hw : (part + 1) * hw]
@@ -1175,7 +1177,7 @@
     fcol_o[1:2, cut:fw] = csum_ref[3:4, 0 : fw - cut] * scale
     fcol_o[2:3, :] = csum_ref[3:4, fw - cut : width] * scale
     for i in range(2):
-        cols = jnp.concatenate([pcol_ref[k, i : i + 1, hw : 2 * hw] for k in range(4)], axis=1)
+        cols = jnp.concatenate([pcol_ref[k, i : i + 1, 0:hw] for k in range(4)], axis=1)
         proj_o[i : i + 1, 0:width] = asum_ref[3 + i : 4 + i, 0:width] * scale
         proj_o[i : i + 1, width : 2 * width] = cols * scale
 

time: 234 us -> 230 us (0.983)
  Pallas kernels: 232 us -> 228 us
    pallas_call x1, Pallas kernels: 125 us -> 122 us  [backward(): pl.pallas_call(backward_kernel, name='backward', grid=(12,), in_specs=[SM...]
where the time goes in v6:
time: 230 us; the launch traced here: 229 us
  Pallas kernels  228 us (99%)
    pallas_call x1, Pallas kernels, backward(): pl.pallas_call(backward_kernel, name='backward', grid=(12,), in_specs=[SM...  122 us
    pallas_call x1, Pallas kernels, forward(): pl.pallas_call(forward_kernel, name='forward', grid=(8,), in_specs=[SMEM_...  89.2 us
    pallas_call x1, Pallas kernels, reduce_stats(): pl.pallas_call(functools.partial(stats_kernel, wide_count), name='stats',...  12.8 us

profile of v6, /device:TPU:0, one launch (start us, length us, event | category | flops | bytes accessed | tf_op | source)
XLA Modules:
  0.0 229.4 jit_solution(3580108384278770921)
XLA Ops:
  1.3 89.2 %forward.1 = (bf16[4,4,16,48,768]{4,3,2,1,0:T(8,128)(2,1)}, f32[4,3,512]{2,1,0:T(4,128)}, f32[256,768]{1,0:T(8,128)}, bf16[768,768]{1,0:T(8,128)(2,1)}, bf16[4,2...) custom-call(s32[1]{0:T(128)S(6)} %copy.25.valid_ref, ...), custom_call_target="tpu_custom_call" | custom-call | tf_op jit(solution)/shard_map/forward/pallas_call | solution.py:506
  90.5 122.4 %backward.1 = (bf16[256,768]{1,0:T(8,128)(2,1)}, f32[4,96,768]{2,1,0:T(8,128)}, f32[256,768]{1,0:T(8,128)}, f32[128,768]{1,0:T(8,128)}, f32[8,768]{1,0:T(8,128)}) custom-call(s32[1]{0:T(128)S(6)} %copy.25.valid_ref, f32[256,768]{1,0:T(8,128)} %get-tuple-element.49.x2_ref, bf16[256,768]{1,0:T(8,128)(2,1)} %cot_ref.1, f32[256,768]{1,0:T(8,128)} %get-tuple-element.50.x1_ref, ...), custom_call_target="tpu_custom_call" | custom-call | tf_op jit(solution)/shard_map/backward/pallas_call | solution.py:959
  212.9 12.8 %stats.1 = (f32[24,128]{1,0:T(8,128)}, f32[4,768]{1,0:T(4,128)}, f32[8,768]{1,0:T(8,128)}, f32[4,4,256]{2,1,0:T(4,128)}) custom-call(f32[4,96,768]{2,1,0:T(8,128)} %get-tuple-element.66.f_ref, f32[8,768]{1,0:T(8,128)} %get-tuple-element.67.a_ref), custom_call_target="tpu_custom_call" | custom-call | tf_op jit(solution)/shard_map/stats/pallas_call | solution.py:1121
  225.7 3.5 %finish.1 = (bf16[256,768]{1,0:T(8,128)(2,1)}, f32[256,768]{1,0:T(8,128)}, f32[128,768]{1,0:T(8,128)}, f32[3,768]{1,0:T(4,128)}, f32[12,32]{1,0:T(8,128)}, /*ind...) custom-call(bf16[256,768]{1,0:T(8,128)(2,1)} %get-tuple-element.63.o, ...), custom_call_target="tpu_custom_call" | custom-call | tf_op jit(solution)/shard_map/finish/pallas_call | solution.py:1187

commit v7 on v6

--- a/solution.py
+++ b/solution.py
@@ -528,8 +528,8 @@
 
 CHUNKS = [(2 + i % 2, i // 2) for i in range(8)] + [(1, i) for i in range(4)] + [(0, i) for i in range(4)]
 HELD = 12
-LAG = 3
-TICKS = [(1, 0), (2, 0), (3, 0), (4, 0), (5, 0), (6, 0), (7, 0), (8, 0), (8, 2), (9, 1), (10, 0), (10, 2), (11, 1)]
+LAG = 4
+TICKS = [(1, 0), (2, 0), (3, 0), (4, 1), (5, 1), (6, 1), (7, 1), (8, 0), (8, 2), (9, 1), (10, 0), (10, 2), (11, 1)]
 
 
 def backward_kernel(

time: 230 us -> 229 us (level)
  no operation moved by 1% of the time
where the time goes in v7:
time: 229 us
  Pallas kernels  228 us (100%)
    pallas_call x1, Pallas kernels, backward(): pl.pallas_call(backward_kernel, name='backward', grid=(12,), in_specs=[SM...  122 us
    pallas_call x1, Pallas kernels, forward(): pl.pallas_call(forward_kernel, name='forward', grid=(8,), in_specs=[SMEM_...  89.2 us
    pallas_call x1, Pallas kernels, reduce_stats(): pl.pallas_call(functools.partial(stats_kernel, wide_count), name='stats',...  12.8 us

profile of v7, /device:TPU:0, one launch (start us, length us, event | category | flops | bytes accessed | tf_op | source)
XLA Modules:
  0.0 229.2 jit_solution(10004505213910131869)
XLA Ops:
  1.3 89.2 %forward.1 = (bf16[4,4,16,48,768]{4,3,2,1,0:T(8,128)(2,1)}, f32[4,3,512]{2,1,0:T(4,128)}, f32[256,768]{1,0:T(8,128)}, bf16[768,768]{1,0:T(8,128)(2,1)}, bf16[4,2...) custom-call(s32[1]{0:T(128)S(6)} %copy.25.valid_ref, ...), custom_call_target="tpu_custom_call" | custom-call | tf_op jit(solution)/shard_map/forward/pallas_call | solution.py:506
  90.5 122.2 %backward.1 = (bf16[256,768]{1,0:T(8,128)(2,1)}, f32[4,96,768]{2,1,0:T(8,128)}, f32[256,768]{1,0:T(8,128)}, f32[128,768]{1,0:T(8,128)}, f32[8,768]{1,0:T(8,128)}) custom-call(s32[1]{0:T(128)S(6)} %copy.25.valid_ref, f32[256,768]{1,0:T(8,128)} %get-tuple-element.49.x2_ref, bf16[256,768]{1,0:T(8,128)(2,1)} %cot_ref.1, f32[256,768]{1,0:T(8,128)} %get-tuple-element.50.x1_ref, ...), custom_call_target="tpu_custom_call" | custom-call | tf_op jit(solution)/shard_map/backward/pallas_call | solution.py:959
  212.7 12.8 %stats.1 = (f32[24,128]{1,0:T(8,128)}, f32[4,768]{1,0:T(4,128)}, f32[8,768]{1,0:T(8,128)}, f32[4,4,256]{2,1,0:T(4,128)}) custom-call(f32[4,96,768]{2,1,0:T(8,128)} %get-tuple-element.66.f_ref, f32[8,768]{1,0:T(8,128)} %get-tuple-element.67.a_ref), custom_call_target="tpu_custom_call" | custom-call | tf_op jit(solution)/shard_map/stats/pallas_call | solution.py:1121
  225.5 3.5 %finish.1 = (bf16[256,768]{1,0:T(8,128)(2,1)}, f32[256,768]{1,0:T(8,128)}, f32[128,768]{1,0:T(8,128)}, f32[3,768]{1,0:T(4,128)}, f32[12,32]{1,0:T(8,128)}, /*ind...) custom-call(bf16[256,768]{1,0:T(8,128)(2,1)} %get-tuple-element.63.o, ...), custom_call_target="tpu_custom_call" | custom-call | tf_op jit(solution)/shard_map/finish/pallas_call | solution.py:1187

commit v8 on v7

--- a/solution.py
+++ b/solution.py
@@ -528,7 +528,7 @@
 
 CHUNKS = [(2 + i % 2, i // 2) for i in range(8)] + [(1, i) for i in range(4)] + [(0, i) for i in range(4)]
 HELD = 12
-LAG = 4
+LAG = 3
 TICKS = [(1, 0), (2, 0), (3, 0), (4, 1), (5, 1), (6, 1), (7, 1), (8, 0), (8, 2), (9, 1), (10, 0), (10, 2), (11, 1)]
 
 

time: 229 us -> 229 us (level)
  no operation moved by 1% of the time
where the time goes in v8:
time: 229 us
  Pallas kernels  227 us (99%)
    pallas_call x1, Pallas kernels, backward(): pl.pallas_call(backward_kernel, name='backward', grid=(12,), in_specs=[SM...  122 us
    pallas_call x1, Pallas kernels, forward(): pl.pallas_call(forward_kernel, name='forward', grid=(8,), in_specs=[SMEM_...  89.2 us
    pallas_call x1, Pallas kernels, reduce_stats(): pl.pallas_call(functools.partial(stats_kernel, wide_count), name='stats',...  12.8 us

profile of v8, /device:TPU:0, one launch (start us, length us, event | category | flops | bytes accessed | tf_op | source)
XLA Modules:
  0.0 228.9 jit_solution(17390140883135332460)
XLA Ops:
  1.3 89.2 %forward.1 = (bf16[4,4,16,48,768]{4,3,2,1,0:T(8,128)(2,1)}, f32[4,3,512]{2,1,0:T(4,128)}, f32[256,768]{1,0:T(8,128)}, bf16[768,768]{1,0:T(8,128)(2,1)}, bf16[4,2...) custom-call(s32[1]{0:T(128)S(6)} %copy.25.valid_ref, ...), custom_call_target="tpu_custom_call" | custom-call | tf_op jit(solution)/shard_map/forward/pallas_call | solution.py:506
  90.5 121.8 %backward.1 = (bf16[256,768]{1,0:T(8,128)(2,1)}, f32[4,96,768]{2,1,0:T(8,128)}, f32[256,768]{1,0:T(8,128)}, f32[128,768]{1,0:T(8,128)}, f32[8,768]{1,0:T(8,128)}) custom-call(s32[1]{0:T(128)S(6)} %copy.25.valid_ref, f32[256,768]{1,0:T(8,128)} %get-tuple-element.49.x2_ref, bf16[256,768]{1,0:T(8,128)(2,1)} %cot_ref.1, f32[256,768]{1,0:T(8,128)} %get-tuple-element.50.x1_ref, ...), custom_call_target="tpu_custom_call" | custom-call | tf_op jit(solution)/shard_map/backward/pallas_call | solution.py:959
  212.4 12.8 %stats.1 = (f32[24,128]{1,0:T(8,128)}, f32[4,768]{1,0:T(4,128)}, f32[8,768]{1,0:T(8,128)}, f32[4,4,256]{2,1,0:T(4,128)}) custom-call(f32[4,96,768]{2,1,0:T(8,128)} %get-tuple-element.66.f_ref, f32[8,768]{1,0:T(8,128)} %get-tuple-element.67.a_ref), custom_call_target="tpu_custom_call" | custom-call | tf_op jit(solution)/shard_map/stats/pallas_call | solution.py:1121
  225.2 3.5 %finish.1 = (bf16[256,768]{1,0:T(8,128)(2,1)}, f32[256,768]{1,0:T(8,128)}, f32[128,768]{1,0:T(8,128)}, f32[3,768]{1,0:T(4,128)}, f32[12,32]{1,0:T(8,128)}, /*ind...) custom-call(bf16[256,768]{1,0:T(8,128)(2,1)} %get-tuple-element.63.o, ...), custom_call_target="tpu_custom_call" | custom-call | tf_op jit(solution)/shard_map/finish/pallas_call | solution.py:1187
